TPU v7x, 32 devices: a whole 2x2x4 slice. The times are simulated.
32 devices in a mesh: dp: 8 (over y, x, core), tp: 4 (over z).
Axes of the slice: x: 2, y: 2, z: 4, core: 2. Of those that a mesh axis runs over, the one named last changes fastest.
Arguments:
- hidden_in: bfloat16 [24, 512, 768], P('dp', 'tp'), may hold values from -6 to 6
- lengths: int32 [24], P('dp'), may hold values from 256 to 512, as said below
- inst_lengths: int32 [24], P('dp'), may hold values from 5 to 40
- w_query: bfloat16 [768, 768], P(None, 'tp'), may hold values from -0.0546875 to 0.0546875
- w_key: bfloat16 [768, 768], P(None, 'tp'), may hold values from -0.15625 to 0.15625
- w_value: bfloat16 [768, 768], P(None, 'tp'), may hold values from -0.21875 to 0.21875
- attention_output_weight: bfloat16 [768, 768], P('tp'), may hold values from -0.75 to 0.75
- feedforward_input_weight: bfloat16 [768, 3072], P(None, 'tp'), may hold values from -0.21875 to 0.21875
- feedforward_output_weight: bfloat16 [3072, 768], P('tp'), may hold values from -0.109375 to 0.109375
- rel_table: bfloat16 [32, 12], P(None, 'tp'), may hold values from -4 to 4
- gain_attn: bfloat16 [768], replicated, may hold values from 0.5 to 1.5
- gain_ffn: bfloat16 [768], replicated, may hold values from 0.5 to 1.5
- grad_output: bfloat16 [24, 512, 768], P('dp', 'tp'), may hold values from -6 to 6
- grad_pooled: bfloat16 [24, 768], P('dp', 'tp'), may hold values from -192 to 192
Outputs:
- layer_out: bfloat16 [24, 512, 768], P('dp', 'tp')
- pooled: float32 [24, 768], P('dp', 'tp')
- grad_hidden: float32 [24, 512, 768], P('dp', 'tp')
- grad_w_query: float32 [768, 768], P(None, 'tp')
- grad_w_key: float32 [768, 768], P(None, 'tp')
- grad_w_value: float32 [768, 768], P(None, 'tp')
- grad_w_out: float32 [768, 768], P('tp')
- grad_w_in: float32 [768, 3072], P(None, 'tp')
- grad_w_ffn_out: float32 [3072, 768], P('tp')
- grad_table: float32 [32, 12], P(None, 'tp')
- grad_gain_attn: float32 [768], replicated
- grad_gain_ffn: float32 [768], replicated
Inputs may be any that keep to these rules, and one draw needn't show every extreme that they name: `lengths`: some row in every draw has length 512.
All inputs are finite; a program needn't handle non-finite values.
Results may differ from a plain program's by a relative error of at most 0.019.
Values may be sent and summed in bfloat16 or wider, within the bound.
No kernel may reach another device: no remote copies, remote signals or barrier semaphores. Data moves between devices by JAX's collectives and lax.ppermute only.
A program may use at most 128 MiB of HBM per device.

v0:
```python
import jax
import jax.numpy as jnp
from jax import lax
from jax.sharding import PartitionSpec as P


def bucket_codes(size):
    places = jnp.arange(size, dtype=jnp.int32)
    offset = places[None, :] - places[:, None]
    upper_half = jnp.where(offset > 0, 16, 0).astype(jnp.int32)
    distance = jnp.abs(offset)
    far_code = 8 + sum(
        ((distance >= threshold).astype(jnp.int32) for threshold in (12, 16, 23, 32, 46, 64, 91))
    )
    return upper_half + jnp.where(distance < 8, distance, far_code)


def rms_scale(values, gain):
    return values * lax.rsqrt(jnp.mean(values * values, axis=-1, keepdims=True) + 1e-06) * gain


def gelu_of(values):
    return jax.nn.gelu(values, approximate=True)


def gelu_backward(activation, incoming):
    unused_value, slope_back = jax.vjp(gelu_of, activation)
    return slope_back(incoming.astype(jnp.float32))[0].astype(jnp.bfloat16)


def local(
    hidden_in,
    lengths,
    inst_lengths,
    w_query,
    w_key,
    w_value,
    attention_output_weight,
    feedforward_input_weight,
    feedforward_output_weight,
    rel_table,
    gain_attn,
    gain_ffn,
    grad_output,
    grad_pooled,
):
    seq_count, shard_len, model_width = hidden_in.shape
    full_len = shard_len * lax.axis_size("tp")
    offset = lax.axis_index("tp") * shard_len
    head_count = rel_table.shape[1]
    inner_width = w_query.shape[1]
    head_size = inner_width // head_count
    gain_one = gain_attn.astype(jnp.float32)
    gain_two = gain_ffn.astype(jnp.float32)
    hidden = hidden_in.astype(jnp.float32)
    combined_weight = jnp.concatenate((w_query, w_key, w_value), axis=1)

    def project(normalized_row_block):
        combined_projection = jnp.einsum(
            "vrf,fp->vrp", normalized_row_block, combined_weight, preferred_element_type=jnp.float32
        ).astype(jnp.bfloat16)
        shaped = combined_projection.reshape(seq_count, full_len, 3, head_count, head_size)
        return (shaped[:, :, 0], shaped[:, :, 1], shaped[:, :, 2])

    def ffn_act_of(normalized_row_block):
        return jnp.einsum(
            "wgu,uz->wgz",
            normalized_row_block,
            feedforward_input_weight,
            preferred_element_type=jnp.float32,
        )

    first_normalized = rms_scale(hidden, gain_one).astype(jnp.bfloat16)
    normed_all = lax.all_gather(first_normalized, "tp", axis=1, tiled=True)
    queries, key_heads, value_heads = project(normed_all)
    codes = bucket_codes(full_len)
    onehot = (
        codes[:, :, None] == jnp.arange(rel_table.shape[0], dtype=jnp.int32)[None, None, :]
    ).astype(jnp.bfloat16)
    bias = jnp.einsum("qkb,bh->hqk", onehot, rel_table, preferred_element_type=jnp.float32)
    places = jnp.arange(full_len, dtype=jnp.int32)
    key_valid = places[None, :] < lengths[:, None]

    def scores_of(query_part, key_part):
        raw = (
            jnp.einsum("sqhe,skhe->shqk", query_part, key_part, preferred_element_type=jnp.float32)
            + bias[None]
        )
        return jnp.where(key_valid[:, None, None, :], raw, -1000000000.0)

    scores = scores_of(queries, key_heads)
    row_max = jnp.max(scores, axis=-1, keepdims=True)
    exp_scores = jnp.exp(scores - row_max)
    row_total = jnp.sum(exp_scores, axis=-1, keepdims=True)
    attn_probs = exp_scores / row_total
    log_total = row_max + jnp.log(row_total)
    attention_mixture = jnp.einsum(
        "shqk,skhe->sqhe",
        attn_probs.astype(jnp.bfloat16),
        value_heads,
        preferred_element_type=jnp.float32,
    )
    attention_mixture = attention_mixture.reshape(seq_count, full_len, inner_width).astype(
        jnp.bfloat16
    )
    residual_branch = lax.psum_scatter(
        jnp.einsum(
            "wcr,rg->wcg",
            attention_mixture,
            attention_output_weight,
            preferred_element_type=jnp.float32,
        ).astype(jnp.bfloat16),
        "tp",
        scatter_dimension=1,
        tiled=True,
    ).astype(jnp.float32)
    middle = hidden + residual_branch
    second_normalized = rms_scale(middle, gain_two).astype(jnp.bfloat16)
    normed_two_all = lax.all_gather(second_normalized, "tp", axis=1, tiled=True)
    feedforward_activation = ffn_act_of(normed_two_all)
    gelu_output = gelu_of(feedforward_activation).astype(jnp.bfloat16)
    feedforward_branch = lax.psum_scatter(
        jnp.einsum(
            "jpi,ic->jpc",
            gelu_output,
            feedforward_output_weight,
            preferred_element_type=jnp.float32,
        ).astype(jnp.bfloat16),
        "tp",
        scatter_dimension=1,
        tiled=True,
    ).astype(jnp.float32)
    result = middle + feedforward_branch
    counts = (lengths - inst_lengths).astype(jnp.float32)
    local_places = offset + jnp.arange(shard_len, dtype=jnp.int32)
    local_mask = (
        (local_places[None, :] >= inst_lengths[:, None])
        & (local_places[None, :] < lengths[:, None])
    ).astype(jnp.float32)
    pooled_terms = jnp.sum(result * local_mask[:, :, None], axis=1) / counts[:, None]
    pooled = lax.psum_scatter(pooled_terms, "tp", scatter_dimension=1, tiled=True)
    cot_rows, cot_pool = (
        lax.all_gather(grad_output, "tp", axis=1, tiled=True),
        lax.all_gather(grad_pooled, "tp", axis=1, tiled=True),
    )
    full_mask = ((places[None, :] >= inst_lengths[:, None]) & key_valid).astype(jnp.float32)
    grad_result_all = (
        cot_rows.astype(jnp.float32)
        + cot_pool.astype(jnp.float32)[:, None, :] * (full_mask / counts[:, None])[:, :, None]
    )
    feedforward_branch_gradient = grad_result_all.astype(jnp.bfloat16)
    grad_result = lax.dynamic_slice_in_dim(grad_result_all, offset, shard_len, 1)
    second_normalized_taken = lax.all_gather(second_normalized, "tp", axis=1, tiled=True)
    act_used = ffn_act_of(second_normalized_taken)
    gelu_taken = gelu_of(act_used).astype(jnp.bfloat16)
    grad_gelu = jnp.einsum(
        "hpg,cg->hpc",
        feedforward_branch_gradient,
        feedforward_output_weight,
        preferred_element_type=jnp.float32,
    ).astype(jnp.bfloat16)
    activation_gradient = gelu_backward(act_used, grad_gelu)
    grad_w_ffn_out = jnp.einsum(
        "iab,iah->bh", gelu_taken, feedforward_branch_gradient, preferred_element_type=jnp.float32
    )
    grad_w_in = jnp.einsum(
        "bnp,bni->pi",
        second_normalized_taken,
        activation_gradient,
        preferred_element_type=jnp.float32,
    )
    grad_normed_two = lax.psum_scatter(
        jnp.einsum(
            "gyj,qj->gyq",
            activation_gradient,
            feedforward_input_weight,
            preferred_element_type=jnp.float32,
        ).astype(jnp.bfloat16),
        "tp",
        scatter_dimension=1,
        tiled=True,
    ).astype(jnp.float32)
    norm_two_value, norm_two_back = jax.vjp(rms_scale, middle, gain_two)
    grad_from_two, gain_ffn_part = norm_two_back(grad_normed_two)
    grad_middle = grad_result + grad_from_two
    branch_gradient_total = lax.all_gather(
        grad_middle.astype(jnp.bfloat16), "tp", axis=1, tiled=True
    )
    first_normalized_taken = lax.all_gather(first_normalized, "tp", axis=1, tiled=True)
    queries_used, keys_used, values_used = project(first_normalized_taken)
    probs_used = jnp.exp(scores_of(queries_used, keys_used) - log_total)
    mixed_again = jnp.einsum(
        "shqk,skhe->sqhe",
        probs_used.astype(jnp.bfloat16),
        values_used,
        preferred_element_type=jnp.float32,
    )
    attention_mixture_taken = mixed_again.reshape(seq_count, full_len, inner_width).astype(
        jnp.bfloat16
    )
    grad_w_out = jnp.einsum(
        "cur,cuz->rz",
        attention_mixture_taken,
        branch_gradient_total,
        preferred_element_type=jnp.float32,
    )
    grad_mixed = jnp.einsum(
        "vkc,xc->vkx",
        branch_gradient_total,
        attention_output_weight,
        preferred_element_type=jnp.float32,
    ).astype(jnp.bfloat16)
    grad_mixed = grad_mixed.reshape(seq_count, full_len, head_count, head_size)
    probs_low = probs_used.astype(jnp.bfloat16)
    grad_values = jnp.einsum(
        "shqk,sqhe->skhe", probs_low, grad_mixed, preferred_element_type=jnp.float32
    ).astype(jnp.bfloat16)
    grad_probs = jnp.einsum(
        "sqhe,skhe->shqk", grad_mixed, values_used, preferred_element_type=jnp.float32
    )
    row_dot = jnp.sum(probs_used * grad_probs, axis=-1, keepdims=True)
    grad_scores = (probs_used * (grad_probs - row_dot)).astype(jnp.bfloat16)
    grad_queries = jnp.einsum(
        "shqk,skhe->sqhe", grad_scores, keys_used, preferred_element_type=jnp.float32
    ).astype(jnp.bfloat16)
    grad_keys = jnp.einsum(
        "shqk,sqhe->skhe", grad_scores, queries_used, preferred_element_type=jnp.float32
    ).astype(jnp.bfloat16)
    grad_table = jnp.sum(
        jnp.einsum("qkb,shqk->sbh", onehot, grad_scores, preferred_element_type=jnp.float32), axis=0
    )
    combined_gradient = jnp.concatenate(
        (
            grad_queries.reshape(seq_count, full_len, inner_width),
            grad_keys.reshape(seq_count, full_len, inner_width),
            grad_values.reshape(seq_count, full_len, inner_width),
        ),
        axis=-1,
    )
    grad_w_joint = jnp.einsum(
        "hxq,hxo->qo", first_normalized_taken, combined_gradient, preferred_element_type=jnp.float32
    )
    grad_normed = lax.psum_scatter(
        jnp.einsum(
            "zhv,xv->zhx", combined_gradient, combined_weight, preferred_element_type=jnp.float32
        ).astype(jnp.bfloat16),
        "tp",
        scatter_dimension=1,
        tiled=True,
    ).astype(jnp.float32)
    norm_one_value, norm_one_back = jax.vjp(rms_scale, hidden, gain_one)
    grad_from_one, gain_attn_part = norm_one_back(grad_normed)
    grad_hidden = grad_middle + grad_from_one
    summed_joint, summed_out, summed_in, summed_ffn_out, summed_table = lax.psum(
        (grad_w_joint, grad_w_out, grad_w_in, grad_w_ffn_out, grad_table), "dp"
    )
    summed_gain_attn, summed_gain_ffn = lax.psum((gain_attn_part, gain_ffn_part), ("dp", "tp"))
    return (
        result.astype(jnp.bfloat16),
        pooled,
        grad_hidden,
        summed_joint[:, :inner_width],
        summed_joint[:, inner_width : 2 * inner_width],
        summed_joint[:, 2 * inner_width :],
        summed_out,
        summed_in,
        summed_ffn_out,
        summed_table,
        summed_gain_attn,
        summed_gain_ffn,
    )


def solution(mesh):
    in_specs = (
        P("dp", "tp", None),
        P("dp"),
        P("dp"),
        P(None, "tp"),
        P(None, "tp"),
        P(None, "tp"),
        P("tp", None),
        P(None, "tp"),
        P("tp", None),
        P(None, "tp"),
        P(),
        P(),
        P("dp", "tp", None),
        P("dp", "tp"),
    )
    out_specs = (
        P("dp", "tp", None),
        P("dp", "tp"),
        P("dp", "tp", None),
        P(None, "tp"),
        P(None, "tp"),
        P(None, "tp"),
        P("tp", None),
        P(None, "tp"),
        P("tp", None),
        P(None, "tp"),
        P(),
        P(),
    )
    return jax.shard_map(local, mesh=mesh, in_specs=in_specs, out_specs=out_specs, check_vma=False)
```

profile of v0, /device:TPU:0, one launch (start us, length us, event | category | flops | bytes accessed | tf_op | source)
XLA Modules:
  0.0 676.0 jit_solution(3572276359953765433)
XLA Ops:
  11.9 8.6 %iota_compare_fusion = pred[512,512,32]{0,2,1:T(32,128)(4,1)} fusion(s32[512,512]{0,1:T(8,128)S(1)} %fusion.48), kind=kLoop, calls=%fused_computation | loop fusion | flops 8388608 | bytes 9437184 | tf_op jit(solution)/shard_map/eq | solution.py:78
  20.5 46.4 %copy.70 = pred[512,512,32]{1,2,0:T(32,128)(4,1)} copy(pred[512,512,32]{0,2,1:T(32,128)(4,1)} %iota_compare_fusion) | data formatting | bytes 16777216 | tf_op jit(solution)/shard_map/eq | solution.py:78
  66.9 9.3 %convolution_bitcast_fusion = f32[3,512,512]{2,0,1:T(4,128)} fusion(pred[512,512,32]{1,2,0:T(32,128)(4,1)} %copy.70, bf16[32,3]{0,1:T(4,128)(2,1)S(1)} %copy-done.46), kind=kOutput, calls=%fused_computation.35 | convolution fusion | flops 50331648 | bytes 11534528 | tf_op jit(solution)/shard_map/qkb,bh->hqk/dot_general | solution.py:80
  76.1 5.1 copy.71
  81.4 3.4 convolution_convert_fusion.4
  95.2 50.8 %reduce-scatter.8.cloned.1.call-done = bf16[3,128,768]{2,1,0:T(8,128)(2,1)} async-done(((bf16[3,512,768]{2,1,0:T(8,128)(2,1)}), bf16[3,128,768]{2,1,0:T(8,128)(2,1)}) %reduce-scatter.8.cloned.1.call-update) | async-done | bytes 589840 | tf_op jit(solution)/shard_map/reduce_scatter | solution.py:106
  150.7 12.1 %all-gather = bf16[4,192,3]{1,2,0:T(4,128)(2,1)S(1)} all-gather(bf16[1,192,3]{1,2,0:T(4,128)(2,1)} %bitcast.131), channel_id=1, replica_groups=mesh['dp'=8,'tp'=4] {'tp'}, dimensions={0}, use_global_device_ids=true | all-gather | bytes 5760 | tf_op jit(solution)/shard_map/all_gather | solution.py:144
  167.3 32.8 %all-gather.8.cloned.1.call-done = bf16[3,512,768]{2,1,0:T(8,128)(2,1)} async-done(((bf16[3,128,768]{2,1,0:T(8,128)(2,1)}), bf16[3,512,768]{2,1,0:T(8,128)(2,1)}) %all-gather.8.cloned.1.call-update) | async-done | bytes 2359312 | tf_op jit(solution)/shard_map/all_gather | solution.py:119
  200.2 5.9 fusion.34
  206.1 44.8 %all-gather.10.cloned.1.call-done = bf16[3,512,768]{2,1,0:T(8,128)(2,1)} async-done(((bf16[3,128,768]{2,1,0:T(8,128)(2,1)}), bf16[3,512,768]{2,1,0:T(8,128)(2,1)}) %all-gather.10.cloned.1.call-update) | async-done | bytes 2359312 | tf_op jit(solution)/shard_map/all_gather | solution.py:143
  250.9 7.2 %fusion.7 = bf16[3,512,768]{2,1,0:T(8,128)(2,1)S(1)} fusion(f32[3,512,768]{2,1,0:T(8,128)} %fusion.34, bf16[768,768]{1,0:T(8,128)(2,1)} %param.22, bf16[3,512,768]{2,1,0:T(8,128)(2,1)} %all-gather.10.cloned.1.call-done, f32[3,512]{1,0:T(4,128)} %convert_divide_fusion, f32[3,768]{1,0:T(4,128)} %bitcast.128), kind=kOutput, calls=%fused_computation.18 | convolution fusion | flops 1842610176 | bytes 10632192 | tf_op jit(solution)/shard_map/hpg,cg->hpc/dot_general | solution.py:156
  259.6 3.4 convolution_convert_fusion.1
  264.3 6.7 convolution_convert_fusion.2
  272.3 4.4 multiply_add_fusion
  276.7 33.4 %reduce-scatter.12.cloned.1.call-done = bf16[3,128,768]{2,1,0:T(8,128)(2,1)} async-done(((bf16[3,512,768]{2,1,0:T(8,128)(2,1)}), bf16[3,128,768]{2,1,0:T(8,128)(2,1)}) %reduce-scatter.12.cloned.1.call-update) | async-done | bytes 589840 | tf_op jit(solution)/shard_map/reduce_scatter | solution.py:172
  310.1 50.3 %reduce-scatter.10.cloned.1.call-done = bf16[3,128,768]{2,1,0:T(8,128)(2,1)} async-done(((bf16[3,512,768]{2,1,0:T(8,128)(2,1)}), bf16[3,128,768]{2,1,0:T(8,128)(2,1)}) %reduce-scatter.10.cloned.1.call-update) | async-done | bytes 589840 | tf_op jit(solution)/shard_map/reduce_scatter | solution.py:122
  360.4 3.4 fusion.25
  368.9 6.2 convolution_convert_fusion.5
  375.1 3.5 convolution_bitcast_fusion.2
  378.6 6.7 convolution_bitcast_fusion.1
  388.0 29.7 %all-gather.12.cloned.1.call-done = bf16[3,512,768]{2,1,0:T(8,128)(2,1)} async-done(((bf16[3,128,768]{2,1,0:T(8,128)(2,1)}), bf16[3,512,768]{2,1,0:T(8,128)(2,1)}) %all-gather.12.cloned.1.call-update) | async-done | bytes 2359312 | tf_op jit(solution)/shard_map/all_gather | solution.py:186
  420.3 6.1 convolution_convert_fusion.6
  426.3 7.6 %multiply_reduce_fusion = (f32[3,3,512]{2,1,0:T(4,128)}, f32[3,3,512,512]{2,3,1,0:T(8,128)}) fusion(f32[3,3,512,512]{2,3,1,0:T(8,128)} %copy-done.2, f32[3,3,512]{2,1,0:T(4,128)S(1)} %copy-done.20, bf16[3,512,3,64]{1,3,2,0:T(8,128)(2,1)S(1)} %bitcast.117, bf16[3,512,3,3,64]{1,4,3,2,0:T(8,128)(2,1)S(1)} %bitcast.113), kind=kOutput, calls=%fused_computation.4 | convolution fusion | flops 309063168 | bytes 20097024 | tf_op jit(solution)/shard_map/sqhe,skhe->shqk/dot_general | solution.py:218
  434.0 11.2 %multiply_convert_fusion = bf16[3,3,512,512]{2,3,1,0:T(8,128)(2,1)} fusion(f32[3,3,512,512]{2,3,1,0:T(8,128)} %get-tuple-element.30, f32[3,3,512,512]{2,3,1,0:T(8,128)} %copy-done.2, f32[3,3,512]{2,1,0:T(4,128)} %get-tuple-element.29, f32[3,3,512]{2,1,0:T(4,128)} %copy-done.19), kind=kLoop, calls=%fused_computation.3 | loop fusion | flops 9437184 | bytes 23629824 | tf_op jit(solution)/shard_map/convert_element_type | solution.py:222
  445.2 4.0 convolution_convert_fusion.7
  457.1 4.6 convolution_convert_fusion
  463.4 12.6 %fusion.43 = f32[3,32]{1,0:T(4,128)S(1)} fusion(bf16[3,3,512,512]{2,3,1,0:T(8,128)(2,1)} %multiply_convert_fusion, s32[512,512]{0,1:T(8,128)S(1)} %copy-done.9), kind=kOutput, calls=%fused_computation.82 | convolution fusion | flops 159383744 | bytes 5767552 | tf_op jit(solution)/shard_map/qkb,shqk->sbh/dot_general | solution.py:230
  476.0 15.6 %psum.53 = f32[32,3]{0,1:T(4,128)} all-reduce(f32[32,3]{0,1:T(4,128)S(1)} %bitcast.132), channel_id=1, replica_groups=mesh['dp'=8,'tp'=4] {'dp'}, use_global_device_ids=true, to_apply=%region_18.19 | all-reduce | flops 96 | bytes 768 | tf_op jit(solution)/shard_map/psum | solution.py:254
  491.5 76.8 %all-reduce.4.cloned.1.call-done = (f32[768,576]{0,1:T(8,128)}, f32[192,768]{1,0:T(8,128)}, f32[768,768]{1,0:T(8,128)}, f32[768,768]{1,0:T(8,128)}) async-done(((f32[768,576]{0,1:T(8,128)}, f32[192,768]{1,0:T(8,128)}, f32[768,768]{1,0:T(8,128)}, f32[768,768]{1,0:T(8,128)}), (f32[768,576]{0,1:T(8,128)}, f32[192,768]{1,0:T(8,128)}, f32[768,768]{1,0:T(8,128)}, ...) | async-done | bytes 7077904 | tf_op jit(solution)/shard_map/psum | solution.py:254
  571.0 48.3 %reduce-scatter.14.cloned.1.call-done = bf16[3,128,768]{2,1,0:T(8,128)(2,1)} async-done(((bf16[3,512,768]{2,1,0:T(8,128)(2,1)}), bf16[3,128,768]{2,1,0:T(8,128)(2,1)}) %reduce-scatter.14.cloned.1.call-update) | async-done | bytes 589840 | tf_op jit(solution)/shard_map/reduce_scatter | solution.py:243
  621.0 39.8 %all-reduce = (f32[768]{0:T(1024)}, f32[768]{0:T(1024)}) all-reduce(f32[768]{0:T(1024)S(1)} %get-tuple-element.15, f32[768]{0:T(1024)S(1)} %copy-done.39), channel_id=1, replica_groups=mesh['dp'=8,'tp'=4] {'dp','tp'}, use_global_device_ids=true, to_apply=%region_20.21 | all-reduce | flops 1536 | bytes 12288 | tf_op jit(solution)/shard_map/psum | solution.py:257
  660.9 3.3 fusion.28
  (162 shorter events, 57.1 us)
Async XLA Ops:
  7.2 193.0 %copy-start = (bf16[768,768]{1,0:T(8,128)(2,1)S(1)}, bf16[768,768]{1,0:T(8,128)(2,1)}, u32[]{:S(2)}) copy-start(bf16[768,768]{1,0:T(8,128)(2,1)} %param.21) | copy-start | bytes 3538948
  7.2 74.2 %all-gather.6.cloned.1.call-start = ((), (), s32[]{:S(2)}) async-start(), calls=%async_computation.5 | async-start | bytes 2949120 | tf_op jit(solution)/shard_map/all_gather | solution.py:74
  8.6 11.9 %copy-start.36 = (f32[3,128]{1,0:T(4,128)}, f32[3,128]{1,0:T(4,128)S(1)}, u32[]{:S(2)}) copy-start(f32[3,128]{1,0:T(4,128)S(1)} %fusion.29) | copy-start | bytes 4612
  11.4 134.6 %reduce-scatter.8.cloned.1.call-start = ((), (), s32[]{:S(2)}) async-start(), calls=%async_computation.6 | async-start | bytes 2949120 | tf_op jit(solution)/shard_map/reduce_scatter | solution.py:106
  11.9 8.6 %copy-start.8 = (s32[512,512]{0,1:T(8,128)}, s32[512,512]{0,1:T(8,128)S(1)}, u32[]{:S(2)}) copy-start(s32[512,512]{0,1:T(8,128)S(1)} %fusion.48) | copy-start | bytes 3145732
  20.5 46.4 %copy-start.46 = (bf16[32,3]{0,1:T(4,128)(2,1)S(1)}, bf16[32,3]{0,1:T(4,128)(2,1)}, u32[]{:S(2)}) copy-start(bf16[32,3]{0,1:T(4,128)(2,1)} %param.23) | copy-start | bytes 580
  76.1 5.2 copy-start.40
  76.1 5.2 copy-start.50
  76.1 5.2 copy-start.51
  92.8 53.2 %copy-start.4 = (bf16[3,128,768]{2,1,0:T(8,128)(2,1)S(1)}, bf16[3,128,768]{2,1,0:T(8,128)(2,1)}, u32[]{:S(2)}) copy-start(bf16[3,128,768]{2,1,0:T(8,128)(2,1)} %param.14) | copy-start | bytes 1769476
  95.1 105.1 %all-gather.8.cloned.1.call-start = ((), (), s32[]{:S(2)}) async-start(), calls=%async_computation.7 | async-start | bytes 2949120 | tf_op jit(solution)/shard_map/all_gather | solution.py:119
  150.0 100.9 %all-gather.10.cloned.1.call-start = ((), (), s32[]{:S(2)}) async-start(), calls=%async_computation.9 | async-start | bytes 2949120 | tf_op jit(solution)/shard_map/all_gather | solution.py:143
  150.6 159.4 %reduce-scatter.12.cloned.1.call-start = ((), (), s32[]{:S(2)}) async-start(), calls=%async_computation.10 | async-start | bytes 2949120 | tf_op jit(solution)/shard_map/reduce_scatter | solution.py:172
  263.0 97.3 %reduce-scatter.10.cloned.1.call-start = ((), (), s32[]{:S(2)}) async-start(), calls=%async_computation.8 | async-start | bytes 2949120 | tf_op jit(solution)/shard_map/reduce_scatter | solution.py:122
  271.0 146.7 %all-gather.12.cloned.1.call-start = ((), (), s32[]{:S(2)}) async-start(), calls=%async_computation.11 | async-start | bytes 2949120 | tf_op jit(solution)/shard_map/all_gather | solution.py:186
  272.3 88.1 %copy-start.6 = (bf16[3,128,768]{2,1,0:T(8,128)(2,1)S(1)}, bf16[3,128,768]{2,1,0:T(8,128)(2,1)}, u32[]{:S(2)}) copy-start(bf16[3,128,768]{2,1,0:T(8,128)(2,1)} %reduce-scatter.8.cloned.1.call-done) | copy-start | bytes 1769476
  310.1 55.0 %copy-start.7 = (bf16[3,128,768]{2,1,0:T(8,128)(2,1)S(1)}, bf16[3,128,768]{2,1,0:T(8,128)(2,1)}, u32[]{:S(2)}) copy-start(bf16[3,128,768]{2,1,0:T(8,128)(2,1)} %reduce-scatter.12.cloned.1.call-done) | copy-start | bytes 1769476
  367.6 94.2 %reduce-scatter.16.cloned.1.call-start = ((), (), s32[]{:S(2)}) async-start(), calls=%async_computation.13 | async-start | bytes 491520
  368.9 6.2 copy-start.19
  368.9 6.2 copy-start.10
  368.9 6.2 copy-start.13
  378.6 6.8 %copy-start.31 = (f32[3,768]{1,0:T(4,128)S(1)}, f32[3,768]{1,0:T(4,128)}, u32[]{:S(2)}) copy-start(f32[3,768]{1,0:T(4,128)} %get-tuple-element.14) | copy-start | bytes 27652
  378.6 6.8 copy-start.45
  387.7 180.6 %all-reduce.4.cloned.1.call-start = ((), (), s32[]{:S(2)}) async-start(), calls=%async_computation.14 | async-start | bytes 14155776 | tf_op jit(solution)/shard_map/psum | solution.py:254
  445.2 4.0 copy-start.3
  450.1 4.1 copy-start.23
  455.7 163.6 %reduce-scatter.14.cloned.1.call-start = ((), (), s32[]{:S(2)}) async-start(), calls=%async_computation.12 | async-start | bytes 2949120 | tf_op jit(solution)/shard_map/reduce_scatter | solution.py:243
  568.4 52.7 %copy-start.37 = (f32[3,128]{1,0:T(4,128)S(1)}, f32[3,128]{1,0:T(4,128)}, u32[]{:S(2)}) copy-start(f32[3,128]{1,0:T(4,128)} %copy-done.36) | copy-start | bytes 4612
  568.4 52.7 %copy-start.39 = (f32[768]{0:T(1024)S(1)}, f32[768]{0:T(1024)}, u32[]{:S(2)}) copy-start(f32[768]{0:T(1024)} %get-tuple-element.12) | copy-start | bytes 9220
  568.4 92.5 %copy-start.35 = (f32[3,128]{1,0:T(4,128)S(1)}, f32[3,128]{1,0:T(4,128)}, u32[]{:S(2)}) copy-start(f32[3,128]{1,0:T(4,128)} %copy-done.34) | copy-start | bytes 4612
  660.9 4.1 copy-start.15
  665.0 3.9 copy-start.1
  (30 other events, 59.6 us)
Sparse Core Ops, SparseCore 0:
  11.5 53.1 all-gather.5
  95.2 50.7 reduce-scatter.7
  150.2 49.9 all-gather.7
  201.6 49.2 all-gather.9
  263.1 46.8 reduce-scatter.11
  312.8 47.5 reduce-scatter.9
  367.7 49.9 all-gather.11
  419.9 19.4 reduce-scatter.15
  455.8 112.4 all-reduce.3
  571.2 48.1 reduce-scatter.13
where the time goes:
time: 682 us; the launch traced here: 676 us
  waiting for transfers between devices  368 us (54%)
  matrix products  101 us (15%)
  local copies, waits for them, and re-layouts  73.5 us (11%)
  blocking collectives  67.5 us (10%)
  other arithmetic  49.9 us (7%)
  between operations  14.8 us (2%)
    psum x1, waiting for transfers between devices, local(): lax.psum((grad_w_joint, grad_w_out, grad_w_in, grad_w_ffn_out, grad_table...  76.8 us
    reduce_scatter x1, waiting for transfers between devices, local(): lax.psum_scatter(jnp.einsum('wcr,rg->wcg', attention_mixture, attention_o...  50.8 us
    reduce_scatter x1, waiting for transfers between devices, local(): lax.psum_scatter(jnp.einsum('jpi,ic->jpc', gelu_output, feedforward_outpu...  50.3 us
    reduce_scatter x1, waiting for transfers between devices, local(): lax.psum_scatter(jnp.einsum('zhv,xv->zhx', combined_gradient, combined_we...  48.3 us
    eq x1, local copies, waits for them, and re-layouts, local(): codes[:, :, None]  46.4 us
    all_gather x1, waiting for transfers between devices, local(): lax.all_gather(grad_output, 'tp', axis=1, tiled=True)  44.8 us
    psum x1, blocking collectives, local(): lax.psum((gain_attn_part, gain_ffn_part), ('dp', 'tp'))  39.8 us
    reduce_scatter x1, waiting for transfers between devices, local(): lax.psum_scatter(jnp.einsum('gyj,qj->gyq', activation_gradient, feedforwa...  33.4 us
  transfers between devices with their start and end apart: 10, of which 8 were waited for; matrix products, arithmetic and copies ran while one was open for 25% of the time, Pallas kernels for 0%

commit v1 on v0

v1 whole, which is shorter than its diff:
```python
import functools

import jax
import jax.numpy as jnp
from jax import lax
from jax.experimental import pallas as pl
from jax.experimental.pallas import tpu as pltpu
from jax.sharding import PartitionSpec as P

F32 = jnp.float32
BF16 = jnp.bfloat16
EPS = 1e-06
NEG = -1000000000.0
THRESHOLDS = (12, 16, 23, 32, 46, 64, 91)
GELU_C = 0.7978845608028654
GELU_K = 0.044715
WIDE = pl.BlockSpec(memory_space=pltpu.VMEM)
SCALARS = pl.BlockSpec(memory_space=pltpu.SMEM)


def dot(left, right, left_dim, right_dim, precision=None):
    return lax.dot_general(
        left,
        right,
        (((left_dim,), (right_dim,)), ((), ())),
        preferred_element_type=F32,
        precision=precision,
    )


def code_of(delta):
    n = abs(delta)
    far = 8 + sum(1 for threshold in THRESHOLDS if n >= threshold)
    return (16 if delta > 0 else 0) + (n if n < 8 else far)


def code_block(size, distance):
    shape = (size, size)
    delta = (
        lax.broadcasted_iota(jnp.int32, shape, 0)
        - lax.broadcasted_iota(jnp.int32, shape, 1)
        + size * distance
    )
    n = jnp.abs(delta)
    far = jnp.full(shape, 8, jnp.int32)
    for threshold in THRESHOLDS:
        far = far + (n >= threshold).astype(jnp.int32)
    return jnp.where(delta > 0, 16, 0) + jnp.where(n < 8, n, far)


def codes_in(size, distance):
    return sorted(
        {code_of(size * distance + inner) for inner in range(1 - size, size)}
    )


def row_block(*shape):
    return pl.BlockSpec((1,) + shape, lambda r: (r,) + (0,) * len(shape))


def fixed(*shape):
    return pl.BlockSpec(shape, lambda r: (0,) * len(shape))


def cost(micros):
    return pl.CostEstimate(
        flops=int(micros * 1.1e9), bytes_accessed=int(micros * 1e6), transcendentals=0
    )


def shaped(shape, dtype):
    return jax.ShapeDtypeStruct(shape, dtype)


def norm_kernel(x_ref, gain_ref, out_ref):
    x = x_ref[0].astype(F32)
    scale = lax.rsqrt(jnp.mean(x * x, axis=-1, keepdims=True) + EPS)
    out_ref[0] = (x * scale * gain_ref[...]).astype(BF16)


def norm_one(hidden, gain):
    rows, size, width = hidden.shape
    return pl.pallas_call(
        norm_kernel,
        grid=(rows,),
        in_specs=[row_block(size, width), fixed(1, width)],
        out_specs=row_block(size, width),
        out_shape=shaped(hidden.shape, BF16),
        cost_estimate=cost(2),
        name="norm_one",
    )(hidden, gain)


def bias_kernel(parts, size, table_ref, out_ref):
    heads = out_ref.shape[0]
    for at in range(2 * parts - 1):
        distance = at - (parts - 1)
        present = codes_in(size, distance)
        codes = code_block(size, distance) if len(present) > 1 else None
        for head in range(heads):
            block = jnp.full((size, size), table_ref[head, present[0]], F32)
            for code in present[1:]:
                block = jnp.where(codes == code, table_ref[head, code], block)
            out_ref[head, at] = block


def bias_blocks(table, parts, size):
    heads = table.shape[0]
    return pl.pallas_call(
        functools.partial(bias_kernel, parts, size),
        in_specs=[SCALARS],
        out_specs=WIDE,
        out_shape=shaped((heads, 2 * parts - 1, size, size), F32),
        cost_estimate=cost(3),
        name="bias_blocks",
    )(table)


def chunk_bias(bias_ref, head, me, parts, first, count):
    return jnp.concatenate(
        [
            jnp.concatenate(
                [
                    bias_ref[head, (a_k ^ me) - (a_q ^ me) + parts - 1]
                    for a_q in range(first, first + count)
                ],
                axis=1,
            )
            for a_k in range(parts)
        ],
        axis=0,
    )


def chunk_valid(length, me, parts, size, count):
    inner = lax.broadcasted_iota(jnp.int32, (size, count * size), 0)
    return jnp.concatenate(
        [inner < length - (a_k ^ me) * size for a_k in range(parts)], axis=0
    )


def attend_kernel(
    heads,
    place_ref,
    length_ref,
    own_ref,
    pair_ref,
    far_low_ref,
    far_high_ref,
    last_low_ref,
    last_high_ref,
    query_ref,
    key_ref,
    value_ref,
    bias_ref,
    normed_ref,
    joint_ref,
    log_ref,
    *mixed_refs,
):
    parts = len(mixed_refs)
    size = own_ref.shape[1]
    me = place_ref[0]
    length = length_ref[pl.program_id(0)]
    normed_ref[0, 0:size] = own_ref[0]
    normed_ref[0, size : 2 * size] = pair_ref[0]
    normed_ref[0, 2 * size : 3 * size] = far_low_ref[0] + far_high_ref[0]
    normed_ref[0, 3 * size : 4 * size] = last_low_ref[0] + last_high_ref[0]
    inner = joint_ref.shape[1] // 3
    for part, ref in enumerate((query_ref, key_ref, value_ref)):
        joint_ref[0, part * inner : (part + 1) * inner] = dot(
            ref[...], normed_ref[0], 1, 1
        ).astype(BF16)
    head_size = inner // heads
    count = 2
    valid = chunk_valid(length, me, parts, size, count)
    for head in range(heads):
        low = head * head_size
        key = joint_ref[0, inner + low : inner + low + head_size, :]
        value = joint_ref[0, 2 * inner + low : 2 * inner + low + head_size, :]
        for first in range(0, parts, count):
            lanes = slice(first * size, (first + count) * size)
            query = joint_ref[0, low : low + head_size, lanes]
            scores = dot(key, query, 0, 0) + chunk_bias(
                bias_ref, head, me, parts, first, count
            )
            scores = jnp.where(valid, scores, NEG)
            peak = jnp.max(scores, axis=0, keepdims=True)
            raised = jnp.exp(scores - peak)
            total = jnp.sum(raised, axis=0, keepdims=True)
            mixed = (dot(value, raised.astype(BF16), 1, 0) / total).astype(BF16)
            for step in range(count):
                mixed_refs[first + step][0, low : low + head_size, :] = mixed[
                    :, step * size : (step + 1) * size
                ]
            log_ref[0, head : head + 1, lanes] = peak + jnp.log(total)


def attend(place, lengths, blocks, weights, bias, heads):
    rows, size, width = blocks[0].shape
    parts = (bias.shape[1] + 1) // 2
    full = parts * size
    inner = weights[0].shape[0]
    joint = 3 * inner
    return pl.pallas_call(
        functools.partial(attend_kernel, heads),
        grid=(rows,),
        in_specs=[SCALARS, SCALARS]
        + [row_block(size, width)] * 6
        + [fixed(inner, width)] * 3
        + [fixed(*bias.shape)],
        out_specs=[row_block(full, width), row_block(joint, full), row_block(heads, full)]
        + [row_block(inner, size)] * parts,
        out_shape=[
            shaped((rows, full, width), BF16),
            shaped((rows, joint, full), BF16),
            shaped((rows, heads, full), F32),
        ]
        + [shaped((rows, inner, size), BF16)] * parts,
        cost_estimate=cost(13),
        name="attend",
    )(place, lengths, *blocks, *weights, bias)


def middle_kernel(weight_ref, hidden_ref, gain_ref, *refs):
    mixed_refs, (middle_ref, normed_ref) = refs[:-2], refs[-2:]
    branch = sum(
        dot(ref[0], weight_ref[a], 0, 0) for a, ref in enumerate(mixed_refs)
    )
    middle = hidden_ref[0].astype(F32) + branch
    scale = lax.rsqrt(jnp.mean(middle * middle, axis=-1, keepdims=True) + EPS)
    middle_ref[0] = middle
    normed_ref[0] = (middle * scale * gain_ref[...]).astype(BF16)


def middle_of(gathered, hidden, gain, mixed):
    rows, size, width = hidden.shape
    inner = mixed[0].shape[1]
    return pl.pallas_call(
        middle_kernel,
        grid=(rows,),
        in_specs=[fixed(*gathered.shape), row_block(size, width), fixed(1, width)]
        + [row_block(inner, size)] * len(mixed),
        out_specs=[row_block(size, width)] * 2,
        out_shape=[shaped(hidden.shape, F32), shaped(hidden.shape, BF16)],
        cost_estimate=cost(4),
        name="middle_of",
    )(gathered, hidden, gain, *mixed)


def ffn_kernel(chained, *refs):
    normed_ref, grad_ref = refs[:2]
    in_refs, out_refs = refs[2:4], refs[4:6]
    gelu_ref, act_ref, branch_ref, back_ref, branch_sum, back_sum = refs[
        6 + chained :
    ]
    step = pl.program_id(0)
    normed = normed_ref[...]
    grad = grad_ref[...]
    branch = back = None
    for shard in range(2):
        weight_in = in_refs[shard][...]
        weight_out = out_refs[shard][...]
        v = dot(normed, weight_in, 1, 0)
        grad_gelu = dot(grad, weight_out, 1, 1).astype(BF16).astype(F32)
        square = v * v
        bent = jnp.tanh(GELU_C * (v + GELU_K * (square * v)))
        half = 0.5 * (1.0 + bent)
        gelu = (v * half).astype(BF16)
        slope = half + (0.5 * GELU_C) * v * (1.0 - bent * bent) * (
            1.0 + (3.0 * GELU_K) * square
        )
        grad_act = (grad_gelu * slope).astype(BF16)
        gelu_ref[shard] = gelu
        act_ref[shard] = grad_act
        more = dot(gelu, weight_out, 1, 0)
        more_back = dot(grad_act, weight_in, 1, 1)
        branch = more if branch is None else branch + more
        back = more_back if back is None else back + more_back

    @pl.when(step == 0)
    def _():
        branch_sum[...] = branch
        back_sum[...] = back

    @pl.when(step > 0)
    def _():
        branch_sum[...] += branch
        back_sum[...] += back

    @pl.when(step == pl.num_programs(0) - 1)
    def _():
        branch_ref[...] = branch_sum[...].astype(branch_ref.dtype)
        back_ref[...] = back_sum[...].astype(back_ref.dtype)


def feed_forward(normed, grad, w_in, w_out, other, half, kept, dtype):
    tokens, width = normed.shape
    units = w_in.shape[1]
    cut = 256 if units % 256 == 0 else units
    down = width // cut
    token_block = pl.BlockSpec((2, tokens, cut), lambda c: (0, half, c))
    in_specs = [
        fixed(tokens, width),
        fixed(tokens, width),
        pl.BlockSpec((width, cut), lambda c: (0, c)),
        pl.BlockSpec((width, cut), lambda c: (0, c)),
        pl.BlockSpec((cut, width), lambda c: (c, 0)),
        pl.BlockSpec((cut, width), lambda c: (c + down, 0)),
    ]
    args = [normed, grad, w_in, other, w_out, other]
    aliases = {}
    if kept is not None:
        in_specs += [pl.BlockSpec(memory_space=pl.ANY)] * 2
        args += list(kept)
        aliases = {6: 0, 7: 1}
    return pl.pallas_call(
        functools.partial(ffn_kernel, len(aliases)),
        grid=(units // cut,),
        in_specs=in_specs,
        out_specs=[token_block, token_block, fixed(tokens, width), fixed(tokens, width)],
        out_shape=[shaped((2, 2 * tokens, units), BF16)] * 2
        + [shaped((tokens, width), dtype)] * 2,
        scratch_shapes=[pltpu.VMEM((tokens, width), F32)] * 2,
        input_output_aliases=aliases,
        cost_estimate=cost(9),
        name="feed_forward",
    )(*args)


def middle_back_kernel(
    weight_ref,
    own_ref,
    other_ref,
    middle_ref,
    result_ref,
    gain_ref,
    grad_ref,
    low_ref,
    gain_grad_ref,
    *mixed_refs,
):
    back = own_ref[0] + other_ref[0].astype(F32)
    middle = middle_ref[0]
    scale = lax.rsqrt(jnp.mean(middle * middle, axis=-1, keepdims=True) + EPS)
    scaled = back * gain_ref[...]
    inner = jnp.mean(scaled * middle, axis=-1, keepdims=True)
    grad = result_ref[0] + scale * scaled - middle * (scale * scale * scale * inner)
    gain_grad = jnp.sum(back * (middle * scale), axis=0, keepdims=True)

    @pl.when(pl.program_id(0) == 0)
    def _():
        gain_grad_ref[...] = gain_grad

    @pl.when(pl.program_id(0) > 0)
    def _():
        gain_grad_ref[...] += gain_grad

    grad_ref[0] = grad
    low = grad.astype(BF16)
    low_ref[0] = low
    for a, ref in enumerate(mixed_refs):
        ref[0] = dot(weight_ref[a], low, 1, 1).astype(BF16)


def middle_back(gathered, own, other, middle, grad_result, gain):
    rows, size, width = middle.shape
    parts = gathered.shape[0]
    inner = gathered.shape[1]
    block = row_block(size, width)
    return pl.pallas_call(
        middle_back_kernel,
        grid=(rows,),
        in_specs=[fixed(*gathered.shape)] + [block] * 4 + [fixed(1, width)],
        out_specs=[block, block, fixed(1, width)] + [row_block(inner, size)] * parts,
        out_shape=[
            shaped(middle.shape, F32),
            shaped(middle.shape, BF16),
            shaped((1, width), F32),
        ]
        + [shaped((rows, inner, size), BF16)] * parts,
        cost_estimate=cost(5),
        name="middle_back",
    )(gathered, own, other, middle, grad_result, gain)


def attend_back_kernel(heads, parts, place_ref, length_ref, joint_ref, bias_ref, log_ref, *refs):
    mixed_refs = refs[:parts]
    joint_grads = refs[parts : 2 * parts]
    table_ref, sums = refs[2 * parts :]
    size = mixed_refs[0].shape[2]
    me = place_ref[0]
    row = pl.program_id(0)
    length = length_ref[row]
    inner = joint_ref.shape[1] // 3
    head_size = inner // heads
    count = 2

    @pl.when(row == 0)
    def _():
        sums[...] = jnp.zeros_like(sums)

    valid = chunk_valid(length, me, parts, size, count)
    for head in range(heads):
        low = head * head_size
        key = joint_ref[0, inner + low : inner + low + head_size, :]
        value = joint_ref[0, 2 * inner + low : 2 * inner + low + head_size, :]
        grad_key = grad_value = None
        for first in range(0, parts, count):
            lanes = slice(first * size, (first + count) * size)
            query = joint_ref[0, low : low + head_size, lanes]
            grad_mixed = jnp.concatenate(
                [mixed_refs[first + step][0, low : low + head_size, :] for step in range(count)],
                axis=1,
            )
            scores = dot(key, query, 0, 0) + chunk_bias(
                bias_ref, head, me, parts, first, count
            )
            probs = jnp.where(
                valid, jnp.exp(scores - log_ref[0, head : head + 1, lanes]), 0.0
            )
            grad_probs = dot(value, grad_mixed, 0, 0)
            inner_sum = jnp.sum(probs * grad_probs, axis=0, keepdims=True)
            grad_scores = probs * (grad_probs - inner_sum)
            low_scores = grad_scores.astype(BF16)
            more_value = dot(grad_mixed, probs.astype(BF16), 1, 1)
            more_key = dot(query, low_scores, 1, 1)
            grad_value = more_value if grad_value is None else grad_value + more_value
            grad_key = more_key if grad_key is None else grad_key + more_key
            grad_query = dot(key, low_scores, 1, 0).astype(BF16)
            for step in range(count):
                joint_grads[first + step][0, low : low + head_size, :] = grad_query[
                    :, step * size : (step + 1) * size
                ]
            for step in range(count):
                for a_k in range(parts):
                    at = (a_k ^ me) - ((first + step) ^ me) + parts - 1
                    sums[head, at] += grad_scores[
                        a_k * size : (a_k + 1) * size, step * size : (step + 1) * size
                    ]
        grad_key = grad_key.astype(BF16)
        grad_value = grad_value.astype(BF16)
        for a in range(parts):
            lanes = slice(a * size, (a + 1) * size)
            joint_grads[a][0, inner + low : inner + low + head_size, :] = grad_key[:, lanes]
            joint_grads[a][0, 2 * inner + low : 2 * inner + low + head_size, :] = grad_value[
                :, lanes
            ]

    @pl.when(row == pl.num_programs(0) - 1)
    def _():
        ones = jnp.ones((8, size), F32)
        for head in range(heads):
            lines = [jnp.zeros((1, size), F32)] * 32
            for at in range(2 * parts - 1):
                distance = at - (parts - 1)
                present = codes_in(size, distance)
                codes = code_block(size, distance) if len(present) > 1 else None
                block = sums[head, at]
                for code in present:
                    chosen = block if codes is None else jnp.where(codes == code, block, 0.0)
                    lines[code] = lines[code] + jnp.sum(chosen, axis=0, keepdims=True)
            lined = jnp.concatenate(lines + [jnp.zeros((size - 32, size), F32)], axis=0)
            table_ref[head] = dot(ones, lined, 1, 1, lax.Precision.HIGHEST)


def attend_back(place, lengths, joint, bias, logs, mixed):
    rows, wide, full = joint.shape
    parts = len(mixed)
    heads = bias.shape[0]
    inner, size = mixed[0].shape[1:]
    return pl.pallas_call(
        functools.partial(attend_back_kernel, heads, parts),
        grid=(rows,),
        in_specs=[
            SCALARS,
            SCALARS,
            row_block(wide, full),
            fixed(*bias.shape),
            row_block(heads, full),
        ]
        + [row_block(inner, size)] * parts,
        out_specs=[row_block(wide, size)] * parts + [fixed(heads, 8, size)],
        out_shape=[shaped((rows, wide, size), BF16)] * parts + [shaped((heads, 8, size), F32)],
        scratch_shapes=[pltpu.VMEM(bias.shape, F32)],
        cost_estimate=cost(15),
        name="attend_back",
    )(place, lengths, joint, bias, logs, *mixed)


def ffn_grad_kernel(normed_ref, normed_pair_ref, grad_ref, grad_pair_ref, gelu_ref, act_ref, out_ref):
    normed = jnp.concatenate((normed_ref[...], normed_pair_ref[...]), axis=0)
    grad = jnp.concatenate((grad_ref[...], grad_pair_ref[...]), axis=0)
    cuts = out_ref.shape[1]
    share = out_ref.shape[2] // 2
    for shard in range(2):
        for side, (left, right) in enumerate(
            ((normed, act_ref[shard]), (gelu_ref[shard], grad))
        ):
            total = dot(left, right, 0, 0).astype(BF16)
            for cut in range(cuts):
                out_ref[side, cut, shard * share : (shard + 1) * share] = total[
                    cut * share : (cut + 1) * share
                ]


def ffn_grad(normed, normed_pair, grad, grad_pair, gelu, act, copies):
    tokens, width = normed.shape
    units = gelu.shape[2]
    steps = 2
    share = (width + units) // copies
    return pl.pallas_call(
        ffn_grad_kernel,
        grid=(steps,),
        in_specs=[
            pl.BlockSpec((tokens, width // steps), lambda m: (0, m)),
            pl.BlockSpec((tokens, width // steps), lambda m: (0, m)),
            fixed(tokens, width),
            fixed(tokens, width),
            pl.BlockSpec((2, 2 * tokens, units // steps), lambda m: (0, 0, m)),
            fixed(2, 2 * tokens, units),
        ],
        out_specs=pl.BlockSpec(
            (2, copies // (2 * steps), 2 * share, width), lambda m: (0, m, 0, 0)
        ),
        out_shape=shaped((2, copies // 2, 2 * share, width), BF16),
        cost_estimate=cost(6),
        name="ffn_grad",
    )(normed, normed_pair, grad, grad_pair, gelu, act)


def joint_grad_kernel(
    parts, normed_ref, weight_ref, gain_ref, gain_two_ref, table_ref, branch_ref, *refs
):
    joint_grads = refs[:parts]
    mixed_refs = refs[parts : 2 * parts]
    out_ref, total, out_total = refs[2 * parts :]
    row = pl.program_id(0)
    grads = jnp.concatenate([ref[0] for ref in joint_grads], axis=1)
    mixed = jnp.concatenate([ref[0] for ref in mixed_refs], axis=0)
    more = dot(grads, normed_ref[0], 1, 0)
    more_out = dot(mixed, branch_ref[0], 1, 0)

    @pl.when(row == 0)
    def _():
        total[...] = more
        out_total[...] = more_out

    @pl.when(row > 0)
    def _():
        total[...] += more
        out_total[...] += more_out

    @pl.when(row == pl.num_programs(0) - 1)
    def _():
        wide, width = total.shape
        inner = mixed_refs[0].shape[1]
        cuts = out_ref.shape[0]
        gain_grad = (
            jnp.sum(total[...] * weight_ref[...].astype(F32), axis=0, keepdims=True)
            / gain_ref[...]
        )
        heads, _, size = table_ref.shape
        pad = jnp.zeros((1, width - size), F32)
        lines = [gain_grad, gain_two_ref[...]] + [
            jnp.concatenate([table_ref[head, 0:1], pad], axis=1) for head in range(heads)
        ]
        lines.append(jnp.zeros((8 - len(lines), width), F32))
        share, out_share = wide // cuts, inner // cuts
        for cut in range(cuts):
            out_ref[cut, 0:share] = total[cut * share : (cut + 1) * share].astype(BF16)
            at = share
            for a in range(parts):
                low = a * inner + cut * out_share
                out_ref[cut, at : at + out_share] = out_total[low : low + out_share].astype(BF16)
                at += out_share
            if cut == 0:
                out_ref[cut, at : at + 8] = jnp.concatenate(lines, axis=0).astype(BF16)
            else:
                out_ref[cut, at : at + 8] = jnp.zeros((8, width), BF16)


def joint_grad(
    normed, weights, gain, gain_two_grad, table_grad, grad_branch, joint_grads, mixed, copies
):
    rows, full, width = normed.shape
    wide, size = joint_grads[0].shape[1:]
    inner = mixed[0].shape[1]
    parts = len(joint_grads)
    cuts = copies if inner % (8 * copies) == 0 else 1
    length = (wide + parts * inner) // cuts + 8
    return pl.pallas_call(
        functools.partial(joint_grad_kernel, parts),
        grid=(rows,),
        in_specs=[
            row_block(full, width),
            fixed(wide, width),
            fixed(1, width),
            fixed(1, width),
            fixed(*table_grad.shape),
            row_block(size, width),
        ]
        + [row_block(wide, size)] * parts
        + [row_block(inner, size)] * parts,
        out_specs=fixed(cuts, length, width),
        out_shape=shaped((cuts, length, width), BF16),
        scratch_shapes=[pltpu.VMEM((wide, width), F32), pltpu.VMEM((parts * inner, width), F32)],
        cost_estimate=cost(6),
        name="joint_grad",
    )(normed, weights, gain, gain_two_grad, table_grad, grad_branch, *joint_grads, *mixed)


def recut(values, wide, parts, inner, copies):
    width = values.shape[2]
    whole = values[0]
    out = [whole[:wide].reshape(copies, -1, width)]
    for a in range(parts):
        low = wide + a * inner
        out.append(whole[low : low + inner].reshape(copies, -1, width))
    extra = whole[None, wide + parts * inner :]
    out.append(jnp.concatenate([extra] + [jnp.zeros_like(extra)] * (copies - 1), axis=0))
    return jnp.concatenate(out, axis=1)


def hidden_grad_kernel(place_ref, weight_ref, middle_ref, hidden_ref, gain_ref, *refs):
    joint_grads, out_ref = refs[:-1], refs[-1]
    me = place_ref[0]
    back = sum(dot(ref[0], weight_ref[a ^ me], 0, 0) for a, ref in enumerate(joint_grads))
    hidden = hidden_ref[0].astype(F32)
    scale = lax.rsqrt(jnp.mean(hidden * hidden, axis=-1, keepdims=True) + EPS)
    scaled = back * gain_ref[...]
    inner = jnp.mean(scaled * hidden, axis=-1, keepdims=True)
    out_ref[0] = middle_ref[0] + scale * scaled - hidden * (scale * scale * scale * inner)


def hidden_grad(place, gathered, grad_middle, hidden, gain, joint_grads):
    rows, size, width = hidden.shape
    wide = joint_grads[0].shape[1]
    block = row_block(size, width)
    return pl.pallas_call(
        hidden_grad_kernel,
        grid=(rows,),
        in_specs=[SCALARS, fixed(*gathered.shape), block, block, fixed(1, width)]
        + [row_block(wide, size)] * len(joint_grads),
        out_specs=block,
        out_shape=shaped(hidden.shape, F32),
        cost_estimate=cost(150),
        name="hidden_grad",
    )(place, gathered, grad_middle, hidden, gain, *joint_grads)


def after(values, *others):
    return lax.optimization_barrier((values, *others))[0]


def swap(values, distance):
    parts = lax.axis_size("tp")
    return lax.ppermute(values, "tp", [(i, i ^ distance) for i in range(parts)])


def swap_all(blocks):
    return [blocks[0]] + [swap(block, a) for a, block in enumerate(blocks) if a]


def gather_line(values, first, second):
    pair = swap(values, 1)
    inner = [(1, 2), (2, 1)]
    outer = [(1, 0), (2, 3)]
    last_low = lax.ppermute(values, "tp", inner)
    pair, last_low, *first = lax.optimization_barrier((pair, last_low, *first))
    far_low = lax.ppermute(pair, "tp", inner)
    far_high = lax.ppermute(last_low, "tp", outer)
    far_low, far_high, *second = lax.optimization_barrier((far_low, far_high, *second))
    last_high = lax.ppermute(far_low, "tp", outer)
    return [values, pair, far_low, far_high, last_low, last_high], first, second


def across(values, bit):
    count = lax.axis_size("dp")
    return lax.ppermute(values, "dp", [(i, i ^ (1 << bit)) for i in range(count)])


def dp_bits():
    return range(lax.axis_size("dp").bit_length() - 1)


def join(values):
    place = lax.axis_index("dp")
    for bit in dp_bits():
        upper = (place >> bit) & 1
        came = across(values, bit)
        values = jnp.where(
            upper == 1,
            jnp.concatenate((came, values), axis=0),
            jnp.concatenate((values, came), axis=0),
        )
    return values


def local(
    hidden_in,
    lengths,
    inst_lengths,
    w_query,
    w_key,
    w_value,
    attention_output_weight,
    feedforward_input_weight,
    feedforward_output_weight,
    rel_table,
    gain_attn,
    gain_ffn,
    grad_output,
    grad_pooled,
):
    rows, size, width = hidden_in.shape
    parts = lax.axis_size("tp")
    copies = lax.axis_size("dp")
    me = lax.axis_index("tp")
    group = lax.axis_index("dp")
    heads = rel_table.shape[1]
    inner = w_query.shape[1]
    tokens = rows * size
    place = me.astype(jnp.int32).reshape(1)
    gain_one = gain_attn.astype(F32).reshape(1, width)
    gain_two = gain_ffn.astype(F32).reshape(1, width)

    def share_of(weights):
        share = weights.shape[0] // copies
        return lax.dynamic_slice_in_dim(weights, group * share, share, 0)

    def fetched(shares, lead):
        everything = lax.all_gather(shares, "dp", axis=0, tiled=False)
        rest = everything[:, lead:].reshape(copies, parts, -1, width)
        return (
            jnp.swapaxes(rest, 0, 1).reshape(parts, -1, width),
            everything[:, :lead].reshape(-1, width),
        )

    first = norm_one(hidden_in, gain_one)
    attention_weights = jnp.concatenate(
        (w_query.T, w_key.T, w_value.T), axis=0
    )
    bias = bias_blocks(rel_table.T.astype(F32), parts, size)

    other_share = share_of(
        jnp.concatenate((feedforward_input_weight, feedforward_output_weight), axis=0)
    )
    ffn_share = other_share.shape[0]
    out_part = share_of(attention_output_weight)
    came_two = swap(jnp.concatenate((other_share, out_part), axis=0), 2)
    came_out = [out_part, swap(out_part, 1), swap(out_part, 3)]
    columns = grad_pooled.shape[1]
    spread = lax.dynamic_update_slice(
        jnp.zeros((rows, width), BF16), grad_pooled, (0, me * columns)
    )
    spread = swap_all([spread] * parts)
    blocks, (bias, came_two, *came_out), spread = gather_line(
        first, [bias, came_two] + came_out, spread
    )
    pool_cot = sum(block.astype(F32) for block in spread)
    counts = (lengths - inst_lengths).astype(F32)
    spots = me * size + jnp.arange(size, dtype=jnp.int32)
    mask = (
        (spots[None, :] >= inst_lengths[:, None]) & (spots[None, :] < lengths[:, None])
    ).astype(F32)
    grad_result = (
        grad_output.astype(F32)
        + pool_cot[:, None, :] * (mask / counts[:, None])[:, :, None]
    )
    grad_low = grad_result.astype(BF16).reshape(tokens, width)
    grad_low_pair = swap(grad_low, 1)


    shares = jnp.concatenate(
        [came_two[:ffn_share], *came_out[:2], came_two[ffn_share:], came_out[2]], axis=0
    )
    out_gathered, other_weights = fetched(shares, ffn_share)
    gathered = lax.all_gather(
        after(share_of(attention_weights), blocks[5]), ("tp", "dp"), axis=0, tiled=True
    ).reshape(parts, -1, width)
    normed, joint, logs, *mixed = attend(
        place, lengths, blocks, (w_query.T, w_key.T, w_value.T), bias, heads
    )
    mixed, grad_low_pair = lax.optimization_barrier((mixed, grad_low_pair))
    mixed = swap_all(mixed)
    middle, second = middle_of(out_gathered, hidden_in, gain_two, mixed)
    second = second.reshape(tokens, width)
    second_pair = swap(second, 1)

    gelu, grad_act, branch, back = feed_forward(
        second,
        grad_low,
        feedforward_input_weight,
        feedforward_output_weight,
        other_weights,
        0,
        None,
        F32,
    )
    gelu, grad_act, branch_pair, back_pair = feed_forward(
        second_pair,
        grad_low_pair,
        feedforward_input_weight,
        feedforward_output_weight,
        other_weights,
        1,
        (gelu, grad_act),
        BF16,
    )
    stacked = ffn_grad(
        second, second_pair, grad_low, grad_low_pair, gelu, grad_act, copies
    )
    summed = lax.psum_scatter(
        stacked.reshape(-1, width), "dp", scatter_dimension=0, tiled=True
    )

    back_came = after(swap(back_pair, 1), stacked, gathered)

    grad_middle, grad_branch, gain_two_grad, *grad_mixed = middle_back(
        out_gathered,
        back.reshape(rows, size, width),
        back_came.reshape(rows, size, width),
        middle,
        grad_result,
        gain_two,
    )
    grad_mixed = swap_all(grad_mixed)

    *joint_grads, table_grad = attend_back(place, lengths, joint, bias, logs, grad_mixed)
    came = swap_all(joint_grads)

    branch_came = swap(after(branch_pair, grad_mixed[-1]), 1)
    result = (
        middle
        + branch.reshape(rows, size, width)
        + branch_came.reshape(rows, size, width).astype(F32)
    )
    wide = 3 * inner
    heads_grad = joint_grad(
        normed,
        attention_weights,
        gain_one,
        gain_two_grad,
        table_grad,
        grad_branch,
        joint_grads,
        mixed,
        copies,
    )
    if heads_grad.shape[0] != copies:
        heads_grad = recut(heads_grad, wide, parts, inner, copies)
    mine = lax.psum_scatter(
        heads_grad.reshape(-1, width), "dp", scatter_dimension=0, tiled=True
    )
    summed = after(summed, heads_grad)
    own_sum = summed[:ffn_share].astype(F32) + swap(summed[ffn_share:], 2).astype(F32)
    whole_ffn = lax.all_gather(own_sum.astype(BF16), "dp", axis=0, tiled=True).astype(F32)
    grad_hidden = hidden_grad(
        place,
        gathered,
        grad_middle,
        hidden_in,
        gain_one,
        [after(came[0], heads_grad, own_sum, branch_came)] + came[1:],
    )
    mine, result = after((mine, result), grad_hidden)

    layer_out = result.astype(BF16)
    pool_part = jnp.sum(result * mask[:, :, None], axis=1) / counts[:, None]
    pool_sum = pool_part + sum(swap(pool_part, a) for a in range(1, parts))
    pooled = lax.dynamic_slice_in_dim(pool_sum, me * columns, columns, 1)
    share, out_share = wide // copies, inner // copies
    extra = mine[share + parts * out_share :]
    moved = swap_all(
        [
            jnp.concatenate(
                (mine[share + a * out_share : share + (a + 1) * out_share], extra), axis=0
            )
            for a in range(parts)
        ]
    )
    moved = sum(block.astype(F32) for block in moved)
    whole = join(
        jnp.concatenate(
            (
                mine[:share].astype(F32),
                moved[:out_share],
                moved[out_share : out_share + 2],
                extra[2:].astype(F32),
            ),
            axis=0,
        )[None].astype(BF16)
    )
    joint_sum = whole[:, :share].reshape(wide, width).astype(F32)
    whole_out = whole[:, share : share + out_share].reshape(inner, width).astype(F32)
    extra = whole[0, share + out_share :].astype(F32)
    table_sum = extra[2 : 2 + heads, : rel_table.shape[0]].T

    return (
        layer_out,
        pooled,
        grad_hidden,
        joint_sum[:inner].T,
        joint_sum[inner : 2 * inner].T,
        joint_sum[2 * inner : wide].T,
        whole_out,
        whole_ffn[:width],
        whole_ffn[width:],
        table_sum,
        extra[0],
        extra[1],
    )


def solution(mesh):
    in_specs = (
        P("dp", "tp", None),
        P("dp"),
        P("dp"),
        P(None, "tp"),
        P(None, "tp"),
        P(None, "tp"),
        P("tp", None),
        P(None, "tp"),
        P("tp", None),
        P(None, "tp"),
        P(),
        P(),
        P("dp", "tp", None),
        P("dp", "tp"),
    )
    out_specs = (
        P("dp", "tp", None),
        P("dp", "tp"),
        P("dp", "tp", None),
        P(None, "tp"),
        P(None, "tp"),
        P(None, "tp"),
        P("tp", None),
        P(None, "tp"),
        P("tp", None),
        P(None, "tp"),
        P(),
        P(),
    )
    return jax.shard_map(local, mesh=mesh, in_specs=in_specs, out_specs=out_specs, check_vma=False)
```

time: 682 us -> 321 us (0.47)
  waiting for transfers between devices: 368 us -> 127 us
  matrix products: 101 us -> 0 us
  Pallas kernels: 0 us -> 84.5 us
  blocking collectives: 67.5 us -> 0 us
  starting transfers between devices: 1.26 us -> 61.4 us
  local copies, waits for them, and re-layouts: 73.5 us -> 25.4 us
  other arithmetic: 49.9 us -> 8.44 us
    reduce_scatter x4 -> x2, waiting for transfers between devices: 183 us -> 2.88 us  [the longest x1 2.86 us: local(): lax.psum_scatter(heads_grad.reshape(-1, width), 'dp', scatter_dimension=0...]
    ppermute x0 -> x34, waiting for transfers between devices: none -> 124 us  [the longest x27 92.1 us: swap(): return lax.ppermute(values, 'tp', [(i, i ^ distance) for i in range(parts)])]
    all_gather x4 -> x3, waiting for transfers between devices: 107 us -> 0.01 us  [the longest x1 0.01 us: fetched(): everything = lax.all_gather(shares, 'dp', axis=0, tiled=False)]
    dot_general x21 -> x0, matrix products: 101 us -> none  [the longest x1 12.6 us: local(): jnp.einsum('qkb,shqk->sbh', onehot, grad_scores, preferred_element_type=j...]
    pallas_call x0 -> x11, Pallas kernels: none -> 84.5 us  [the longest x2 18.1 us: feed_forward(): pl.pallas_call(functools.partial(ffn_kernel, len(aliases)), grid=(units /...]
    psum x1 -> x0, waiting for transfers between devices: 76.8 us -> none  [local(): lax.psum((grad_w_joint, grad_w_out, grad_w_in, grad_w_ffn_out, grad_table...]
    ppermute x0 -> x34, starting transfers between devices: none -> 60.8 us  [the longest x27 52.9 us: swap(): return lax.ppermute(values, 'tp', [(i, i ^ distance) for i in range(parts)])]
    psum x2 -> x0, blocking collectives: 55.4 us -> none  [the longest x1 39.8 us: local(): lax.psum((gain_attn_part, gain_ffn_part), ('dp', 'tp'))]
  transfers between devices with their start and end apart: 10 -> 39, of which waited for: 8 -> 20; matrix products, arithmetic and copies ran while one was open for 25% -> 7% of each run, Pallas kernels for 0% -> 26%
where the time goes in v1:
time: 321 us
  waiting for transfers between devices  127 us (40%)
  Pallas kernels  84.5 us (26%)
  starting transfers between devices  61.4 us (19%)
  local copies, waits for them, and re-layouts  25.4 us (8%)
  between operations  14.4 us (4%)
  other arithmetic  8.44 us (3%)
    ppermute x27, waiting for transfers between devices, swap(): return lax.ppermute(values, 'tp', [(i, i ^ distance) for i in range(parts)])  92.1 us
    ppermute x27, starting transfers between devices, swap(): return lax.ppermute(values, 'tp', [(i, i ^ distance) for i in range(parts)])  52.9 us
    ppermute x3, waiting for transfers between devices, across(): return lax.ppermute(values, 'dp', [(i, i ^ 1 << bit) for i in range(count)])  19.4 us
    pallas_call x2, Pallas kernels, feed_forward(): pl.pallas_call(functools.partial(ffn_kernel, len(aliases)), grid=(units /...  18.1 us
    pallas_call x1, Pallas kernels, attend_back(): pl.pallas_call(functools.partial(attend_back_kernel, heads, parts), grid=...  14.9 us
    pallas_call x1, Pallas kernels, attend(): pl.pallas_call(functools.partial(attend_kernel, heads), grid=(rows,), in_...  13.2 us
    ppermute x1, waiting for transfers between devices, gather_line(): last_high = lax.ppermute(far_low, 'tp', outer)  12.2 us
    pallas_call x1, Pallas kernels, ffn_grad(): pl.pallas_call(ffn_grad_kernel, grid=(steps,), in_specs=[pl.BlockSpec((to...  8.25 us
  transfers between devices with their start and end apart: 39, of which 20 were waited for; matrix products, arithmetic and copies ran while one was open for 7% of the time, Pallas kernels for 26%

profile of v1, /device:TPU:0, one launch (start us, length us, event | category | flops | bytes accessed | tf_op | source)
XLA Modules:
  0.0 320.7 jit_solution(3519309975232519727)
XLA Ops:
  8.2 3.0 collective-permute-start.3
  14.9 3.1 norm_one.1.own_ref
  20.5 3.3 %collective-permute-start.2 = (bf16[216,768]{1,0:T(8,128)(2,1)S(1)}, bf16[216,768]{1,0:T(8,128)(2,1)S(1)}, u32[]{:S(2)}, u32[]{:S(2)}) collective-permute-start(bf16[216,768]{1,0:T(8,128)(2,1)S(1)} %pad_maximum_fusion.1), channel_id=1, source_target_pairs={{0,2},{1,3},{2,0},{3,1},{4,6},{5,7},{6,4},{7,5},{8,10},{9,11},{10,... | collective-permute-start | bytes 995336 | tf_op jit(solution)/shard_map/ppermute | solution.py:658
  27.0 22.9 %collective-permute-done.2 = bf16[216,768]{1,0:T(8,128)(2,1)S(1)} collective-permute-done((bf16[216,768]{1,0:T(8,128)(2,1)S(1)}, bf16[216,768]{1,0:T(8,128)(2,1)S(1)}, u32[]{:S(2)}, u32[]{:S(2)}) %collective-permute-start.2) | collective-permute-done | bytes 331808 | tf_op jit(solution)/shard_map/ppermute | solution.py:658
  53.1 3.6 %collective-permute-start.7 = (bf16[3,768]{1,0:T(4,128)(2,1)S(1)}, bf16[3,768]{1,0:T(4,128)(2,1)S(1)}, u32[]{:S(2)}, u32[]{:S(2)}) collective-permute-start(bf16[3,768]{1,0:T(4,128)(2,1)S(1)} %dynamic_update_slice.3), channel_id=1, source_target_pairs={{0,1},{1,0},{2,3},{3,2},{4,5},{5,4},{6,7},{7,6},{8,9},{9,8},{10,11... | collective-permute-start | bytes 13832 | tf_op jit(solution)/shard_map/ppermute | solution.py:658
  59.1 8.3 %collective-permute-done.7 = bf16[3,768]{1,0:T(4,128)(2,1)S(1)} collective-permute-done((bf16[3,768]{1,0:T(4,128)(2,1)S(1)}, bf16[3,768]{1,0:T(4,128)(2,1)S(1)}, u32[]{:S(2)}, u32[]{:S(2)}) %collective-permute-start.7) | collective-permute-done | bytes 4640 | tf_op jit(solution)/shard_map/ppermute | solution.py:658
  69.7 12.2 %collective-permute-done.10.last_high_ref = bf16[3,128,768]{2,1,0:T(8,128)(2,1)} collective-permute-done((bf16[3,128,768]{2,1,0:T(8,128)(2,1)S(1)}, bf16[3,128,768]{2,1,0:T(8,128)(2,1)}, u32[]{:S(2)}, u32[]{:S(2)}) %collective-permute-start.10) | collective-permute-done | bytes 589856 | tf_op jit(solution)/shard_map/ppermute | solution.py:674
  84.7 13.2 %attend.1 = (bf16[3,512,768]{2,1,0:T(8,128)(2,1)}, bf16[3,576,512]{2,1,0:T(8,128)(2,1)}, f32[3,3,512]{2,1,0:T(4,128)}, bf16[3,192,128]{2,1,0:T(8,128)(2,1)}, bf1...) custom-call(s32[1]{0:T(128)} %bitcast.place_ref, s32[3]{0:T(128)} %length_ref.3, ...), custom_call_target="tpu_custom_call" | custom-call | flops 14300000256 | bytes 13000000 | tf_op jit(solution)/shard_map/attend/pallas_call | solution.py:205
  104.3 3.2 %slice.105 = bf16[8,192,768]{2,1,0:T(8,128)(2,1)} slice(bf16[8,288,768]{2,1,0:T(8,128)(2,1)} %bitcast.47), slice={[0:8], [0:192], [0:768]} | slice | bytes 4718592 | tf_op jit(solution)/shard_map/slice | solution.py:737
  108.6 3.2 collective-permute-done.13.refs_2_.refs_6_
  112.5 4.4 %middle_of.1 = (f32[3,128,768]{2,1,0:T(8,128)}, bf16[3,128,768]{2,1,0:T(8,128)(2,1)}) custom-call(bf16[4,192,768]{2,1,0:T(8,128)(2,1)} %bitcast.53, bf16[3,128,768]{2,1,0:T(8,128)(2,1)} %hidden_ref.3, f32[1,768]{1,0:T(1,128)} %reshape.278.gain_ref, bf16[3,192,128]{2,1,0:T(8,128)(2,1)} %get-tuple-element.84.refs_0_.refs_4_, bf16[3,192,128]{2,1,0:T(8,128)(2,1)} %copy-done.34, ...), custom_call_target="tpu_custom_call" | custom-call | flops 4400000000 | bytes 4000000 | tf_op jit(solution)/shard_map/middle_of/pallas_call | solution.py:239
  116.9 3.0 collective-permute-start.15
  119.9 9.3 %feed_forward.2 = (bf16[2,768,768]{2,1,0:T(8,128)(2,1)}, bf16[2,768,768]{2,1,0:T(8,128)(2,1)}, f32[384,768]{1,0:T(8,128)}, f32[384,768]{1,0:T(8,128)}) custom-call(bf16[384,768]{1,0:T(8,128)(2,1)} %bitcast.68, bf16[384,768]{1,0:T(8,128)(2,1)} %bitcast.58, bf16[768,768]{1,0:T(8,128)(2,1)} %refs_2_.3, bf16[1536,768]{1,0:T(8,128)(2,1)} %bitcast.48, ...), custom_call_target="tpu_custom_call" | custom-call | flops 9900000256 | bytes 9000000 | tf_op jit(solution)/shard_map/feed_forward/pallas_call | solution.py:317
  129.2 7.7 %collective-permute-done.15.refs_0_.normed_pair_ref = bf16[384,768]{1,0:T(8,128)(2,1)S(1)} collective-permute-done((bf16[384,768]{1,0:T(8,128)(2,1)}, bf16[384,768]{1,0:T(8,128)(2,1)S(1)}, u32[]{:S(2)}, u32[]{:S(2)}) %collective-permute-start.15) | collective-permute-done | bytes 589856 | tf_op jit(solution)/shard_map/ppermute | solution.py:658
  137.7 8.8 %feed_forward.3 = (bf16[2,768,768]{2,1,0:T(8,128)(2,1)}, bf16[2,768,768]{2,1,0:T(8,128)(2,1)}, bf16[384,768]{1,0:T(8,128)(2,1)}, bf16[384,768]{1,0:T(8,128)(2,1)}) custom-call(bf16[384,768]{1,0:T(8,128)(2,1)} %copy-done.30, bf16[384,768]{1,0:T(8,128)(2,1)} %copy-done.27, bf16[768,768]{1,0:T(8,128)(2,1)} %refs_2_.3, ...), custom_call_target="tpu_custom_call", output_to_operand_aliasing={{0}: (6, {}), {1}: (7, {})} | custom-call | flops 9900000256 | bytes 9000000 | tf_op jit(solution)/shard_map/feed_forward/pallas_call | solution.py:317
  146.6 8.2 %ffn_grad.1 = bf16[2,4,384,768]{3,2,1,0:T(8,128)(2,1)} custom-call(bf16[384,768]{1,0:T(8,128)(2,1)} %bitcast.69, bf16[384,768]{1,0:T(8,128)(2,1)} %copy-done.30, bf16[384,768]{1,0:T(8,128)(2,1)} %bitcast.59, bf16[384,768]{1,0:T(8,128)(2,1)} %copy-done.27, bf16[2,768,768]{2,1,0:T(8,128)(2,1)} %get-tuple-element.94.gelu_ref, ...), custom_call_target="tpu_custom_call" | custom-call | flops 6600000000 | bytes 6000000 | tf_op jit(solution)/shard_map/ffn_grad/pallas_call | solution.py:512
  158.4 10.9 %collective-permute-done.16 = bf16[384,768]{1,0:T(8,128)(2,1)S(1)} collective-permute-done((bf16[384,768]{1,0:T(8,128)(2,1)S(1)}, bf16[384,768]{1,0:T(8,128)(2,1)S(1)}, u32[]{:S(2)}, u32[]{:S(2)}) %collective-permute-start.16) | collective-permute-done | bytes 589856 | tf_op jit(solution)/shard_map/ppermute | solution.py:658
  170.1 5.5 %middle_back.1 = (f32[3,128,768]{2,1,0:T(8,128)}, bf16[3,128,768]{2,1,0:T(8,128)(2,1)}, f32[1,768]{1,0:T(1,128)}, bf16[3,192,128]{2,1,0:T(8,128)(2,1)}, bf16[3,1...) custom-call(bf16[4,192,768]{2,1,0:T(8,128)(2,1)} %bitcast.54, ...), custom_call_target="tpu_custom_call" | custom-call | flops 5500000256 | bytes 5000000 | tf_op jit(solution)/shard_map/middle_back/pallas_call | solution.py:371
  180.1 4.3 %collective-permute-done.19.refs_3_ = bf16[3,192,128]{2,1,0:T(8,128)(2,1)S(1)} collective-permute-done((bf16[3,192,128]{2,1,0:T(8,128)(2,1)}, bf16[3,192,128]{2,1,0:T(8,128)(2,1)S(1)}, u32[]{:S(2)}, u32[]{:S(2)}) %collective-permute-start.19) | collective-permute-done | bytes 147488 | tf_op jit(solution)/shard_map/ppermute | solution.py:658
  184.3 3.1 collective-permute-start.20
  190.2 14.9 %attend_back.1 = (bf16[3,576,128]{2,1,0:T(8,128)(2,1)}, bf16[3,576,128]{2,1,0:T(8,128)(2,1)}, bf16[3,576,128]{2,1,0:T(8,128)(2,1)}, bf16[3,576,128]{2,1,0:T(8,128)(2,1)}, f32[3,8,128]{2,1,0:T(8,128)}) custom-call(s32[1]{0:T(128)} %bitcast.place_ref, s32[3]{0:T(128)} %length_ref.3, bf16[3,576,512]{2,1,0:T(8,128)(2,1)} %get-tuple-element.100.joint_ref, ...), custom_call_target="tpu_custom_call" | custom-call | flops 16499999744 | bytes 15000000 | tf_op jit(solution)/shard_map/attend_back/pallas_call | solution.py:472
  209.7 7.7 %joint_grad.1 = bf16[8,176,768]{2,1,0:T(8,128)(2,1)} custom-call(bf16[3,512,768]{2,1,0:T(8,128)(2,1)} %get-tuple-element.71.normed_ref, bf16[576,768]{1,0:T(8,128)(2,1)} %copy-done.5, f32[1,768]{1,0:T(1,128)} %reshape.276.gain_ref, f32[1,768]{1,0:T(1,128)} %get-tuple-element.99.gain_two_ref, f32[3,8,128]{2,1,0:T(8,128)} %get-tuple-element.106.table_ref, ...), custom_call_target="tpu_custom_call" | custom-call | flops 6600000000 | bytes 6000000 | tf_op jit(solution)/shard_map/joint_grad/pallas_call | solution.py:592
  217.6 5.9 %collective-permute-done.22.refs_1_ = bf16[3,576,128]{2,1,0:T(8,128)(2,1)S(1)} collective-permute-done((bf16[3,576,128]{2,1,0:T(8,128)(2,1)}, bf16[3,576,128]{2,1,0:T(8,128)(2,1)S(1)}, u32[]{:S(2)}, u32[]{:S(2)}) %collective-permute-start.22) | collective-permute-done | bytes 442400 | tf_op jit(solution)/shard_map/ppermute | solution.py:658
  223.5 16.0 %collective-permute-done.23.refs_2_ = bf16[3,576,128]{2,1,0:T(8,128)(2,1)S(1)} collective-permute-done((bf16[3,576,128]{2,1,0:T(8,128)(2,1)}, bf16[3,576,128]{2,1,0:T(8,128)(2,1)S(1)}, u32[]{:S(2)}, u32[]{:S(2)}) %collective-permute-start.23) | collective-permute-done | bytes 442400 | tf_op jit(solution)/shard_map/ppermute | solution.py:658
  240.4 6.7 %hidden_grad.1 = f32[3,128,768]{2,1,0:T(8,128)} custom-call(s32[1]{0:T(128)} %bitcast.place_ref, bf16[4,576,768]{2,1,0:T(8,128)(2,1)} %bitcast.66, f32[3,128,768]{2,1,0:T(8,128)} %get-tuple-element.115.middle_ref, bf16[3,128,768]{2,1,0:T(8,128)(2,1)} %hidden_ref.3, f32[1,768]{1,0:T(1,128)} %reshape.276.gain_ref, ...), custom_call_target="tpu_custom_call" | custom-call | flops 165000003584 | bytes 150000000 | tf_op jit(solution)/shard_map/hidden_grad/pallas_call | solution.py:640
  248.1 6.4 %collective-permute-start.21 = (bf16[192,768]{1,0:T(8,128)(2,1)S(1)}, bf16[192,768]{1,0:T(8,128)(2,1)S(1)}, u32[]{:S(2)}, u32[]{:S(2)}) collective-permute-start(bf16[192,768]{1,0:T(8,128)(2,1)S(1)} %slice.85), channel_id=1, source_target_pairs={{0,2},{1,3},{2,0},{3,1},{4,6},{5,7},{6,4},{7,5},{8,10},{9,11},{10,... | collective-permute-start | bytes 884744 | tf_op jit(solution)/shard_map/ppermute | solution.py:658
  261.0 3.0 collective-permute-done.21
  266.4 3.0 collective-permute-start.30
  275.2 8.5 %collective-permute-done.32 = bf16[2,104,768]{2,1,0:T(8,128)(2,1)S(1)} collective-permute-done((bf16[2,104,768]{2,1,0:T(8,128)(2,1)S(1)}, bf16[2,104,768]{2,1,0:T(8,128)(2,1)S(1)}, u32[]{:S(2)}, u32[]{:S(2)}) %collective-permute-start.32) | collective-permute-done | bytes 319520 | tf_op jit(solution)/shard_map/ppermute | solution.py:680
  292.7 3.3 %collective-permute-done.27 = f32[3,768]{1,0:T(4,128)S(1)} collective-permute-done((f32[3,768]{1,0:T(4,128)S(1)}, f32[3,768]{1,0:T(4,128)S(1)}, u32[]{:S(2)}, u32[]{:S(2)}) %collective-permute-start.27) | collective-permute-done | bytes 9248 | tf_op jit(solution)/shard_map/ppermute | solution.py:658
  296.6 9.5 %collective-permute-done.33 = bf16[4,104,768]{2,1,0:T(8,128)(2,1)S(1)} collective-permute-done((bf16[4,104,768]{2,1,0:T(8,128)(2,1)S(1)}, bf16[4,104,768]{2,1,0:T(8,128)(2,1)S(1)}, u32[]{:S(2)}, u32[]{:S(2)}) %collective-permute-start.33) | collective-permute-done | bytes 639008 | tf_op jit(solution)/shard_map/ppermute | solution.py:680
  309.9 4.2 %fusion.5 = (f32[768,768]{1,0:T(8,128)}, f32[768,768]{1,0:T(8,128)}) fusion(bf16[1536,768]{1,0:T(8,128)(2,1)} %all-gather.7.cloned.1.call-done), kind=kLoop, calls=%fused_computation.49 | loop fusion | bytes 9437184 | tf_op jit(solution)/shard_map/slice | solution.py:909
  (192 shorter events, 75.8 us)
Async XLA Ops:
  7.2 95.8 %all-gather.9.cloned.1.call-start = ((), (), s32[]{:S(2)}) async-start(), calls=%async_computation.6 | async-start | bytes 3981312 | tf_op jit(solution)/shard_map/all_gather | solution.py:733
  8.2 18.9 %collective-permute-start.3 = (bf16[24,768]{1,0:T(8,128)(2,1)S(1)}, bf16[24,768]{1,0:T(8,128)(2,1)S(1)}, u32[]{:S(2)}, u32[]{:S(2)}) collective-permute-start(bf16[24,768]{1,0:T(8,128)(2,1)S(1)} %constant_dynamic-slice_fusion.1), channel_id=1, source_target_pairs={{0,1},{1,0},{2,3},{3,2},{4,5},{5,4},{6,7},{7,6},{8,9},{9,8},{10,11... | collective-permute-start | bytes 110600 | tf_op jit(solution)/shard_map/ppermute | solution.py:658
  11.2 15.9 %collective-permute-start.4 = (bf16[24,768]{1,0:T(8,128)(2,1)S(1)}, bf16[24,768]{1,0:T(8,128)(2,1)S(1)}, u32[]{:S(2)}, u32[]{:S(2)}) collective-permute-start(bf16[24,768]{1,0:T(8,128)(2,1)S(1)} %constant_dynamic-slice_fusion.1), channel_id=1, source_target_pairs={{0,3},{1,2},{2,1},{3,0},{4,7},{5,6},{6,5},{7,4},{8,11},{9,10},{10,... | collective-permute-start | bytes 110600 | tf_op jit(solution)/shard_map/ppermute | solution.py:658
  18.0 32.0 %collective-permute-start = (bf16[3,128,768]{2,1,0:T(8,128)(2,1)}, bf16[3,128,768]{2,1,0:T(8,128)(2,1)}, u32[]{:S(2)}, u32[]{:S(2)}) collective-permute-start(bf16[3,128,768]{2,1,0:T(8,128)(2,1)} %norm_one.1.own_ref), channel_id=1, source_target_pairs={{0,1},{1,0},{2,3},{3,2},{4,5},{5,4},{6,7},{7,6},{8,9},{9,8},{10,11... | collective-permute-start | bytes 1769480 | tf_op jit(solution)/shard_map/ppermute | solution.py:658
  18.7 31.3 %collective-permute-start.1 = (bf16[3,128,768]{2,1,0:T(8,128)(2,1)}, bf16[3,128,768]{2,1,0:T(8,128)(2,1)}, u32[]{:S(2)}, u32[]{:S(2)}) collective-permute-start(bf16[3,128,768]{2,1,0:T(8,128)(2,1)} %norm_one.1.own_ref), channel_id=1, source_target_pairs={{1,2},{2,1},{5,6},{6,5},{9,10},{10,9},{13,14},{14,13},{17,18},{18,... | collective-permute-start | bytes 1769480 | tf_op jit(solution)/shard_map/ppermute | solution.py:669
  20.5 29.5 %collective-permute-start.2 = (bf16[216,768]{1,0:T(8,128)(2,1)S(1)}, bf16[216,768]{1,0:T(8,128)(2,1)S(1)}, u32[]{:S(2)}, u32[]{:S(2)}) collective-permute-start(bf16[216,768]{1,0:T(8,128)(2,1)S(1)} %pad_maximum_fusion.1), channel_id=1, source_target_pairs={{0,2},{1,3},{2,0},{3,1},{4,6},{5,7},{6,4},{7,5},{8,10},{9,11},{10,... | collective-permute-start | bytes 995336 | tf_op jit(solution)/shard_map/ppermute | solution.py:658
  50.9 118.4 %all-gather.5.cloned.1.call-start = ((), (), s32[]{:S(2)}) async-start(), calls=%async_computation.2 | async-start | bytes 3649536 | tf_op jit(solution)/shard_map/all_gather | solution.py:779
  50.9 16.6 %collective-permute-start.5 = (bf16[3,128,768]{2,1,0:T(8,128)(2,1)}, bf16[3,128,768]{2,1,0:T(8,128)(2,1)S(1)}, u32[]{:S(2)}, u32[]{:S(2)}) collective-permute-start(bf16[3,128,768]{2,1,0:T(8,128)(2,1)} %collective-permute-done.pair_ref), channel_id=1, source_target_pairs={{1,2},{2,1},{5,6},{6,5},{9,10},{10,9},{13,14},{14,13},{17,18},{18,... | collective-permute-start | bytes 1769480 | tf_op jit(solution)/shard_map/ppermute | solution.py:671
  51.6 15.9 %collective-permute-start.6 = (bf16[3,128,768]{2,1,0:T(8,128)(2,1)}, bf16[3,128,768]{2,1,0:T(8,128)(2,1)}, u32[]{:S(2)}, u32[]{:S(2)}) collective-permute-start(bf16[3,128,768]{2,1,0:T(8,128)(2,1)} %collective-permute-done.1.last_low_ref), channel_id=1, source_target_pairs={{1,0},{2,3},{5,4},{6,7},{9,8},{10,11},{13,12},{14,15},{17,16},{18,... | collective-permute-start | bytes 1769480 | tf_op jit(solution)/shard_map/ppermute | solution.py:672
  53.1 14.3 %collective-permute-start.7 = (bf16[3,768]{1,0:T(4,128)(2,1)S(1)}, bf16[3,768]{1,0:T(4,128)(2,1)S(1)}, u32[]{:S(2)}, u32[]{:S(2)}) collective-permute-start(bf16[3,768]{1,0:T(4,128)(2,1)S(1)} %dynamic_update_slice.3), channel_id=1, source_target_pairs={{0,1},{1,0},{2,3},{3,2},{4,5},{5,4},{6,7},{7,6},{8,9},{9,8},{10,11... | collective-permute-start | bytes 13832 | tf_op jit(solution)/shard_map/ppermute | solution.py:658
  56.7 10.8 %collective-permute-start.8 = (bf16[3,768]{1,0:T(4,128)(2,1)S(1)}, bf16[3,768]{1,0:T(4,128)(2,1)S(1)}, u32[]{:S(2)}, u32[]{:S(2)}) collective-permute-start(bf16[3,768]{1,0:T(4,128)(2,1)S(1)} %dynamic_update_slice.3), channel_id=1, source_target_pairs={{0,2},{1,3},{2,0},{3,1},{4,6},{5,7},{6,4},{7,5},{8,10},{9,11},{10,... | collective-permute-start | bytes 13832 | tf_op jit(solution)/shard_map/ppermute | solution.py:658
  56.7 10.8 %collective-permute-start.9 = (bf16[3,768]{1,0:T(4,128)(2,1)S(1)}, bf16[3,768]{1,0:T(4,128)(2,1)S(1)}, u32[]{:S(2)}, u32[]{:S(2)}) collective-permute-start(bf16[3,768]{1,0:T(4,128)(2,1)S(1)} %dynamic_update_slice.3), channel_id=1, source_target_pairs={{0,3},{1,2},{2,1},{3,0},{4,7},{5,6},{6,5},{7,4},{8,11},{9,10},{10,... | collective-permute-start | bytes 13832 | tf_op jit(solution)/shard_map/ppermute | solution.py:658
  67.5 14.4 %collective-permute-start.10 = (bf16[3,128,768]{2,1,0:T(8,128)(2,1)S(1)}, bf16[3,128,768]{2,1,0:T(8,128)(2,1)}, u32[]{:S(2)}, u32[]{:S(2)}) collective-permute-start(bf16[3,128,768]{2,1,0:T(8,128)(2,1)S(1)} %collective-permute-done.5.far_low_ref), channel_id=1, source_target_pairs={{1,0},{2,3},{5,4},{6,7},{9,8},{10,11},{13,12},{14,15},{17,16},{18,... | collective-permute-start | bytes 1769480 | tf_op jit(solution)/shard_map/ppermute | solution.py:674
  81.9 165.2 %reduce-scatter.5.cloned.1.call-start = ((), (), s32[]{:S(2)}) async-start(), calls=%async_computation.4 | async-start | bytes 5308416 | tf_op jit(solution)/shard_map/reduce_scatter | solution.py:814
  84.7 13.2 %collective-permute-start.11 = (bf16[384,768]{1,0:T(8,128)(2,1)S(1)}, bf16[384,768]{1,0:T(8,128)(2,1)S(1)}, u32[]{:S(2)}, u32[]{:S(2)}) collective-permute-start(bf16[384,768]{1,0:T(8,128)(2,1)S(1)} %bitcast.57), channel_id=1, source_target_pairs={{0,1},{1,0},{2,3},{3,2},{4,5},{5,4},{6,7},{7,6},{8,9},{9,8},{10,11... | collective-permute-start | bytes 1769480 | tf_op jit(solution)/shard_map/ppermute | solution.py:658
  97.9 10.7 %collective-permute-start.12 = (bf16[3,192,128]{2,1,0:T(8,128)(2,1)}, bf16[3,192,128]{2,1,0:T(8,128)(2,1)S(1)}, u32[]{:S(2)}, u32[]{:S(2)}) collective-permute-start(bf16[3,192,128]{2,1,0:T(8,128)(2,1)} %get-tuple-element.85), channel_id=1, source_target_pairs={{0,1},{1,0},{2,3},{3,2},{4,5},{5,4},{6,7},{7,6},{8,9},{9,8},{10,11... | collective-permute-start | bytes 442376 | tf_op jit(solution)/shard_map/ppermute | solution.py:658
  99.8 12.0 %collective-permute-start.13 = (bf16[3,192,128]{2,1,0:T(8,128)(2,1)}, bf16[3,192,128]{2,1,0:T(8,128)(2,1)S(1)}, u32[]{:S(2)}, u32[]{:S(2)}) collective-permute-start(bf16[3,192,128]{2,1,0:T(8,128)(2,1)} %get-tuple-element.86), channel_id=1, source_target_pairs={{0,2},{1,3},{2,0},{3,1},{4,6},{5,7},{6,4},{7,5},{8,10},{9,11},{10,... | collective-permute-start | bytes 442376 | tf_op jit(solution)/shard_map/ppermute | solution.py:658
  99.9 11.9 %collective-permute-start.14 = (bf16[3,192,128]{2,1,0:T(8,128)(2,1)}, bf16[3,192,128]{2,1,0:T(8,128)(2,1)S(1)}, u32[]{:S(2)}, u32[]{:S(2)}) collective-permute-start(bf16[3,192,128]{2,1,0:T(8,128)(2,1)} %get-tuple-element.87), channel_id=1, source_target_pairs={{0,3},{1,2},{2,1},{3,0},{4,7},{5,6},{6,5},{7,4},{8,11},{9,10},{10,... | collective-permute-start | bytes 442376 | tf_op jit(solution)/shard_map/ppermute | solution.py:658
  116.9 20.0 %collective-permute-start.15 = (bf16[384,768]{1,0:T(8,128)(2,1)}, bf16[384,768]{1,0:T(8,128)(2,1)S(1)}, u32[]{:S(2)}, u32[]{:S(2)}) collective-permute-start(bf16[384,768]{1,0:T(8,128)(2,1)} %bitcast.67), channel_id=1, source_target_pairs={{0,1},{1,0},{2,3},{3,2},{4,5},{5,4},{6,7},{7,6},{8,9},{9,8},{10,11... | collective-permute-start | bytes 1769480 | tf_op jit(solution)/shard_map/ppermute | solution.py:658
  154.9 104.6 %reduce-scatter.3.cloned.1.call-start = ((), (), s32[]{:S(2)}) async-start(), calls=%async_computation.3 | async-start | bytes 2433024 | tf_op jit(solution)/shard_map/reduce_scatter | solution.py:853
  155.9 13.4 %collective-permute-start.16 = (bf16[384,768]{1,0:T(8,128)(2,1)S(1)}, bf16[384,768]{1,0:T(8,128)(2,1)S(1)}, u32[]{:S(2)}, u32[]{:S(2)}) collective-permute-start(bf16[384,768]{1,0:T(8,128)(2,1)S(1)} %copy-done.28), channel_id=1, source_target_pairs={{0,1},{1,0},{2,3},{3,2},{4,5},{5,4},{6,7},{7,6},{8,9},{9,8},{10,11... | collective-permute-start | bytes 1769480 | tf_op jit(solution)/shard_map/ppermute | solution.py:658
  175.6 8.7 %collective-permute-start.19 = (bf16[3,192,128]{2,1,0:T(8,128)(2,1)}, bf16[3,192,128]{2,1,0:T(8,128)(2,1)S(1)}, u32[]{:S(2)}, u32[]{:S(2)}) collective-permute-start(bf16[3,192,128]{2,1,0:T(8,128)(2,1)} %get-tuple-element.105), channel_id=1, source_target_pairs={{0,3},{1,2},{2,1},{3,0},{4,7},{5,6},{6,5},{7,4},{8,11},{9,10},{10,... | collective-permute-start | bytes 442376 | tf_op jit(solution)/shard_map/ppermute | solution.py:658
  178.4 10.3 %collective-permute-start.17 = (bf16[3,192,128]{2,1,0:T(8,128)(2,1)}, bf16[3,192,128]{2,1,0:T(8,128)(2,1)S(1)}, u32[]{:S(2)}, u32[]{:S(2)}) collective-permute-start(bf16[3,192,128]{2,1,0:T(8,128)(2,1)} %get-tuple-element.103), channel_id=1, source_target_pairs={{0,1},{1,0},{2,3},{3,2},{4,5},{5,4},{6,7},{7,6},{8,9},{9,8},{10,11... | collective-permute-start | bytes 442376 | tf_op jit(solution)/shard_map/ppermute | solution.py:658
  178.4 11.1 %collective-permute-start.18 = (bf16[3,192,128]{2,1,0:T(8,128)(2,1)}, bf16[3,192,128]{2,1,0:T(8,128)(2,1)S(1)}, u32[]{:S(2)}, u32[]{:S(2)}) collective-permute-start(bf16[3,192,128]{2,1,0:T(8,128)(2,1)} %get-tuple-element.104), channel_id=1, source_target_pairs={{0,2},{1,3},{2,0},{3,1},{4,6},{5,7},{6,4},{7,5},{8,10},{9,11},{10,... | collective-permute-start | bytes 442376 | tf_op jit(solution)/shard_map/ppermute | solution.py:658
  184.3 33.2 %collective-permute-start.20 = (bf16[384,768]{1,0:T(8,128)(2,1)S(1)}, bf16[384,768]{1,0:T(8,128)(2,1)S(1)}, u32[]{:S(2)}, u32[]{:S(2)}) collective-permute-start(bf16[384,768]{1,0:T(8,128)(2,1)S(1)} %copy-done.25), channel_id=1, source_target_pairs={{0,1},{1,0},{2,3},{3,2},{4,5},{5,4},{6,7},{7,6},{8,9},{9,8},{10,11... | collective-permute-start | bytes 1769480 | tf_op jit(solution)/shard_map/ppermute | solution.py:658
  205.1 18.4 %collective-permute-start.22 = (bf16[3,576,128]{2,1,0:T(8,128)(2,1)}, bf16[3,576,128]{2,1,0:T(8,128)(2,1)S(1)}, u32[]{:S(2)}, u32[]{:S(2)}) collective-permute-start(bf16[3,576,128]{2,1,0:T(8,128)(2,1)} %get-tuple-element.109.refs_1_), channel_id=1, source_target_pairs={{0,1},{1,0},{2,3},{3,2},{4,5},{5,4},{6,7},{7,6},{8,9},{9,8},{10,11... | collective-permute-start | bytes 1327112 | tf_op jit(solution)/shard_map/ppermute | solution.py:658
  206.8 32.7 %collective-permute-start.23 = (bf16[3,576,128]{2,1,0:T(8,128)(2,1)}, bf16[3,576,128]{2,1,0:T(8,128)(2,1)S(1)}, u32[]{:S(2)}, u32[]{:S(2)}) collective-permute-start(bf16[3,576,128]{2,1,0:T(8,128)(2,1)} %get-tuple-element.110.refs_2_), channel_id=1, source_target_pairs={{0,2},{1,3},{2,0},{3,1},{4,6},{5,7},{6,4},{7,5},{8,10},{9,11},{10,... | collective-permute-start | bytes 1327112 | tf_op jit(solution)/shard_map/ppermute | solution.py:658
  208.3 31.1 %collective-permute-start.24 = (bf16[3,576,128]{2,1,0:T(8,128)(2,1)}, bf16[3,576,128]{2,1,0:T(8,128)(2,1)S(1)}, u32[]{:S(2)}, u32[]{:S(2)}) collective-permute-start(bf16[3,576,128]{2,1,0:T(8,128)(2,1)} %get-tuple-element.111.refs_3_), channel_id=1, source_target_pairs={{0,3},{1,2},{2,1},{3,0},{4,7},{5,6},{6,5},{7,4},{8,11},{9,10},{10,... | collective-permute-start | bytes 1327112 | tf_op jit(solution)/shard_map/ppermute | solution.py:658
  217.5 92.4 %all-gather.7.cloned.1.call-start = ((), (), s32[]{:S(2)}) async-start(), calls=%async_computation.5 | async-start | bytes 2654208 | tf_op jit(solution)/shard_map/all_gather | solution.py:858
  248.1 15.9 %collective-permute-start.21 = (bf16[192,768]{1,0:T(8,128)(2,1)S(1)}, bf16[192,768]{1,0:T(8,128)(2,1)S(1)}, u32[]{:S(2)}, u32[]{:S(2)}) collective-permute-start(bf16[192,768]{1,0:T(8,128)(2,1)S(1)} %slice.85), channel_id=1, source_target_pairs={{0,2},{1,3},{2,0},{3,1},{4,6},{5,7},{6,4},{7,5},{8,10},{9,11},{10,... | collective-permute-start | bytes 884744 | tf_op jit(solution)/shard_map/ppermute | solution.py:658
  273.8 9.9 %collective-permute-start.32 = (bf16[2,104,768]{2,1,0:T(8,128)(2,1)S(1)}, bf16[2,104,768]{2,1,0:T(8,128)(2,1)S(1)}, u32[]{:S(2)}, u32[]{:S(2)}) collective-permute-start(bf16[2,104,768]{2,1,0:T(8,128)(2,1)S(1)} %maximum_select_fusion.2), channel_id=1, source_target_pairs={{0,8},{4,12},{8,0},{12,4},{16,24},{20,28},{24,16},{28,20},{1,9},{5... | collective-permute-start | bytes 958472 | tf_op jit(solution)/shard_map/ppermute | solution.py:680
  283.8 22.2 %collective-permute-start.33 = (bf16[4,104,768]{2,1,0:T(8,128)(2,1)S(1)}, bf16[4,104,768]{2,1,0:T(8,128)(2,1)S(1)}, u32[]{:S(2)}, u32[]{:S(2)}) collective-permute-start(bf16[4,104,768]{2,1,0:T(8,128)(2,1)S(1)} %maximum_select_fusion.1), channel_id=1, source_target_pairs={{0,16},{4,20},{8,24},{12,28},{16,0},{20,4},{24,8},{28,12},{1,17},{... | collective-permute-start | bytes 1916936 | tf_op jit(solution)/shard_map/ppermute | solution.py:680
  (47 other events, 525.2 us)
Sparse Core Ops, SparseCore 0:
  51.0 32.9 all-gather.8
  86.9 65.0 all-gather.4
  155.4 52.8 reduce-scatter.4
  217.6 41.7 reduce-scatter.2
  265.0 35.8 all-gather.6

commit v2 on v1

v2 whole, which is shorter than its diff:
```python
import functools

import jax
import jax.numpy as jnp
from jax import lax
from jax.experimental import pallas as pl
from jax.experimental.pallas import tpu as pltpu
from jax.sharding import PartitionSpec as P

F32 = jnp.float32
BF16 = jnp.bfloat16
EPS = 1e-06
ROOM = 16 << 20
NEG = -1000000000.0
THRESHOLDS = (12, 16, 23, 32, 46, 64, 91)
GELU_C = 0.7978845608028654
GELU_K = 0.044715
WIDE = pl.BlockSpec(memory_space=pltpu.VMEM)
SCALARS = pl.BlockSpec(memory_space=pltpu.SMEM)


def dot(left, right, left_dim, right_dim, precision=None):
    return lax.dot_general(
        left,
        right,
        (((left_dim,), (right_dim,)), ((), ())),
        preferred_element_type=F32,
        precision=precision,
    )


def code_of(delta):
    n = abs(delta)
    far = 8 + sum(1 for threshold in THRESHOLDS if n >= threshold)
    return (16 if delta > 0 else 0) + (n if n < 8 else far)


def code_block(size, distance):
    shape = (size, size)
    delta = (
        lax.broadcasted_iota(jnp.int32, shape, 0)
        - lax.broadcasted_iota(jnp.int32, shape, 1)
        + size * distance
    )
    n = jnp.abs(delta)
    far = jnp.full(shape, 8, jnp.int32)
    for threshold in THRESHOLDS:
        far = far + (n >= threshold).astype(jnp.int32)
    return jnp.where(delta > 0, 16, 0) + jnp.where(n < 8, n, far)


def codes_in(size, distance):
    return sorted(
        {code_of(size * distance + inner) for inner in range(1 - size, size)}
    )


def cost(micros):
    return pl.CostEstimate(
        flops=int(micros * 1.1e9), bytes_accessed=int(micros * 1e6), transcendentals=0
    )


def shaped(shape, dtype):
    return jax.ShapeDtypeStruct(shape, dtype)


def near(values):
    return pltpu.with_memory_space_constraint(values, pltpu.VMEM)


def call(kernel, name, micros, rows, scalars, arrays, outs, scratch=()):
    def spec(shape, mark):
        if mark == "h":
            return pl.BlockSpec((1, *shape[1:]), lambda row: (row,) + (0,) * (len(shape) - 1))
        if mark == "w":
            return pl.BlockSpec(shape, lambda row: (0,) * len(shape))
        return WIDE

    marked = [(array if isinstance(array, tuple) else (array, "v")) for array in arrays]
    return pl.pallas_call(
        kernel,
        grid=(rows,),
        in_specs=[SCALARS] * len(scalars) + [spec(array.shape, mark) for array, mark in marked],
        out_specs=[spec(shape, mark) for shape, _, mark in outs],
        out_shape=[
            (pltpu.VMEM if mark == "v" else pltpu.HBM)(shape, dtype) for shape, dtype, mark in outs
        ],
        scratch_shapes=list(scratch),
        compiler_params=pltpu.CompilerParams(vmem_limit_bytes=ROOM),
        cost_estimate=cost(micros),
        name=name,
    )(
        *scalars,
        *[near(array) if mark == "v" else array for array, mark in marked],
    )


def turn():
    row = pl.program_id(0)
    return row, lambda ref: 0 if ref.shape[0] == 1 else row


def norm_kernel(x_ref, gain_ref, out_ref):
    gain = gain_ref[...]
    for row in range(x_ref.shape[0]):
        x = x_ref[row].astype(F32)
        scale = lax.rsqrt(jnp.mean(x * x, axis=-1, keepdims=True) + EPS)
        out_ref[row] = (x * scale * gain).astype(BF16)


def norm_one(hidden, gain):
    return call(norm_kernel, "norm_one", 2, 1, [], [hidden, gain], [(hidden.shape, BF16, "v")])[0]


def bias_kernel(parts, size, table_ref, out_ref):
    heads = out_ref.shape[0]
    for at in range(2 * parts - 1):
        distance = at - (parts - 1)
        present = codes_in(size, distance)
        codes = code_block(size, distance) if len(present) > 1 else None
        for head in range(heads):
            block = jnp.full((size, size), table_ref[head, present[0]], F32)
            for code in present[1:]:
                block = jnp.where(codes == code, table_ref[head, code], block)
            out_ref[head, at] = block


def bias_blocks(table, parts, size):
    heads = table.shape[0]
    return call(
        functools.partial(bias_kernel, parts, size),
        "bias_blocks",
        3,
        1,
        [table],
        [],
        [((heads, 2 * parts - 1, size, size), F32, "w")],
    )[0]


def chunk_bias(bias_ref, head, me, parts, first, count):
    return jnp.concatenate(
        [
            jnp.concatenate(
                [
                    bias_ref[head, (a_k ^ me) - (a_q ^ me) + parts - 1]
                    for a_q in range(first, first + count)
                ],
                axis=1,
            )
            for a_k in range(parts)
        ],
        axis=0,
    )


def chunk_valid(length, me, parts, size, count):
    inner = lax.broadcasted_iota(jnp.int32, (size, count * size), 0)
    return jnp.concatenate(
        [inner < length - (a_k ^ me) * size for a_k in range(parts)], axis=0
    )


def attend_kernel(
    heads,
    place_ref,
    length_ref,
    own_ref,
    pair_ref,
    far_low_ref,
    far_high_ref,
    last_low_ref,
    last_high_ref,
    query_ref,
    key_ref,
    value_ref,
    bias_ref,
    normed_ref,
    joint_ref,
    log_ref,
    *mixed_refs,
):
    parts = len(mixed_refs)
    size = own_ref.shape[1]
    me = place_ref[0]
    inner = joint_ref.shape[1] // 3
    head_size = inner // heads
    count = 2

    row, at = turn()
    out = at(normed_ref)
    normed_ref[out, 0:size] = own_ref[row]
    normed_ref[out, size : 2 * size] = pair_ref[row]
    normed_ref[out, 2 * size : 3 * size] = far_low_ref[row] + far_high_ref[row]
    normed_ref[out, 3 * size : 4 * size] = last_low_ref[row] + last_high_ref[row]
    for part, ref in enumerate((query_ref, key_ref, value_ref)):
        joint_ref[out, part * inner : (part + 1) * inner] = dot(
            ref[...], normed_ref[out], 1, 1
        ).astype(BF16)
    valid = chunk_valid(length_ref[row], me, parts, size, count)
    for head in range(heads):
        low = head * head_size
        key = joint_ref[out, inner + low : inner + low + head_size, :]
        value = joint_ref[out, 2 * inner + low : 2 * inner + low + head_size, :]
        for first in range(0, parts, count):
            lanes = slice(first * size, (first + count) * size)
            query = joint_ref[out, low : low + head_size, lanes]
            scores = dot(key, query, 0, 0) + chunk_bias(bias_ref, head, me, parts, first, count)
            scores = jnp.where(valid, scores, NEG)
            peak = jnp.max(scores, axis=0, keepdims=True)
            raised = jnp.exp(scores - peak)
            total = jnp.sum(raised, axis=0, keepdims=True)
            mixed = (dot(value, raised.astype(BF16), 1, 0) / total).astype(BF16)
            for step in range(count):
                mixed_refs[first + step][row, low : low + head_size, :] = mixed[
                    :, step * size : (step + 1) * size
                ]
            log_ref[out, head : head + 1, lanes] = peak + jnp.log(total)


def attend(place, lengths, blocks, weights, bias, heads):
    rows, size, width = blocks[0].shape
    parts = (bias.shape[1] + 1) // 2
    full = parts * size
    inner = weights[0].shape[0]
    return call(
        functools.partial(attend_kernel, heads),
        "attend",
        12,
        rows,
        [place, lengths],
        [*blocks, *weights, bias],
        [
            ((rows, full, width), BF16, "h"),
            ((rows, 3 * inner, full), BF16, "h"),
            ((rows, heads, full), F32, "h"),
        ]
        + [((rows, inner, size), BF16, "v")] * parts,
    )


def middle_kernel(weight_ref, hidden_ref, gain_ref, *refs):
    mixed_refs, (middle_ref, normed_ref, all_ref) = refs[:-3], refs[-3:]
    row, at = turn()
    mixed = jnp.concatenate([ref[row] for ref in mixed_refs], axis=0)
    all_ref[at(all_ref)] = mixed
    middle = hidden_ref[at(hidden_ref)].astype(F32) + dot(mixed, weight_ref[...], 0, 0)
    scale = lax.rsqrt(jnp.mean(middle * middle, axis=-1, keepdims=True) + EPS)
    middle_ref[at(middle_ref)] = middle
    normed_ref[row] = (middle * scale * gain_ref[...]).astype(BF16)


def middle_of(gathered, hidden, gain, mixed):
    rows, size, width = hidden.shape
    return call(
        middle_kernel,
        "middle_of",
        3,
        rows,
        [],
        [gathered, (hidden, "h"), gain, *mixed],
        [
            (hidden.shape, F32, "h"),
            (hidden.shape, BF16, "v"),
            ((rows, gathered.shape[0], size), BF16, "h"),
        ],
    )


def ffn_kernel(
    normed_ref,
    grad_ref,
    in_one_ref,
    in_two_ref,
    out_one_ref,
    out_two_ref,
    gelu_ref,
    act_ref,
    branch_ref,
    back_ref,
):
    shards = ((in_one_ref, out_one_ref), (in_two_ref, out_two_ref))
    for shard, (in_ref, out_ref) in enumerate(shards):
        v = dot(normed_ref[...], in_ref[...], 1, 0)
        grad_gelu = dot(grad_ref[...], out_ref[...], 1, 1).astype(BF16).astype(F32)
        square = v * v
        bent = jnp.tanh(GELU_C * (v + GELU_K * (square * v)))
        half = 0.5 * (1.0 + bent)
        slope = half + (0.5 * GELU_C) * v * (1.0 - bent * bent) * (
            1.0 + (3.0 * GELU_K) * square
        )
        gelu_ref[shard] = (v * half).astype(BF16)
        act_ref[shard] = (grad_gelu * slope).astype(BF16)
    back_ref[...] = sum(
        dot(act_ref[shard], in_ref[...], 1, 1) for shard, (in_ref, _) in enumerate(shards)
    ).astype(back_ref.dtype)
    branch_ref[...] = sum(
        dot(gelu_ref[shard], out_ref[...], 1, 0) for shard, (_, out_ref) in enumerate(shards)
    ).astype(branch_ref.dtype)


def feed_forward(normed, grad, w_in, w_out, other):
    tokens, width = normed.shape
    units = w_in.shape[1]
    return call(
        ffn_kernel,
        "feed_forward",
        6,
        1,
        [],
        [normed, grad, w_in, other[:width], w_out, other[width:]],
        [((2, tokens, units), BF16, "v")] * 2 + [((tokens, width), BF16, "w")] * 2,
    )


def middle_back_kernel(
    weight_ref,
    own_ref,
    other_ref,
    middle_ref,
    result_ref,
    gain_ref,
    grad_ref,
    low_ref,
    gain_grad_ref,
    *mixed_refs,
):
    row, at = turn()
    inner_size = mixed_refs[0].shape[1]
    back = own_ref[at(own_ref)].astype(F32) + other_ref[at(other_ref)].astype(F32)
    middle = middle_ref[at(middle_ref)]
    scale = lax.rsqrt(jnp.mean(middle * middle, axis=-1, keepdims=True) + EPS)
    scaled = back * gain_ref[...]
    inner = jnp.mean(scaled * middle, axis=-1, keepdims=True)
    grad = result_ref[at(result_ref)] + scale * scaled - middle * (scale * scale * scale * inner)
    gain_grad = jnp.sum(back * (middle * scale), axis=0, keepdims=True)

    @pl.when(row == 0)
    def _():
        gain_grad_ref[...] = gain_grad

    @pl.when(row > 0)
    def _():
        gain_grad_ref[...] += gain_grad

    grad_ref[at(grad_ref)] = grad
    low = grad.astype(BF16)
    low_ref[at(low_ref)] = low
    mixed = dot(weight_ref[...], low, 1, 1).astype(BF16)
    for a, ref in enumerate(mixed_refs):
        ref[row] = mixed[a * inner_size : (a + 1) * inner_size]


def middle_back(gathered, own, other, middle, grad_result, gain, parts):
    rows, size, width = middle.shape
    inner = gathered.shape[0] // parts
    return call(
        middle_back_kernel,
        "middle_back",
        4,
        rows,
        [],
        [gathered, (own, "h"), (other, "h"), (middle, "h"), (grad_result, "h"), gain],
        [(middle.shape, F32, "h"), (middle.shape, BF16, "h"), ((1, width), F32, "w")]
        + [((rows, inner, size), BF16, "v")] * parts,
    )


def attend_back_kernel(heads, parts, place_ref, length_ref, joint_ref, bias_ref, log_ref, *refs):
    mixed_refs = refs[:parts]
    joint_grads = refs[parts : 2 * parts]
    table_ref, sums = refs[2 * parts :]
    size = mixed_refs[0].shape[2]
    me = place_ref[0]
    inner = joint_ref.shape[1] // 3
    head_size = inner // heads
    count = 2
    row, at = turn()
    come = at(joint_ref)

    @pl.when(row == 0)
    def _():
        sums[...] = jnp.zeros_like(sums)

    valid = chunk_valid(length_ref[row], me, parts, size, count)
    for head in range(heads):
        low = head * head_size
        key_rows = slice(inner + low, inner + low + head_size)
        value_rows = slice(2 * inner + low, 2 * inner + low + head_size)
        key = joint_ref[come, key_rows, :]
        value = joint_ref[come, value_rows, :]
        grad_key = grad_value = None
        for first in range(0, parts, count):
            lanes = slice(first * size, (first + count) * size)
            query = joint_ref[come, low : low + head_size, lanes]
            grad_mixed = jnp.concatenate(
                [
                    mixed_refs[first + step][row, low : low + head_size, :]
                    for step in range(count)
                ],
                axis=1,
            )
            scores = dot(key, query, 0, 0) + chunk_bias(bias_ref, head, me, parts, first, count)
            probs = jnp.where(
                valid, jnp.exp(scores - log_ref[come, head : head + 1, lanes]), 0.0
            )
            grad_probs = dot(value, grad_mixed, 0, 0)
            inner_sum = jnp.sum(probs * grad_probs, axis=0, keepdims=True)
            grad_scores = probs * (grad_probs - inner_sum)
            low_scores = grad_scores.astype(BF16)
            more_value = dot(grad_mixed, probs.astype(BF16), 1, 1)
            more_key = dot(query, low_scores, 1, 1)
            grad_value = more_value if grad_value is None else grad_value + more_value
            grad_key = more_key if grad_key is None else grad_key + more_key
            grad_query = dot(key, low_scores, 1, 0).astype(BF16)
            for step in range(count):
                joint_grads[first + step][row, low : low + head_size, :] = grad_query[
                    :, step * size : (step + 1) * size
                ]
            for step in range(count):
                for a_k in range(parts):
                    place = (a_k ^ me) - ((first + step) ^ me) + parts - 1
                    sums[head, place] += grad_scores[
                        a_k * size : (a_k + 1) * size, step * size : (step + 1) * size
                    ]
        grad_key = grad_key.astype(BF16)
        grad_value = grad_value.astype(BF16)
        for a in range(parts):
            lanes = slice(a * size, (a + 1) * size)
            joint_grads[a][row, key_rows, :] = grad_key[:, lanes]
            joint_grads[a][row, value_rows, :] = grad_value[:, lanes]

    pl.when(row == pl.num_programs(0) - 1)(
        functools.partial(table_sums, heads, parts, size, sums, table_ref)
    )


def table_sums(heads, parts, size, sums, table_ref):
    ones = jnp.ones((8, size), F32)
    for head in range(heads):
        lines = [jnp.zeros((1, size), F32)] * 32
        for at in range(2 * parts - 1):
            distance = at - (parts - 1)
            present = codes_in(size, distance)
            codes = code_block(size, distance) if len(present) > 1 else None
            block = sums[head, at]
            for code in present:
                chosen = block if codes is None else jnp.where(codes == code, block, 0.0)
                lines[code] = lines[code] + jnp.sum(chosen, axis=0, keepdims=True)
        lined = jnp.concatenate(lines + [jnp.zeros((size - 32, size), F32)], axis=0)
        table_ref[head] = dot(ones, lined, 1, 1, lax.Precision.HIGHEST)


def attend_back(place, lengths, joint, bias, logs, mixed):
    rows, wide, full = joint.shape
    parts = len(mixed)
    heads = bias.shape[0]
    inner, size = mixed[0].shape[1:]
    return call(
        functools.partial(attend_back_kernel, heads, parts),
        "attend_back",
        14,
        rows,
        [place, lengths],
        [(joint, "h"), bias, (logs, "h"), *mixed],
        [((rows, wide, size), BF16, "v")] * parts + [((heads, 8, size), F32, "w")],
        [pltpu.VMEM(bias.shape, F32)],
    )


def ffn_grad_kernel(
    normed_ref,
    normed_pair_ref,
    grad_ref,
    grad_pair_ref,
    gelu_ref,
    gelu_pair_ref,
    act_ref,
    act_pair_ref,
    out_ref,
):
    half = pl.program_id(0)
    cuts = out_ref.shape[1]
    share = out_ref.shape[2] // 2
    size = cuts * share
    lanes = pl.ds(pl.multiple_of(half * size, size), size)
    normed = jnp.concatenate((normed_ref[:, lanes], normed_pair_ref[:, lanes]), axis=0)
    grad = jnp.concatenate((grad_ref[...], grad_pair_ref[...]), axis=0)
    for shard in range(2):
        act = jnp.concatenate((act_ref[shard], act_pair_ref[shard]), axis=0)
        gelu = jnp.concatenate(
            (gelu_ref[shard, :, lanes], gelu_pair_ref[shard, :, lanes]), axis=0
        )
        for side, (left, right) in enumerate(((normed, act), (gelu, grad))):
            total = dot(left, right, 0, 0).astype(BF16)
            for cut in range(cuts):
                out_ref[side, cut, shard * share : (shard + 1) * share] = total[
                    cut * share : (cut + 1) * share
                ]


def ffn_grad(arrays, copies):
    width, units = arrays[0].shape[1], arrays[4].shape[2]
    steps = 2
    share = (width + units) // copies
    return pl.pallas_call(
        ffn_grad_kernel,
        grid=(steps,),
        in_specs=[WIDE] * len(arrays),
        out_specs=pl.BlockSpec(
            (2, copies // (2 * steps), 2 * share, width), lambda m: (0, m, 0, 0)
        ),
        out_shape=pltpu.HBM((2, copies // 2, 2 * share, width), BF16),
        compiler_params=pltpu.CompilerParams(vmem_limit_bytes=ROOM),
        cost_estimate=cost(6),
        name="ffn_grad",
    )(*[near(array) for array in arrays])


def joint_grad_kernel(
    parts,
    normed_ref,
    query_ref,
    key_ref,
    value_ref,
    gain_ref,
    gain_two_ref,
    table_ref,
    branch_ref,
    mixed_ref,
    *refs,
):
    joint_grads = refs[:parts]
    out_ref, total, out_total = refs[parts:]
    row, at = turn()
    more = dot(
        jnp.concatenate([ref[row] for ref in joint_grads], axis=1), normed_ref[at(normed_ref)], 1, 0
    )
    more_out = dot(mixed_ref[at(mixed_ref)], branch_ref[at(branch_ref)], 1, 0)

    @pl.when(row == 0)
    def _():
        total[...] = more
        out_total[...] = more_out

    @pl.when(row > 0)
    def _():
        total[...] += more
        out_total[...] += more_out

    @pl.when(row == pl.num_programs(0) - 1)
    def _():
        width = out_ref.shape[2]
        wide = total.shape[0]
        inner = wide // 3
        cuts = out_ref.shape[0]
        gain_grad = (
            sum(
                jnp.sum(
                    total[part * inner : (part + 1) * inner] * ref[...].astype(F32),
                    axis=0,
                    keepdims=True,
                )
                for part, ref in enumerate((query_ref, key_ref, value_ref))
            )
            / gain_ref[...]
        )
        heads, _, size = table_ref.shape
        pad = jnp.zeros((1, width - size), F32)
        lines = [gain_grad, gain_two_ref[...]] + [
            jnp.concatenate([table_ref[head, 0:1], pad], axis=1) for head in range(heads)
        ]
        lines.append(jnp.zeros((8 - len(lines), width), F32))
        share, out_share = wide // cuts, inner // cuts
        for cut in range(cuts):
            out_ref[cut, 0:share] = total[cut * share : (cut + 1) * share].astype(BF16)
            low = share
            for a in range(parts):
                from_ = a * inner + cut * out_share
                out_ref[cut, low : low + out_share] = out_total[
                    from_ : from_ + out_share
                ].astype(BF16)
                low += out_share
            if cut == 0:
                out_ref[cut, low : low + 8] = jnp.concatenate(lines, axis=0).astype(BF16)
            else:
                out_ref[cut, low : low + 8] = jnp.zeros((8, width), BF16)


def joint_grad(
    normed, weights, gain, gain_two_grad, table_grad, grad_branch, joint_grads, mixed, copies
):
    rows, _, width = normed.shape
    wide = joint_grads[0].shape[1]
    inner = wide // 3
    parts = len(joint_grads)
    cuts = copies if inner % (8 * copies) == 0 else 1
    length = (wide + parts * inner) // cuts + 8
    return call(
        functools.partial(joint_grad_kernel, parts),
        "joint_grad",
        6,
        rows,
        [],
        [
            (normed, "h"),
            *weights,
            gain,
            (gain_two_grad, "w"),
            (table_grad, "w"),
            (grad_branch, "h"),
            (mixed, "h"),
            *joint_grads,
        ],
        [((cuts, length, width), BF16, "w")],
        [pltpu.VMEM((wide, width), F32), pltpu.VMEM((parts * inner, width), F32)],
    )[0]


def recut(values, wide, parts, inner, copies):
    width = values.shape[2]
    whole = values[0]
    out = [whole[:wide].reshape(copies, -1, width)]
    for a in range(parts):
        low = wide + a * inner
        out.append(whole[low : low + inner].reshape(copies, -1, width))
    extra = whole[None, wide + parts * inner :]
    out.append(jnp.concatenate([extra] + [jnp.zeros_like(extra)] * (copies - 1), axis=0))
    return jnp.concatenate(out, axis=1)


def hidden_grad_kernel(place_ref, weight_ref, middle_ref, hidden_ref, gain_ref, *refs):
    joint_grads, out_ref = refs[:-1], refs[-1]
    me = place_ref[0]
    row, at = turn()
    back = sum(dot(ref[row], weight_ref[a], 0, 0) for a, ref in enumerate(joint_grads))
    hidden = hidden_ref[at(hidden_ref)].astype(F32)
    scale = lax.rsqrt(jnp.mean(hidden * hidden, axis=-1, keepdims=True) + EPS)
    scaled = back * gain_ref[...]
    inner = jnp.mean(scaled * hidden, axis=-1, keepdims=True)
    out_ref[at(out_ref)] = (
        middle_ref[at(middle_ref)] + scale * scaled - hidden * (scale * scale * scale * inner)
    )


def hidden_grad(place, gathered, grad_middle, hidden, gain, joint_grads):
    return call(
        hidden_grad_kernel,
        "hidden_grad",
        150,
        hidden.shape[0],
        [place],
        [gathered, (grad_middle, "h"), (hidden, "h"), gain, *joint_grads],
        [(hidden.shape, F32, "h")],
    )[0]


def after(values, *others):
    return lax.optimization_barrier((values, *others))[0]


def swap(values, distance):
    parts = lax.axis_size("tp")
    return lax.ppermute(values, "tp", [(i, i ^ distance) for i in range(parts)])


def swap_all(blocks):
    return [blocks[0]] + [swap(block, a) for a, block in enumerate(blocks) if a]


def gather_line(values, first, second):
    pair = swap(values, 1)
    inner = [(1, 2), (2, 1)]
    outer = [(1, 0), (2, 3)]
    last_low = lax.ppermute(values, "tp", inner)
    pair, last_low, *first = lax.optimization_barrier((pair, last_low, *first))
    far_low = lax.ppermute(pair, "tp", inner)
    far_high = lax.ppermute(last_low, "tp", outer)
    far_low, far_high, *second = lax.optimization_barrier((far_low, far_high, *second))
    last_high = lax.ppermute(far_low, "tp", outer)
    return [values, pair, far_low, far_high, last_low, last_high], first, second


def across(values, bit):
    count = lax.axis_size("dp")
    return lax.ppermute(values, "dp", [(i, i ^ (1 << bit)) for i in range(count)])


def dp_bits():
    return range(lax.axis_size("dp").bit_length() - 1)


def join(values, other=None):
    place = lax.axis_index("dp")
    for bit in reversed(dp_bits()):
        upper = (place >> bit) & 1
        if bit == 0 and other is not None:
            values, other = lax.optimization_barrier((values, other))
        came = across(values, bit)
        values = jnp.where(
            upper == 1,
            jnp.concatenate((came, values), axis=0),
            jnp.concatenate((values, came), axis=0),
        )
    return values, other


def by_place(values):
    count = len(dp_bits())
    order = tuple(reversed(range(count))) + tuple(range(count, count + values.ndim - 1))
    return values.reshape((2,) * count + values.shape[1:]).transpose(order).reshape(values.shape)


def local(
    hidden_in,
    lengths,
    inst_lengths,
    w_query,
    w_key,
    w_value,
    attention_output_weight,
    feedforward_input_weight,
    feedforward_output_weight,
    rel_table,
    gain_attn,
    gain_ffn,
    grad_output,
    grad_pooled,
):
    rows, size, width = hidden_in.shape
    parts = lax.axis_size("tp")
    copies = lax.axis_size("dp")
    me = lax.axis_index("tp")
    group = lax.axis_index("dp")
    heads = rel_table.shape[1]
    inner = w_query.shape[1]
    tokens = rows * size
    place = me.astype(jnp.int32).reshape(1)
    gain_one = gain_attn.astype(F32).reshape(1, width)
    gain_two = gain_ffn.astype(F32).reshape(1, width)

    def share_of(weights):
        share = weights.shape[0] // copies
        return lax.dynamic_slice_in_dim(weights, group * share, share, 0)

    def fetched(shares, lead):
        everything = lax.all_gather(shares, "dp", axis=0, tiled=False)
        rest = everything[:, lead:].reshape(copies, parts, -1, width)
        return (
            jnp.swapaxes(rest, 0, 1).reshape(-1, width),
            everything[:, :lead].reshape(-1, width),
            everything,
        )

    first = norm_one(hidden_in, gain_one)
    attention_weights = jnp.concatenate(
        (w_query.T, w_key.T, w_value.T), axis=0
    )
    bias = bias_blocks(rel_table.T.astype(F32), parts, size)

    other_share = share_of(
        jnp.concatenate((feedforward_input_weight, feedforward_output_weight), axis=0)
    )
    ffn_share = other_share.shape[0]
    out_part = share_of(attention_output_weight)
    columns = grad_pooled.shape[1]
    spread = lax.dynamic_update_slice(
        jnp.zeros((rows, width), BF16), grad_pooled, (0, me * columns)
    )
    spread = swap_all([spread] * parts)
    blocks, (bias,), (out_part, other_share, *spread) = gather_line(
        first, [bias], [out_part, other_share] + spread
    )
    pool_cot = sum(block.astype(F32) for block in spread)
    counts = (lengths - inst_lengths).astype(F32)
    spots = me * size + jnp.arange(size, dtype=jnp.int32)
    mask = (
        (spots[None, :] >= inst_lengths[:, None]) & (spots[None, :] < lengths[:, None])
    ).astype(F32)
    grad_result = (
        grad_output.astype(F32)
        + pool_cot[:, None, :] * (mask / counts[:, None])[:, :, None]
    )
    grad_low = grad_result.astype(BF16).reshape(tokens, width)

    came = swap_all([out_part, out_part, jnp.concatenate((out_part, other_share), axis=0), out_part])
    out_size = out_part.shape[0]
    out_gathered, other_weights, _ = fetched(
        after(
            jnp.concatenate([came[2][out_size:]] + [block[:out_size] for block in came], axis=0),
            blocks[5],
        ),
        ffn_share,
    )
    blocks[5], grad_low = lax.optimization_barrier((blocks[5], grad_low))
    grad_low_pair = swap(grad_low, 1)
    came_joint = jnp.concatenate(
        swap_all([after(share_of(attention_weights), blocks[5])] * parts), axis=0
    )
    normed, joint, logs, *mixed = attend(
        place, lengths, blocks, (w_query.T, w_key.T, w_value.T), bias, heads
    )
    mixed, grad_low_pair, came_joint = lax.optimization_barrier((mixed, grad_low_pair, came_joint))
    gathered, _, joint_there = fetched(came_joint, 0)
    gathered = gathered.reshape(parts, -1, width)
    mixed = swap_all(mixed)
    middle, second, mixed = middle_of(out_gathered, hidden_in, gain_two, mixed)
    second = second.reshape(tokens, width)
    second_pair = swap(second, 1)

    weights = (feedforward_input_weight, feedforward_output_weight, other_weights)
    gelu, act, branch, back = feed_forward(second, grad_low, *weights)
    gelu_pair, act_pair, branch_pair, back_pair = feed_forward(
        second_pair, grad_low_pair, *weights
    )

    stacked = ffn_grad(
        (second, second_pair, grad_low, grad_low_pair, gelu, gelu_pair, act, act_pair), copies
    )
    summed = lax.psum_scatter(
        after(stacked, joint_there).reshape(-1, width), "dp", scatter_dimension=0, tiled=True
    )

    back_came = after(swap(back_pair, 1), stacked)

    grad_middle, grad_branch, gain_two_grad, *grad_mixed = middle_back(
        out_gathered,
        back.reshape(rows, size, width),
        back_came.reshape(rows, size, width),
        middle,
        grad_result,
        gain_two,
        parts,
    )
    grad_mixed = swap_all(grad_mixed)

    *joint_grads, table_grad = attend_back(place, lengths, joint, bias, logs, grad_mixed)
    came = swap_all(joint_grads)

    branch_came = swap(after(branch_pair, grad_mixed[-1]), 1)
    result = (
        middle
        + branch.reshape(rows, size, width).astype(F32)
        + branch_came.reshape(rows, size, width).astype(F32)
    )
    wide = 3 * inner
    heads_grad = joint_grad(
        normed,
        (w_query.T, w_key.T, w_value.T),
        gain_one,
        gain_two_grad,
        table_grad,
        grad_branch,
        joint_grads,
        mixed,
        copies,
    )
    if heads_grad.shape[0] != copies:
        heads_grad = recut(heads_grad, wide, parts, inner, copies)
    mine = lax.psum_scatter(
        heads_grad.reshape(-1, width), "dp", scatter_dimension=0, tiled=True
    )
    summed = after(summed, heads_grad)
    own_sum = summed[:ffn_share].astype(F32) + swap(summed[ffn_share:], 2).astype(F32)
    whole_ffn = lax.all_gather(own_sum.astype(BF16), "dp", axis=0, tiled=True).astype(F32)
    grad_hidden = hidden_grad(
        place,
        gathered,
        grad_middle,
        hidden_in,
        gain_one,
        [after(came[0], heads_grad, own_sum, branch_came)] + came[1:],
    )
    mine, result = after((mine, result), grad_hidden)

    layer_out = result.astype(BF16)
    pool_part = jnp.sum(result * mask[:, :, None], axis=1) / counts[:, None]
    pool_sum = pool_part + sum(swap(pool_part, a) for a in range(1, parts))
    pooled = lax.dynamic_slice_in_dim(pool_sum, me * columns, columns, 1)
    share, out_share = wide // copies, inner // copies
    extra = mine[share + parts * out_share :]
    moved = swap_all(
        [
            jnp.concatenate(
                (mine[share + a * out_share : share + (a + 1) * out_share], extra), axis=0
            )
            for a in range(parts)
        ]
    )
    moved = sum(block.astype(F32) for block in moved)
    whole, _ = join(
        jnp.concatenate(
            (
                mine[:share].astype(F32),
                moved[:out_share],
                moved[out_share : out_share + 2],
                extra[2:].astype(F32),
            ),
            axis=0,
        )[None].astype(BF16)
    )
    joint_sum = by_place(whole[:, :share]).reshape(wide, width).astype(F32)
    whole_out = by_place(whole[:, share : share + out_share]).reshape(inner, width).astype(F32)
    extra = whole[0, share + out_share :].astype(F32)
    table_sum = extra[2 : 2 + heads, : rel_table.shape[0]].T

    return (
        layer_out,
        pooled,
        grad_hidden,
        joint_sum[:inner].T,
        joint_sum[inner : 2 * inner].T,
        joint_sum[2 * inner : wide].T,
        whole_out,
        whole_ffn[:width],
        whole_ffn[width:],
        table_sum,
        extra[0],
        extra[1],
    )


def solution(mesh):
    in_specs = (
        P("dp", "tp", None),
        P("dp"),
        P("dp"),
        P(None, "tp"),
        P(None, "tp"),
        P(None, "tp"),
        P("tp", None),
        P(None, "tp"),
        P("tp", None),
        P(None, "tp"),
        P(),
        P(),
        P("dp", "tp", None),
        P("dp", "tp"),
    )
    out_specs = (
        P("dp", "tp", None),
        P("dp", "tp"),
        P("dp", "tp", None),
        P(None, "tp"),
        P(None, "tp"),
        P(None, "tp"),
        P("tp", None),
        P(None, "tp"),
        P("tp", None),
        P(None, "tp"),
        P(),
        P(),
    )
    return jax.shard_map(local, mesh=mesh, in_specs=in_specs, out_specs=out_specs, check_vma=False)
```

time: 321 us -> 306 us (0.953)
  Pallas kernels: 84.5 us -> 66.4 us
  waiting for transfers between devices: 127 us -> 119 us
  starting transfers between devices: 61.4 us -> 68.4 us
  local copies, waits for them, and re-layouts: 25.4 us -> 28.7 us
    pallas_call x11, Pallas kernels: 84.5 us -> 66.4 us  [the longest x10 59.8 us: call(): pl.pallas_call(kernel, grid=(rows,), in_specs=[SCALARS] * len(scalars) +...]
    ppermute x27 -> x30, waiting for transfers between devices: 92.1 us -> 84.8 us  [swap(): return lax.ppermute(values, 'tp', [(i, i ^ distance) for i in range(parts)])]
    ppermute x27 -> x30, starting transfers between devices: 52.9 us -> 59.1 us  [swap(): return lax.ppermute(values, 'tp', [(i, i ^ distance) for i in range(parts)])]
    all_gather x1 -> x2, waiting for transfers between devices: 0.01 us -> 5.29 us  [fetched(): everything = lax.all_gather(shares, 'dp', axis=0, tiled=False)]
    ppermute x1, waiting for transfers between devices: 12.2 us -> 7.06 us  [gather_line(): last_high = lax.ppermute(far_low, 'tp', outer)]
    unnamed x84 -> x120, local copies, waits for them, and re-layouts: 7.59 us -> 12.1 us
  transfers between devices with their start and end apart: 39 -> 42, of which waited for: 20 -> 22; matrix products, arithmetic and copies ran while one was open for 7% -> 7% of each run, Pallas kernels for 26% -> 22%
where the time goes in v2:
time: 306 us; the launch traced here: 305 us
  waiting for transfers between devices  119 us (39%)
  starting transfers between devices  68.4 us (22%)
  Pallas kernels  66.4 us (22%)
  local copies, waits for them, and re-layouts  28.7 us (9%)
  between operations  14.6 us (5%)
  other arithmetic  8.5 us (3%)
    ppermute x30, waiting for transfers between devices, swap(): return lax.ppermute(values, 'tp', [(i, i ^ distance) for i in range(parts)])  84.8 us
    pallas_call x10, Pallas kernels, call(): pl.pallas_call(kernel, grid=(rows,), in_specs=[SCALARS] * len(scalars) +...  59.8 us
    ppermute x30, starting transfers between devices, swap(): return lax.ppermute(values, 'tp', [(i, i ^ distance) for i in range(parts)])  59.1 us
    ppermute x3, waiting for transfers between devices, across(): return lax.ppermute(values, 'dp', [(i, i ^ 1 << bit) for i in range(count)])  18.1 us
    unnamed x120, local copies, waits for them, and re-layouts  12.1 us
    ppermute x1, waiting for transfers between devices, gather_line(): last_high = lax.ppermute(far_low, 'tp', outer)  7.06 us
    pallas_call x1, Pallas kernels, ffn_grad(): pl.pallas_call(ffn_grad_kernel, grid=(steps,), in_specs=[WIDE] * len(arra...  6.62 us
  transfers between devices with their start and end apart: 42, of which 22 were waited for; matrix products, arithmetic and copies ran while one was open for 7% of the time, Pallas kernels for 22%

profile of v2, /device:TPU:0, one launch (start us, length us, event | category | flops | bytes accessed | tf_op | source)
XLA Modules:
  0.0 305.3 jit_solution(11270946789914105683)
XLA Ops:
  9.3 3.1 %collective-permute-start = (bf16[3,128,768]{2,1,0:T(8,128)(2,1)S(1)}, bf16[3,128,768]{2,1,0:T(8,128)(2,1)}, u32[]{:S(2)}, u32[]{:S(2)}) collective-permute-start(bf16[3,128,768]{2,1,0:T(8,128)(2,1)S(1)} %norm_one.1.own_ref), channel_id=1, source_target_pairs={{0,1},{1,0},{2,3},{3,2},{4,5},{5,4},{6,7},{7,6},{8,9},{9,8},{10,11... | collective-permute-start | bytes 1769480 | tf_op jit(solution)/shard_map/ppermute | solution.py:665
  13.9 2.5 bias_blocks.1.bias_ref
  16.4 9.4 %collective-permute-done.pair_ref = bf16[3,128,768]{2,1,0:T(8,128)(2,1)} collective-permute-done((bf16[3,128,768]{2,1,0:T(8,128)(2,1)S(1)}, bf16[3,128,768]{2,1,0:T(8,128)(2,1)}, u32[]{:S(2)}, u32[]{:S(2)}) %collective-permute-start) | collective-permute-done | bytes 589856 | tf_op jit(solution)/shard_map/ppermute | solution.py:665
  28.8 7.9 %collective-permute-start.4 = (bf16[3,768]{1,0:T(4,128)(2,1)S(1)}, bf16[3,768]{1,0:T(4,128)(2,1)}, u32[]{:S(2)}, u32[]{:S(2)}) collective-permute-start(bf16[3,768]{1,0:T(4,128)(2,1)S(1)} %dynamic_update_slice.3), channel_id=1, source_target_pairs={{0,1},{1,0},{2,3},{3,2},{4,5},{5,4},{6,7},{7,6},{8,9},{9,8},{10,11... | collective-permute-start | bytes 13832 | tf_op jit(solution)/shard_map/ppermute | solution.py:665
  39.5 8.6 %collective-permute-done.4 = bf16[3,768]{1,0:T(4,128)(2,1)} collective-permute-done((bf16[3,768]{1,0:T(4,128)(2,1)S(1)}, bf16[3,768]{1,0:T(4,128)(2,1)}, u32[]{:S(2)}, u32[]{:S(2)}) %collective-permute-start.4) | collective-permute-done | bytes 4640 | tf_op jit(solution)/shard_map/ppermute | solution.py:665
  53.9 9.9 %collective-permute-done.8 = bf16[216,768]{1,0:T(8,128)(2,1)S(1)} collective-permute-done((bf16[216,768]{1,0:T(8,128)(2,1)S(1)}, bf16[216,768]{1,0:T(8,128)(2,1)S(1)}, u32[]{:S(2)}, u32[]{:S(2)}) %collective-permute-start.8) | collective-permute-done | bytes 331808 | tf_op jit(solution)/shard_map/ppermute | solution.py:665
  67.0 7.1 %collective-permute-done.7.last_high_ref = bf16[3,128,768]{2,1,0:T(8,128)(2,1)} collective-permute-done((bf16[3,128,768]{2,1,0:T(8,128)(2,1)}, bf16[3,128,768]{2,1,0:T(8,128)(2,1)}, u32[]{:S(2)}, u32[]{:S(2)}) %collective-permute-start.7) | collective-permute-done | bytes 589856 | tf_op jit(solution)/shard_map/ppermute | solution.py:681
  81.0 12.6 %attend.1 = (bf16[3,512,768]{2,1,0:T(8,128)(2,1)}, bf16[3,576,512]{2,1,0:T(8,128)(2,1)}, f32[3,3,512]{2,1,0:T(4,128)}, bf16[3,192,128]{2,1,0:T(8,128)(2,1)S(1)},...) custom-call(s32[1]{0:T(128)} %bitcast.place_ref, ...), custom_call_target="tpu_custom_call" | custom-call | flops 13200000000 | bytes 12000000 | tf_op jit(solution)/shard_map/attend/pallas_call | solution.py:81
  102.4 5.3 %all-gather.8.cloned.1.call-done = bf16[2304,768]{1,0:T(8,128)(2,1)} async-done(((bf16[288,768]{1,0:T(8,128)(2,1)}), bf16[2304,768]{1,0:T(8,128)(2,1)}) %all-gather.8.cloned.1.call-update) | async-done | bytes 3538960 | tf_op jit(solution)/shard_map/all_gather | solution.py:748
  109.1 2.6 collective-permute-done.16.refs_2_
  111.8 3.5 %middle_of.1 = (f32[3,128,768]{2,1,0:T(8,128)}, bf16[3,128,768]{2,1,0:T(8,128)(2,1)S(1)}, bf16[3,768,128]{2,1,0:T(8,128)(2,1)}) custom-call(bf16[768,768]{1,0:T(8,128)(2,1)S(1)} %bitcast.54, bf16[3,128,768]{2,1,0:T(8,128)(2,1)S(1)} %copy-done.18, f32[1,768]{1,0:T(1,128)S(1)} %reshape.280.gain_ref, bf16[3,192,128]{2,1,0:T(8,128)(2,1)S(1)} %copy-done.34, ...), custom_call_target="tpu_custom_call" | custom-call | flops 3300000000 | bytes 3000000 | tf_op jit(solution)/shard_map/middle_of/pallas_call | solution.py:81
  117.6 5.0 %feed_forward.2 = (bf16[2,384,768]{2,1,0:T(8,128)(2,1)S(1)}, bf16[2,384,768]{2,1,0:T(8,128)(2,1)S(1)}, bf16[384,768]{1,0:T(8,128)(2,1)}, bf16[384,768]{1,0:T(8,128)(2,1)}) custom-call(bf16[384,768]{1,0:T(8,128)(2,1)S(1)} %bitcast.73, bf16[384,768]{1,0:T(8,128)(2,1)S(1)} %bitcast.61, bf16[768,768]{1,0:T(8,128)(2,1)S(1)} %copy-done.3, ...), custom_call_target="tpu_custom_call" | custom-call | flops 6600000000 | bytes 6000000 | tf_op jit(solution)/shard_map/feed_forward/pallas_call | solution.py:81
  122.6 6.9 %collective-permute-done.18.normed_ref.normed_pair_ref = bf16[384,768]{1,0:T(8,128)(2,1)S(1)} collective-permute-done((bf16[384,768]{1,0:T(8,128)(2,1)S(1)}, bf16[384,768]{1,0:T(8,128)(2,1)S(1)}, u32[]{:S(2)}, u32[]{:S(2)}) %collective-permute-start.18) | collective-permute-done | bytes 589856 | tf_op jit(solution)/shard_map/ppermute | solution.py:665
  129.5 6.3 %feed_forward.3 = (bf16[2,384,768]{2,1,0:T(8,128)(2,1)S(1)}, bf16[2,384,768]{2,1,0:T(8,128)(2,1)S(1)}, bf16[384,768]{1,0:T(8,128)(2,1)}, bf16[384,768]{1,0:T(8,128)(2,1)}) custom-call(bf16[384,768]{1,0:T(8,128)(2,1)S(1)} %collective-permute-done.18.normed_ref.normed_pair_ref, bf16[384,768]{1,0:T(8,128)(2,1)} %collective-permute-done.11.grad_ref.grad_pair_ref, ...), custom_call_target="tpu_custom_call" | custom-call | flops 6600000000 | bytes 6000000 | tf_op jit(solution)/shard_map/feed_forward/pallas_call | solution.py:81
  135.7 6.6 %ffn_grad.1 = bf16[2,4,384,768]{3,2,1,0:T(8,128)(2,1)} custom-call(bf16[384,768]{1,0:T(8,128)(2,1)S(1)} %bitcast.74, bf16[384,768]{1,0:T(8,128)(2,1)S(1)} %collective-permute-done.18.normed_ref.normed_pair_ref, bf16[384,768]{1,0:T(8,128)(2,1)S(1)} %bitcast.62, bf16[384,768]{1,0:T(8,128)(2,1)} %collective-permute-done.11.grad_ref.grad_pair_ref, ...), custom_call_target="tpu_custom_call" | custom-call | flops 6600000000 | bytes 6000000 | tf_op jit(solution)/shard_map/ffn_grad/pallas_call | solution.py:507
  144.4 11.6 %collective-permute-done.19 = bf16[384,768]{1,0:T(8,128)(2,1)S(1)} collective-permute-done((bf16[384,768]{1,0:T(8,128)(2,1)}, bf16[384,768]{1,0:T(8,128)(2,1)S(1)}, u32[]{:S(2)}, u32[]{:S(2)}) %collective-permute-start.19) | collective-permute-done | bytes 589856 | tf_op jit(solution)/shard_map/ppermute | solution.py:665
  157.1 3.1 %middle_back.1 = (f32[3,128,768]{2,1,0:T(8,128)}, bf16[3,128,768]{2,1,0:T(8,128)(2,1)}, f32[1,768]{1,0:T(1,128)}, bf16[3,192,128]{2,1,0:T(8,128)(2,1)S(1)}, bf16...) custom-call(bf16[768,768]{1,0:T(8,128)(2,1)S(1)} %bitcast.55, ...), custom_call_target="tpu_custom_call" | custom-call | flops 4400000000 | bytes 4000000 | tf_op jit(solution)/shard_map/middle_back/pallas_call | solution.py:81
  160.8 4.7 %collective-permute-start.22 = (bf16[3,192,128]{2,1,0:T(8,128)(2,1)}, bf16[3,192,128]{2,1,0:T(8,128)(2,1)}, u32[]{:S(2)}, u32[]{:S(2)}) collective-permute-start(bf16[3,192,128]{2,1,0:T(8,128)(2,1)} %get-tuple-element.110), channel_id=1, source_target_pairs={{0,3},{1,2},{2,1},{3,0},{4,7},{5,6},{6,5},{7,4},{8,11},{9,10},{10,... | collective-permute-start | bytes 442376 | tf_op jit(solution)/shard_map/ppermute | solution.py:665
  170.6 3.1 %collective-permute-start.23 = (bf16[384,768]{1,0:T(8,128)(2,1)}, bf16[384,768]{1,0:T(8,128)(2,1)}, u32[]{:S(2)}, u32[]{:S(2)}) collective-permute-start(bf16[384,768]{1,0:T(8,128)(2,1)} %get-tuple-element.120), channel_id=1, source_target_pairs={{0,1},{1,0},{2,3},{3,2},{4,5},{5,4},{6,7},{7,6},{8,9},{9,8},{10,11... | collective-permute-start | bytes 1769480 | tf_op jit(solution)/shard_map/ppermute | solution.py:665
  176.5 14.9 %attend_back.1 = (bf16[3,576,128]{2,1,0:T(8,128)(2,1)S(1)}, bf16[3,576,128]{2,1,0:T(8,128)(2,1)}, bf16[3,576,128]{2,1,0:T(8,128)(2,1)}, bf16[3,576,128]{2,1,0:T(8,128)(2,1)}, f32[3,8,128]{2,1,0:T(8,128)}) custom-call(s32[1]{0:T(128)} %bitcast.place_ref, s32[3]{0:T(128)S(1)} %copy-done.16, bf16[3,576,512]{2,1,0:T(8,128)(2,1)S(1)} %copy-done.37, ...), custom_call_target="tpu_custom_call" | custom-call | flops 15399999488 | bytes 14000000 | tf_op jit(solution)/shard_map/attend_back/pallas_call | solution.py:81
  197.0 7.0 %joint_grad.1 = bf16[8,176,768]{2,1,0:T(8,128)(2,1)} custom-call(bf16[3,512,768]{2,1,0:T(8,128)(2,1)S(1)} %copy-done.27, bf16[192,768]{1,0:T(8,128)(2,1)S(1)} %bitcast.65, bf16[192,768]{1,0:T(8,128)(2,1)S(1)} %bitcast.68, bf16[192,768]{1,0:T(8,128)(2,1)S(1)} %bitcast.71, f32[1,768]{1,0:T(1,128)S(1)} %reshape.278.gain_ref, f32[1,768]{1,0:T(1,128)S(1)} %copy-done.39, ...), custom_call_target="tpu_custom_call" | custom-call | flops 6600000000 | bytes 6000000 | tf_op jit(solution)/shard_map/joint_grad/pallas_call | solution.py:81
  204.3 6.7 %collective-permute-done.25.refs_1_ = bf16[3,576,128]{2,1,0:T(8,128)(2,1)} collective-permute-done((bf16[3,576,128]{2,1,0:T(8,128)(2,1)}, bf16[3,576,128]{2,1,0:T(8,128)(2,1)}, u32[]{:S(2)}, u32[]{:S(2)}) %collective-permute-start.25) | collective-permute-done | bytes 442400 | tf_op jit(solution)/shard_map/ppermute | solution.py:665
  211.0 14.7 %collective-permute-done.26.refs_2_ = bf16[3,576,128]{2,1,0:T(8,128)(2,1)} collective-permute-done((bf16[3,576,128]{2,1,0:T(8,128)(2,1)}, bf16[3,576,128]{2,1,0:T(8,128)(2,1)}, u32[]{:S(2)}, u32[]{:S(2)}) %collective-permute-start.26) | collective-permute-done | bytes 442400 | tf_op jit(solution)/shard_map/ppermute | solution.py:665
  229.2 4.8 %hidden_grad.1 = f32[3,128,768]{2,1,0:T(8,128)} custom-call(s32[1]{0:T(128)} %bitcast.place_ref, bf16[4,576,768]{2,1,0:T(8,128)(2,1)S(1)} %bitcast.53, f32[3,128,768]{2,1,0:T(8,128)S(1)} %copy-done.28, bf16[3,128,768]{2,1,0:T(8,128)(2,1)S(1)} %copy-done.19, f32[1,768]{1,0:T(1,128)S(1)} %reshape.278.gain_ref, bf16[3,576,128]{2,1,0:T(8,128)(2,1)S(1)} %copy-done.32, ...), custom_call_target="tpu_custom_call" | custom-call | flops 165000003584 | bytes 150000000 | tf_op jit(solution)/shard_map/hidden_grad/pallas_call | solution.py:81
  235.1 6.5 %collective-permute-start.24 = (bf16[192,768]{1,0:T(8,128)(2,1)S(1)}, bf16[192,768]{1,0:T(8,128)(2,1)S(1)}, u32[]{:S(2)}, u32[]{:S(2)}) collective-permute-start(bf16[192,768]{1,0:T(8,128)(2,1)S(1)} %slice.102), channel_id=1, source_target_pairs={{0,2},{1,3},{2,0},{3,1},{4,6},{5,7},{6,4},{7,5},{8,10},{9,11},{10,... | collective-permute-start | bytes 884744 | tf_op jit(solution)/shard_map/ppermute | solution.py:665
  243.4 3.3 %reduce-scatter.3.cloned.1.call-done = bf16[176,768]{1,0:T(8,128)(2,1)} async-done(((bf16[1408,768]{1,0:T(8,128)(2,1)}), bf16[176,768]{1,0:T(8,128)(2,1)}) %reduce-scatter.3.cloned.1.call-update) | async-done | bytes 270352 | tf_op jit(solution)/shard_map/reduce_scatter | solution.py:861
  251.2 2.5 collective-permute-start.32
  256.3 3.3 %collective-permute-done.33 = bf16[32,768]{1,0:T(8,128)(2,1)S(1)} collective-permute-done((bf16[32,768]{1,0:T(8,128)(2,1)S(1)}, bf16[32,768]{1,0:T(8,128)(2,1)S(1)}, u32[]{:S(2)}, u32[]{:S(2)}) %collective-permute-start.33) | collective-permute-done | bytes 49184 | tf_op jit(solution)/shard_map/ppermute | solution.py:665
  260.8 5.8 %collective-permute-done.34 = bf16[1,104,768]{2,1,0:T(8,128)(2,1)S(1)} collective-permute-done((bf16[1,104,768]{2,1,0:T(8,128)(2,1)S(1)}, bf16[1,104,768]{2,1,0:T(8,128)(2,1)S(1)}, u32[]{:S(2)}, u32[]{:S(2)}) %collective-permute-start.34) | collective-permute-done | bytes 159776 | tf_op jit(solution)/shard_map/ppermute | solution.py:687
  268.3 12.3 %collective-permute-done.35 = bf16[2,104,768]{2,1,0:T(8,128)(2,1)S(1)} collective-permute-done((bf16[2,104,768]{2,1,0:T(8,128)(2,1)S(1)}, bf16[2,104,768]{2,1,0:T(8,128)(2,1)S(1)}, u32[]{:S(2)}, u32[]{:S(2)}) %collective-permute-start.35) | collective-permute-done | bytes 319520 | tf_op jit(solution)/shard_map/ppermute | solution.py:687
  282.1 4.3 %collective-permute-start.30 = (f32[3,768]{1,0:T(4,128)S(1)}, f32[3,768]{1,0:T(4,128)S(1)}, u32[]{:S(2)}, u32[]{:S(2)}) collective-permute-start(f32[3,768]{1,0:T(4,128)S(1)} %broadcast_divide_fusion), channel_id=1, source_target_pairs={{0,3},{1,2},{2,1},{3,0},{4,7},{5,6},{6,5},{7,4},{8,11},{9,10},{10,... | collective-permute-start | bytes 27656 | tf_op jit(solution)/shard_map/ppermute | solution.py:665
  294.6 4.2 %fusion.8 = (f32[768,768]{1,0:T(8,128)}, f32[768,768]{1,0:T(8,128)}) fusion(bf16[1536,768]{1,0:T(8,128)(2,1)} %all-gather.6.cloned.1.call-done), kind=kLoop, calls=%fused_computation.55 | loop fusion | bytes 9437184 | tf_op jit(solution)/shard_map/slice | solution.py:917
  (238 shorter events, 80.8 us)
Async XLA Ops:
  7.2 100.5 %all-gather.8.cloned.1.call-start = ((), (), s32[]{:S(2)}) async-start(), calls=%async_computation.5 | async-start | bytes 3981312 | tf_op jit(solution)/shard_map/all_gather | solution.py:748
  9.3 16.5 %collective-permute-start = (bf16[3,128,768]{2,1,0:T(8,128)(2,1)S(1)}, bf16[3,128,768]{2,1,0:T(8,128)(2,1)}, u32[]{:S(2)}, u32[]{:S(2)}) collective-permute-start(bf16[3,128,768]{2,1,0:T(8,128)(2,1)S(1)} %norm_one.1.own_ref), channel_id=1, source_target_pairs={{0,1},{1,0},{2,3},{3,2},{4,5},{5,4},{6,7},{7,6},{8,9},{9,8},{10,11... | collective-permute-start | bytes 1769480 | tf_op jit(solution)/shard_map/ppermute | solution.py:665
  12.4 13.4 %collective-permute-start.1 = (bf16[3,128,768]{2,1,0:T(8,128)(2,1)S(1)}, bf16[3,128,768]{2,1,0:T(8,128)(2,1)}, u32[]{:S(2)}, u32[]{:S(2)}) collective-permute-start(bf16[3,128,768]{2,1,0:T(8,128)(2,1)S(1)} %norm_one.1.own_ref), channel_id=1, source_target_pairs={{1,2},{2,1},{5,6},{6,5},{9,10},{10,9},{13,14},{14,13},{17,18},{18,... | collective-permute-start | bytes 1769480 | tf_op jit(solution)/shard_map/ppermute | solution.py:676
  25.8 22.3 %collective-permute-start.2 = (bf16[3,128,768]{2,1,0:T(8,128)(2,1)}, bf16[3,128,768]{2,1,0:T(8,128)(2,1)}, u32[]{:S(2)}, u32[]{:S(2)}) collective-permute-start(bf16[3,128,768]{2,1,0:T(8,128)(2,1)} %collective-permute-done.pair_ref), channel_id=1, source_target_pairs={{1,2},{2,1},{5,6},{6,5},{9,10},{10,9},{13,14},{14,13},{17,18},{18,... | collective-permute-start | bytes 1769480 | tf_op jit(solution)/shard_map/ppermute | solution.py:678
  27.3 20.7 %collective-permute-start.3 = (bf16[3,128,768]{2,1,0:T(8,128)(2,1)}, bf16[3,128,768]{2,1,0:T(8,128)(2,1)}, u32[]{:S(2)}, u32[]{:S(2)}) collective-permute-start(bf16[3,128,768]{2,1,0:T(8,128)(2,1)} %collective-permute-done.1.last_low_ref), channel_id=1, source_target_pairs={{1,0},{2,3},{5,4},{6,7},{9,8},{10,11},{13,12},{14,15},{17,16},{18,... | collective-permute-start | bytes 1769480 | tf_op jit(solution)/shard_map/ppermute | solution.py:679
  28.8 19.2 %collective-permute-start.4 = (bf16[3,768]{1,0:T(4,128)(2,1)S(1)}, bf16[3,768]{1,0:T(4,128)(2,1)}, u32[]{:S(2)}, u32[]{:S(2)}) collective-permute-start(bf16[3,768]{1,0:T(4,128)(2,1)S(1)} %dynamic_update_slice.3), channel_id=1, source_target_pairs={{0,1},{1,0},{2,3},{3,2},{4,5},{5,4},{6,7},{7,6},{8,9},{9,8},{10,11... | collective-permute-start | bytes 13832 | tf_op jit(solution)/shard_map/ppermute | solution.py:665
  36.7 11.4 %collective-permute-start.5 = (bf16[3,768]{1,0:T(4,128)(2,1)S(1)}, bf16[3,768]{1,0:T(4,128)(2,1)}, u32[]{:S(2)}, u32[]{:S(2)}) collective-permute-start(bf16[3,768]{1,0:T(4,128)(2,1)S(1)} %dynamic_update_slice.3), channel_id=1, source_target_pairs={{0,2},{1,3},{2,0},{3,1},{4,6},{5,7},{6,4},{7,5},{8,10},{9,11},{10,... | collective-permute-start | bytes 13832 | tf_op jit(solution)/shard_map/ppermute | solution.py:665
  36.7 11.4 %collective-permute-start.6 = (bf16[3,768]{1,0:T(4,128)(2,1)S(1)}, bf16[3,768]{1,0:T(4,128)(2,1)}, u32[]{:S(2)}, u32[]{:S(2)}) collective-permute-start(bf16[3,768]{1,0:T(4,128)(2,1)S(1)} %dynamic_update_slice.3), channel_id=1, source_target_pairs={{0,3},{1,2},{2,1},{3,0},{4,7},{5,6},{6,5},{7,4},{8,11},{9,10},{10,... | collective-permute-start | bytes 13832 | tf_op jit(solution)/shard_map/ppermute | solution.py:665
  48.1 15.6 %collective-permute-start.8 = (bf16[216,768]{1,0:T(8,128)(2,1)S(1)}, bf16[216,768]{1,0:T(8,128)(2,1)S(1)}, u32[]{:S(2)}, u32[]{:S(2)}) collective-permute-start(bf16[216,768]{1,0:T(8,128)(2,1)S(1)} %pad_maximum_fusion.1), channel_id=1, source_target_pairs={{0,2},{1,3},{2,0},{3,1},{4,6},{5,7},{6,4},{7,5},{8,10},{9,11},{10,... | collective-permute-start | bytes 995336 | tf_op jit(solution)/shard_map/ppermute | solution.py:665
  48.5 16.6 %collective-permute-start.9 = (bf16[24,768]{1,0:T(8,128)(2,1)S(1)}, bf16[24,768]{1,0:T(8,128)(2,1)S(1)}, u32[]{:S(2)}, u32[]{:S(2)}) collective-permute-start(bf16[24,768]{1,0:T(8,128)(2,1)S(1)} %constant_dynamic-slice_fusion), channel_id=1, source_target_pairs={{0,1},{1,0},{2,3},{3,2},{4,5},{5,4},{6,7},{7,6},{8,9},{9,8},{10,11... | collective-permute-start | bytes 110600 | tf_op jit(solution)/shard_map/ppermute | solution.py:665
  50.3 16.1 %collective-permute-start.10 = (bf16[24,768]{1,0:T(8,128)(2,1)S(1)}, bf16[24,768]{1,0:T(8,128)(2,1)S(1)}, u32[]{:S(2)}, u32[]{:S(2)}) collective-permute-start(bf16[24,768]{1,0:T(8,128)(2,1)S(1)} %constant_dynamic-slice_fusion), channel_id=1, source_target_pairs={{0,3},{1,2},{2,1},{3,0},{4,7},{5,6},{6,5},{7,4},{8,11},{9,10},{10,... | collective-permute-start | bytes 110600 | tf_op jit(solution)/shard_map/ppermute | solution.py:665
  52.6 21.4 %collective-permute-start.7 = (bf16[3,128,768]{2,1,0:T(8,128)(2,1)}, bf16[3,128,768]{2,1,0:T(8,128)(2,1)}, u32[]{:S(2)}, u32[]{:S(2)}) collective-permute-start(bf16[3,128,768]{2,1,0:T(8,128)(2,1)} %collective-permute-done.2.far_low_ref), channel_id=1, source_target_pairs={{1,0},{2,3},{5,4},{6,7},{9,8},{10,11},{13,12},{14,15},{17,16},{18,... | collective-permute-start | bytes 1769480 | tf_op jit(solution)/shard_map/ppermute | solution.py:681
  74.0 92.0 %all-gather.10.cloned.1.call-start = ((), (), s32[]{:S(2)}) async-start(), calls=%async_computation.6 | async-start | bytes 3981312 | tf_op jit(solution)/shard_map/all_gather | solution.py:748
  76.6 18.3 %collective-permute-start.12 = (bf16[72,768]{1,0:T(8,128)(2,1)S(1)}, bf16[72,768]{1,0:T(8,128)(2,1)S(1)}, u32[]{:S(2)}, u32[]{:S(2)}) collective-permute-start(bf16[72,768]{1,0:T(8,128)(2,1)S(1)} %fusion.3), channel_id=1, source_target_pairs={{0,1},{1,0},{2,3},{3,2},{4,5},{5,4},{6,7},{7,6},{8,9},{9,8},{10,11... | collective-permute-start | bytes 331784 | tf_op jit(solution)/shard_map/ppermute | solution.py:665
  76.6 18.3 %collective-permute-start.13 = (bf16[72,768]{1,0:T(8,128)(2,1)S(1)}, bf16[72,768]{1,0:T(8,128)(2,1)S(1)}, u32[]{:S(2)}, u32[]{:S(2)}) collective-permute-start(bf16[72,768]{1,0:T(8,128)(2,1)S(1)} %fusion.3), channel_id=1, source_target_pairs={{0,2},{1,3},{2,0},{3,1},{4,6},{5,7},{6,4},{7,5},{8,10},{9,11},{10,... | collective-permute-start | bytes 331784 | tf_op jit(solution)/shard_map/ppermute | solution.py:665
  78.9 16.0 %collective-permute-start.14 = (bf16[72,768]{1,0:T(8,128)(2,1)S(1)}, bf16[72,768]{1,0:T(8,128)(2,1)S(1)}, u32[]{:S(2)}, u32[]{:S(2)}) collective-permute-start(bf16[72,768]{1,0:T(8,128)(2,1)S(1)} %fusion.3), channel_id=1, source_target_pairs={{0,3},{1,2},{2,1},{3,0},{4,7},{5,6},{6,5},{7,4},{8,11},{9,10},{10,... | collective-permute-start | bytes 331784 | tf_op jit(solution)/shard_map/ppermute | solution.py:665
  81.0 16.7 %collective-permute-start.11 = (bf16[384,768]{1,0:T(8,128)(2,1)S(1)}, bf16[384,768]{1,0:T(8,128)(2,1)}, u32[]{:S(2)}, u32[]{:S(2)}) collective-permute-start(bf16[384,768]{1,0:T(8,128)(2,1)S(1)} %bitcast.60), channel_id=1, source_target_pairs={{0,1},{1,0},{2,3},{3,2},{4,5},{5,4},{6,7},{7,6},{8,9},{9,8},{10,11... | collective-permute-start | bytes 1769480 | tf_op jit(solution)/shard_map/ppermute | solution.py:665
  97.7 136.4 %reduce-scatter.5.cloned.1.call-start = ((), (), s32[]{:S(2)}) async-start(), calls=%async_computation.3 | async-start | bytes 5308416 | tf_op jit(solution)/shard_map/reduce_scatter | solution.py:821
  97.9 11.2 %collective-permute-start.15 = (bf16[3,192,128]{2,1,0:T(8,128)(2,1)S(1)}, bf16[3,192,128]{2,1,0:T(8,128)(2,1)S(1)}, u32[]{:S(2)}, u32[]{:S(2)}) collective-permute-start(bf16[3,192,128]{2,1,0:T(8,128)(2,1)S(1)} %copy-done.23), channel_id=1, source_target_pairs={{0,1},{1,0},{2,3},{3,2},{4,5},{5,4},{6,7},{7,6},{8,9},{9,8},{10,11... | collective-permute-start | bytes 442376 | tf_op jit(solution)/shard_map/ppermute | solution.py:665
  98.1 13.7 %collective-permute-start.16 = (bf16[3,192,128]{2,1,0:T(8,128)(2,1)S(1)}, bf16[3,192,128]{2,1,0:T(8,128)(2,1)}, u32[]{:S(2)}, u32[]{:S(2)}) collective-permute-start(bf16[3,192,128]{2,1,0:T(8,128)(2,1)S(1)} %get-tuple-element.92), channel_id=1, source_target_pairs={{0,2},{1,3},{2,0},{3,1},{4,6},{5,7},{6,4},{7,5},{8,10},{9,11},{10,... | collective-permute-start | bytes 442376 | tf_op jit(solution)/shard_map/ppermute | solution.py:665
  100.3 11.5 %collective-permute-start.17 = (bf16[3,192,128]{2,1,0:T(8,128)(2,1)S(1)}, bf16[3,192,128]{2,1,0:T(8,128)(2,1)}, u32[]{:S(2)}, u32[]{:S(2)}) collective-permute-start(bf16[3,192,128]{2,1,0:T(8,128)(2,1)S(1)} %get-tuple-element.93), channel_id=1, source_target_pairs={{0,3},{1,2},{2,1},{3,0},{4,7},{5,6},{6,5},{7,4},{8,11},{9,10},{10,... | collective-permute-start | bytes 442376 | tf_op jit(solution)/shard_map/ppermute | solution.py:665
  115.3 14.2 %collective-permute-start.18 = (bf16[384,768]{1,0:T(8,128)(2,1)S(1)}, bf16[384,768]{1,0:T(8,128)(2,1)S(1)}, u32[]{:S(2)}, u32[]{:S(2)}) collective-permute-start(bf16[384,768]{1,0:T(8,128)(2,1)S(1)} %bitcast.72), channel_id=1, source_target_pairs={{0,1},{1,0},{2,3},{3,2},{4,5},{5,4},{6,7},{7,6},{8,9},{9,8},{10,11... | collective-permute-start | bytes 1769480 | tf_op jit(solution)/shard_map/ppermute | solution.py:665
  142.4 104.3 %reduce-scatter.3.cloned.1.call-start = ((), (), s32[]{:S(2)}) async-start(), calls=%async_computation.2 | async-start | bytes 2433024 | tf_op jit(solution)/shard_map/reduce_scatter | solution.py:861
  142.7 13.3 %collective-permute-start.19 = (bf16[384,768]{1,0:T(8,128)(2,1)}, bf16[384,768]{1,0:T(8,128)(2,1)S(1)}, u32[]{:S(2)}, u32[]{:S(2)}) collective-permute-start(bf16[384,768]{1,0:T(8,128)(2,1)} %get-tuple-element.97), channel_id=1, source_target_pairs={{0,1},{1,0},{2,3},{3,2},{4,5},{5,4},{6,7},{7,6},{8,9},{9,8},{10,11... | collective-permute-start | bytes 1769480 | tf_op jit(solution)/shard_map/ppermute | solution.py:665
  165.5 11.0 %collective-permute-start.21 = (bf16[3,192,128]{2,1,0:T(8,128)(2,1)}, bf16[3,192,128]{2,1,0:T(8,128)(2,1)}, u32[]{:S(2)}, u32[]{:S(2)}) collective-permute-start(bf16[3,192,128]{2,1,0:T(8,128)(2,1)} %get-tuple-element.109), channel_id=1, source_target_pairs={{0,2},{1,3},{2,0},{3,1},{4,6},{5,7},{6,4},{7,5},{8,10},{9,11},{10,... | collective-permute-start | bytes 442376 | tf_op jit(solution)/shard_map/ppermute | solution.py:665
  170.6 33.7 %collective-permute-start.23 = (bf16[384,768]{1,0:T(8,128)(2,1)}, bf16[384,768]{1,0:T(8,128)(2,1)}, u32[]{:S(2)}, u32[]{:S(2)}) collective-permute-start(bf16[384,768]{1,0:T(8,128)(2,1)} %get-tuple-element.120), channel_id=1, source_target_pairs={{0,1},{1,0},{2,3},{3,2},{4,5},{5,4},{6,7},{7,6},{8,9},{9,8},{10,11... | collective-permute-start | bytes 1769480 | tf_op jit(solution)/shard_map/ppermute | solution.py:665
  191.4 19.6 %collective-permute-start.25 = (bf16[3,576,128]{2,1,0:T(8,128)(2,1)}, bf16[3,576,128]{2,1,0:T(8,128)(2,1)}, u32[]{:S(2)}, u32[]{:S(2)}) collective-permute-start(bf16[3,576,128]{2,1,0:T(8,128)(2,1)} %get-tuple-element.115.refs_1_), channel_id=1, source_target_pairs={{0,1},{1,0},{2,3},{3,2},{4,5},{5,4},{6,7},{7,6},{8,9},{9,8},{10,11... | collective-permute-start | bytes 1327112 | tf_op jit(solution)/shard_map/ppermute | solution.py:665
  192.5 33.3 %collective-permute-start.26 = (bf16[3,576,128]{2,1,0:T(8,128)(2,1)}, bf16[3,576,128]{2,1,0:T(8,128)(2,1)}, u32[]{:S(2)}, u32[]{:S(2)}) collective-permute-start(bf16[3,576,128]{2,1,0:T(8,128)(2,1)} %get-tuple-element.116.refs_2_), channel_id=1, source_target_pairs={{0,2},{1,3},{2,0},{3,1},{4,6},{5,7},{6,4},{7,5},{8,10},{9,11},{10,... | collective-permute-start | bytes 1327112 | tf_op jit(solution)/shard_map/ppermute | solution.py:665
  194.9 30.9 %collective-permute-start.27 = (bf16[3,576,128]{2,1,0:T(8,128)(2,1)}, bf16[3,576,128]{2,1,0:T(8,128)(2,1)}, u32[]{:S(2)}, u32[]{:S(2)}) collective-permute-start(bf16[3,576,128]{2,1,0:T(8,128)(2,1)} %get-tuple-element.117.refs_3_), channel_id=1, source_target_pairs={{0,3},{1,2},{2,1},{3,0},{4,7},{5,6},{6,5},{7,4},{8,11},{9,10},{10,... | collective-permute-start | bytes 1327112 | tf_op jit(solution)/shard_map/ppermute | solution.py:665
  204.0 90.6 %all-gather.6.cloned.1.call-start = ((), (), s32[]{:S(2)}) async-start(), calls=%async_computation.4 | async-start | bytes 2654208 | tf_op jit(solution)/shard_map/all_gather | solution.py:866
  235.1 15.2 %collective-permute-start.24 = (bf16[192,768]{1,0:T(8,128)(2,1)S(1)}, bf16[192,768]{1,0:T(8,128)(2,1)S(1)}, u32[]{:S(2)}, u32[]{:S(2)}) collective-permute-start(bf16[192,768]{1,0:T(8,128)(2,1)S(1)} %slice.102), channel_id=1, source_target_pairs={{0,2},{1,3},{2,0},{3,1},{4,6},{5,7},{6,4},{7,5},{8,10},{9,11},{10,... | collective-permute-start | bytes 884744 | tf_op jit(solution)/shard_map/ppermute | solution.py:665
  266.7 13.9 %collective-permute-start.35 = (bf16[2,104,768]{2,1,0:T(8,128)(2,1)S(1)}, bf16[2,104,768]{2,1,0:T(8,128)(2,1)S(1)}, u32[]{:S(2)}, u32[]{:S(2)}) collective-permute-start(bf16[2,104,768]{2,1,0:T(8,128)(2,1)S(1)} %maximum_select_fusion.2), channel_id=1, source_target_pairs={{0,8},{4,12},{8,0},{12,4},{16,24},{20,28},{24,16},{28,20},{1,9},{5... | collective-permute-start | bytes 958472 | tf_op jit(solution)/shard_map/ppermute | solution.py:687
  (69 other events, 732.9 us)
Sparse Core Ops, SparseCore 0:
  74.2 33.4 all-gather.7
  109.5 33.9 all-gather.9
  147.0 53.8 reduce-scatter.4
  205.0 41.6 reduce-scatter.2
  251.2 31.9 all-gather.5

commit v3 on v2

--- a/solution.py
+++ b/solution.py
@@ -186,7 +186,7 @@
     me = place_ref[0]
     inner = joint_ref.shape[1] // 3
     head_size = inner // heads
-    count = 2
+    count = parts
 
     row, at = turn()
     out = at(normed_ref)
@@ -199,24 +199,25 @@
             ref[...], normed_ref[out], 1, 1
         ).astype(BF16)
     valid = chunk_valid(length_ref[row], me, parts, size, count)
-    for head in range(heads):
-        low = head * head_size
-        key = joint_ref[out, inner + low : inner + low + head_size, :]
-        value = joint_ref[out, 2 * inner + low : 2 * inner + low + head_size, :]
-        for first in range(0, parts, count):
-            lanes = slice(first * size, (first + count) * size)
-            query = joint_ref[out, low : low + head_size, lanes]
-            scores = dot(key, query, 0, 0) + chunk_bias(bias_ref, head, me, parts, first, count)
-            scores = jnp.where(valid, scores, NEG)
-            peak = jnp.max(scores, axis=0, keepdims=True)
-            raised = jnp.exp(scores - peak)
-            total = jnp.sum(raised, axis=0, keepdims=True)
-            mixed = (dot(value, raised.astype(BF16), 1, 0) / total).astype(BF16)
-            for step in range(count):
-                mixed_refs[first + step][row, low : low + head_size, :] = mixed[
-                    :, step * size : (step + 1) * size
-                ]
-            log_ref[out, head : head + 1, lanes] = peak + jnp.log(total)
+    spans = [slice(head * head_size, (head + 1) * head_size) for head in range(heads)]
+    scores = [
+        dot(joint_ref[out, inner + span.start : inner + span.stop, :], joint_ref[out, span, :], 0, 0)
+        for span in spans
+    ]
+    for head, span in enumerate(spans):
+        biased = scores[head] + chunk_bias(bias_ref, head, me, parts, 0, parts)
+        biased = jnp.where(valid, biased, NEG)
+        peak = jnp.max(biased, axis=0, keepdims=True)
+        raised = jnp.exp(biased - peak)
+        total = jnp.sum(raised, axis=0, keepdims=True)
+        scores[head] = (raised.astype(BF16), total)
+        log_ref[out, head : head + 1, :] = peak + jnp.log(total)
+    for head, span in enumerate(spans):
+        raised, total = scores[head]
+        value = joint_ref[out, 2 * inner + span.start : 2 * inner + span.stop, :]
+        mixed = (dot(value, raised, 1, 0) / total).astype(BF16)
+        for step in range(parts):
+            mixed_refs[step][row, span, :] = mixed[:, step * size : (step + 1) * size]
 
 
 def attend(place, lengths, blocks, weights, bias, heads):
@@ -375,7 +376,7 @@
     me = place_ref[0]
     inner = joint_ref.shape[1] // 3
     head_size = inner // heads
-    count = 2
+    count = parts
     row, at = turn()
     come = at(joint_ref)
 
@@ -604,13 +605,13 @@
         rows,
         [],
         [
-            (normed, "h"),
+            normed,
             *weights,
             gain,
             (gain_two_grad, "w"),
             (table_grad, "w"),
             (grad_branch, "h"),
-            (mixed, "h"),
+            mixed,
             *joint_grads,
         ],
         [((cuts, length, width), BF16, "w")],

time: 306 us -> 305 us (level)
  Pallas kernels: 66.4 us -> 60.9 us
  waiting for transfers between devices: 119 us -> 123 us
    pallas_call x10, Pallas kernels: 59.8 us -> 54.2 us  [call(): pl.pallas_call(kernel, grid=(rows,), in_specs=[SCALARS] * len(scalars) +...]
  transfers between devices with their start and end apart: 42 -> 42, of which waited for: 22 -> 21; matrix products, arithmetic and copies ran while one was open for 7% -> 7% of each run, Pallas kernels for 22% -> 20%
where the time goes in v3:
time: 305 us; the launch traced here: 304 us
  waiting for transfers between devices  123 us (40%)
  starting transfers between devices  68.3 us (22%)
  Pallas kernels  60.9 us (20%)
  local copies, waits for them, and re-layouts  28.7 us (9%)
  between operations  14.6 us (5%)
  other arithmetic  8.63 us (3%)
    ppermute x30, waiting for transfers between devices, swap(): return lax.ppermute(values, 'tp', [(i, i ^ distance) for i in range(parts)])  87.7 us
    ppermute x30, starting transfers between devices, swap(): return lax.ppermute(values, 'tp', [(i, i ^ distance) for i in range(parts)])  59.1 us
    pallas_call x10, Pallas kernels, call(): pl.pallas_call(kernel, grid=(rows,), in_specs=[SCALARS] * len(scalars) +...  54.2 us
    ppermute x3, waiting for transfers between devices, across(): return lax.ppermute(values, 'dp', [(i, i ^ 1 << bit) for i in range(count)])  17.6 us
    unnamed x120, local copies, waits for them, and re-layouts  12.1 us
    ppermute x1, waiting for transfers between devices, gather_line(): last_high = lax.ppermute(far_low, 'tp', outer)  7.06 us
    pallas_call x1, Pallas kernels, ffn_grad(): pl.pallas_call(ffn_grad_kernel, grid=(steps,), in_specs=[WIDE] * len(arra...  6.62 us
  transfers between devices with their start and end apart: 42, of which 21 were waited for; matrix products, arithmetic and copies ran while one was open for 7% of the time, Pallas kernels for 20%

profile of v3, /device:TPU:0, one launch (start us, length us, event | category | flops | bytes accessed | tf_op | source)
XLA Modules:
  0.0 304.4 jit_solution(15543968287087171197)
XLA Ops:
  9.3 3.1 %collective-permute-start = (bf16[3,128,768]{2,1,0:T(8,128)(2,1)S(1)}, bf16[3,128,768]{2,1,0:T(8,128)(2,1)}, u32[]{:S(2)}, u32[]{:S(2)}) collective-permute-start(bf16[3,128,768]{2,1,0:T(8,128)(2,1)S(1)} %norm_one.1.own_ref), channel_id=1, source_target_pairs={{0,1},{1,0},{2,3},{3,2},{4,5},{5,4},{6,7},{7,6},{8,9},{9,8},{10,11... | collective-permute-start | bytes 1769480 | tf_op jit(solution)/shard_map/ppermute | solution.py:666
  13.9 2.5 bias_blocks.1.bias_ref
  16.4 9.4 %collective-permute-done.pair_ref = bf16[3,128,768]{2,1,0:T(8,128)(2,1)} collective-permute-done((bf16[3,128,768]{2,1,0:T(8,128)(2,1)S(1)}, bf16[3,128,768]{2,1,0:T(8,128)(2,1)}, u32[]{:S(2)}, u32[]{:S(2)}) %collective-permute-start) | collective-permute-done | bytes 589856 | tf_op jit(solution)/shard_map/ppermute | solution.py:666
  28.8 7.9 %collective-permute-start.4 = (bf16[3,768]{1,0:T(4,128)(2,1)S(1)}, bf16[3,768]{1,0:T(4,128)(2,1)}, u32[]{:S(2)}, u32[]{:S(2)}) collective-permute-start(bf16[3,768]{1,0:T(4,128)(2,1)S(1)} %dynamic_update_slice.3), channel_id=1, source_target_pairs={{0,1},{1,0},{2,3},{3,2},{4,5},{5,4},{6,7},{7,6},{8,9},{9,8},{10,11... | collective-permute-start | bytes 13832 | tf_op jit(solution)/shard_map/ppermute | solution.py:666
  39.5 8.6 %collective-permute-done.4 = bf16[3,768]{1,0:T(4,128)(2,1)} collective-permute-done((bf16[3,768]{1,0:T(4,128)(2,1)S(1)}, bf16[3,768]{1,0:T(4,128)(2,1)}, u32[]{:S(2)}, u32[]{:S(2)}) %collective-permute-start.4) | collective-permute-done | bytes 4640 | tf_op jit(solution)/shard_map/ppermute | solution.py:666
  53.9 9.9 %collective-permute-done.8 = bf16[216,768]{1,0:T(8,128)(2,1)S(1)} collective-permute-done((bf16[216,768]{1,0:T(8,128)(2,1)S(1)}, bf16[216,768]{1,0:T(8,128)(2,1)S(1)}, u32[]{:S(2)}, u32[]{:S(2)}) %collective-permute-start.8) | collective-permute-done | bytes 331808 | tf_op jit(solution)/shard_map/ppermute | solution.py:666
  67.0 7.1 %collective-permute-done.7.last_high_ref = bf16[3,128,768]{2,1,0:T(8,128)(2,1)} collective-permute-done((bf16[3,128,768]{2,1,0:T(8,128)(2,1)}, bf16[3,128,768]{2,1,0:T(8,128)(2,1)}, u32[]{:S(2)}, u32[]{:S(2)}) %collective-permute-start.7) | collective-permute-done | bytes 589856 | tf_op jit(solution)/shard_map/ppermute | solution.py:682
  81.0 9.4 %attend.1 = (bf16[3,512,768]{2,1,0:T(8,128)(2,1)}, bf16[3,576,512]{2,1,0:T(8,128)(2,1)}, f32[3,3,512]{2,1,0:T(4,128)}, bf16[3,192,128]{2,1,0:T(8,128)(2,1)S(1)},...) custom-call(s32[1]{0:T(128)} %bitcast.place_ref, ...), custom_call_target="tpu_custom_call" | custom-call | flops 13200000000 | bytes 12000000 | tf_op jit(solution)/shard_map/attend/pallas_call | solution.py:81
  92.6 5.0 %collective-permute-done.11.grad_ref.grad_pair_ref = bf16[384,768]{1,0:T(8,128)(2,1)} collective-permute-done((bf16[384,768]{1,0:T(8,128)(2,1)S(1)}, bf16[384,768]{1,0:T(8,128)(2,1)}, u32[]{:S(2)}, u32[]{:S(2)}) %collective-permute-start.11) | collective-permute-done | bytes 589856 | tf_op jit(solution)/shard_map/ppermute | solution.py:666
  102.4 5.2 %all-gather.8.cloned.1.call-done = bf16[2304,768]{1,0:T(8,128)(2,1)} async-done(((bf16[288,768]{1,0:T(8,128)(2,1)}), bf16[2304,768]{1,0:T(8,128)(2,1)}) %all-gather.8.cloned.1.call-update) | async-done | bytes 3538960 | tf_op jit(solution)/shard_map/all_gather | solution.py:749
  109.1 2.7 collective-permute-done.16.refs_2_
  111.8 3.5 %middle_of.1 = (f32[3,128,768]{2,1,0:T(8,128)}, bf16[3,128,768]{2,1,0:T(8,128)(2,1)S(1)}, bf16[3,768,128]{2,1,0:T(8,128)(2,1)}) custom-call(bf16[768,768]{1,0:T(8,128)(2,1)S(1)} %bitcast.54, bf16[3,128,768]{2,1,0:T(8,128)(2,1)S(1)} %copy-done.18, f32[1,768]{1,0:T(1,128)S(1)} %reshape.280.gain_ref, bf16[3,192,128]{2,1,0:T(8,128)(2,1)S(1)} %copy-done.34, ...), custom_call_target="tpu_custom_call" | custom-call | flops 3300000000 | bytes 3000000 | tf_op jit(solution)/shard_map/middle_of/pallas_call | solution.py:81
  117.6 5.0 %feed_forward.2 = (bf16[2,384,768]{2,1,0:T(8,128)(2,1)S(1)}, bf16[2,384,768]{2,1,0:T(8,128)(2,1)S(1)}, bf16[384,768]{1,0:T(8,128)(2,1)}, bf16[384,768]{1,0:T(8,128)(2,1)}) custom-call(bf16[384,768]{1,0:T(8,128)(2,1)S(1)} %bitcast.73, bf16[384,768]{1,0:T(8,128)(2,1)S(1)} %bitcast.61, bf16[768,768]{1,0:T(8,128)(2,1)S(1)} %copy-done.3, ...), custom_call_target="tpu_custom_call" | custom-call | flops 6600000000 | bytes 6000000 | tf_op jit(solution)/shard_map/feed_forward/pallas_call | solution.py:81
  122.6 6.9 %collective-permute-done.18.normed_ref.normed_pair_ref = bf16[384,768]{1,0:T(8,128)(2,1)S(1)} collective-permute-done((bf16[384,768]{1,0:T(8,128)(2,1)S(1)}, bf16[384,768]{1,0:T(8,128)(2,1)S(1)}, u32[]{:S(2)}, u32[]{:S(2)}) %collective-permute-start.18) | collective-permute-done | bytes 589856 | tf_op jit(solution)/shard_map/ppermute | solution.py:666
  129.5 6.3 %feed_forward.3 = (bf16[2,384,768]{2,1,0:T(8,128)(2,1)S(1)}, bf16[2,384,768]{2,1,0:T(8,128)(2,1)S(1)}, bf16[384,768]{1,0:T(8,128)(2,1)}, bf16[384,768]{1,0:T(8,128)(2,1)}) custom-call(bf16[384,768]{1,0:T(8,128)(2,1)S(1)} %collective-permute-done.18.normed_ref.normed_pair_ref, bf16[384,768]{1,0:T(8,128)(2,1)} %collective-permute-done.11.grad_ref.grad_pair_ref, ...), custom_call_target="tpu_custom_call" | custom-call | flops 6600000000 | bytes 6000000 | tf_op jit(solution)/shard_map/feed_forward/pallas_call | solution.py:81
  135.8 6.6 %ffn_grad.1 = bf16[2,4,384,768]{3,2,1,0:T(8,128)(2,1)} custom-call(bf16[384,768]{1,0:T(8,128)(2,1)S(1)} %bitcast.74, bf16[384,768]{1,0:T(8,128)(2,1)S(1)} %collective-permute-done.18.normed_ref.normed_pair_ref, bf16[384,768]{1,0:T(8,128)(2,1)S(1)} %bitcast.62, bf16[384,768]{1,0:T(8,128)(2,1)} %collective-permute-done.11.grad_ref.grad_pair_ref, ...), custom_call_target="tpu_custom_call" | custom-call | flops 6600000000 | bytes 6000000 | tf_op jit(solution)/shard_map/ffn_grad/pallas_call | solution.py:508
  144.4 11.5 %collective-permute-done.19 = bf16[384,768]{1,0:T(8,128)(2,1)S(1)} collective-permute-done((bf16[384,768]{1,0:T(8,128)(2,1)}, bf16[384,768]{1,0:T(8,128)(2,1)S(1)}, u32[]{:S(2)}, u32[]{:S(2)}) %collective-permute-start.19) | collective-permute-done | bytes 589856 | tf_op jit(solution)/shard_map/ppermute | solution.py:666
  157.1 3.1 %middle_back.1 = (f32[3,128,768]{2,1,0:T(8,128)}, bf16[3,128,768]{2,1,0:T(8,128)(2,1)}, f32[1,768]{1,0:T(1,128)}, bf16[3,192,128]{2,1,0:T(8,128)(2,1)S(1)}, bf16...) custom-call(bf16[768,768]{1,0:T(8,128)(2,1)S(1)} %bitcast.55, ...), custom_call_target="tpu_custom_call" | custom-call | flops 4400000000 | bytes 4000000 | tf_op jit(solution)/shard_map/middle_back/pallas_call | solution.py:81
  160.8 4.6 %collective-permute-start.22 = (bf16[3,192,128]{2,1,0:T(8,128)(2,1)}, bf16[3,192,128]{2,1,0:T(8,128)(2,1)}, u32[]{:S(2)}, u32[]{:S(2)}) collective-permute-start(bf16[3,192,128]{2,1,0:T(8,128)(2,1)} %get-tuple-element.110), channel_id=1, source_target_pairs={{0,3},{1,2},{2,1},{3,0},{4,7},{5,6},{6,5},{7,4},{8,11},{9,10},{10,... | collective-permute-start | bytes 442376 | tf_op jit(solution)/shard_map/ppermute | solution.py:666
  170.6 3.1 %collective-permute-start.23 = (bf16[384,768]{1,0:T(8,128)(2,1)}, bf16[384,768]{1,0:T(8,128)(2,1)}, u32[]{:S(2)}, u32[]{:S(2)}) collective-permute-start(bf16[384,768]{1,0:T(8,128)(2,1)} %get-tuple-element.120), channel_id=1, source_target_pairs={{0,1},{1,0},{2,3},{3,2},{4,5},{5,4},{6,7},{7,6},{8,9},{9,8},{10,11... | collective-permute-start | bytes 1769480 | tf_op jit(solution)/shard_map/ppermute | solution.py:666
  176.5 12.5 %attend_back.1 = (bf16[3,576,128]{2,1,0:T(8,128)(2,1)S(1)}, bf16[3,576,128]{2,1,0:T(8,128)(2,1)}, bf16[3,576,128]{2,1,0:T(8,128)(2,1)}, bf16[3,576,128]{2,1,0:T(8,128)(2,1)}, f32[3,8,128]{2,1,0:T(8,128)}) custom-call(s32[1]{0:T(128)} %bitcast.place_ref, s32[3]{0:T(128)S(1)} %copy-done.16, bf16[3,576,512]{2,1,0:T(8,128)(2,1)S(1)} %copy-done.37, ...), custom_call_target="tpu_custom_call" | custom-call | flops 15399999488 | bytes 14000000 | tf_op jit(solution)/shard_map/attend_back/pallas_call | solution.py:81
  194.6 6.9 %joint_grad.1 = bf16[8,176,768]{2,1,0:T(8,128)(2,1)} custom-call(bf16[3,512,768]{2,1,0:T(8,128)(2,1)S(1)} %copy-done.27, bf16[192,768]{1,0:T(8,128)(2,1)S(1)} %bitcast.65, bf16[192,768]{1,0:T(8,128)(2,1)S(1)} %bitcast.68, bf16[192,768]{1,0:T(8,128)(2,1)S(1)} %bitcast.71, f32[1,768]{1,0:T(1,128)S(1)} %reshape.278.gain_ref, f32[1,768]{1,0:T(1,128)S(1)} %copy-done.39, ...), custom_call_target="tpu_custom_call" | custom-call | flops 6600000000 | bytes 6000000 | tf_op jit(solution)/shard_map/joint_grad/pallas_call | solution.py:81
  201.6 7.0 %collective-permute-done.25.refs_1_ = bf16[3,576,128]{2,1,0:T(8,128)(2,1)} collective-permute-done((bf16[3,576,128]{2,1,0:T(8,128)(2,1)}, bf16[3,576,128]{2,1,0:T(8,128)(2,1)}, u32[]{:S(2)}, u32[]{:S(2)}) %collective-permute-start.25) | collective-permute-done | bytes 442400 | tf_op jit(solution)/shard_map/ppermute | solution.py:666
  208.6 14.8 %collective-permute-done.26.refs_2_ = bf16[3,576,128]{2,1,0:T(8,128)(2,1)} collective-permute-done((bf16[3,576,128]{2,1,0:T(8,128)(2,1)}, bf16[3,576,128]{2,1,0:T(8,128)(2,1)}, u32[]{:S(2)}, u32[]{:S(2)}) %collective-permute-start.26) | collective-permute-done | bytes 442400 | tf_op jit(solution)/shard_map/ppermute | solution.py:666
  226.8 4.8 %hidden_grad.1 = f32[3,128,768]{2,1,0:T(8,128)} custom-call(s32[1]{0:T(128)} %bitcast.place_ref, bf16[4,576,768]{2,1,0:T(8,128)(2,1)S(1)} %bitcast.53, f32[3,128,768]{2,1,0:T(8,128)S(1)} %copy-done.28, bf16[3,128,768]{2,1,0:T(8,128)(2,1)S(1)} %copy-done.19, f32[1,768]{1,0:T(1,128)S(1)} %reshape.278.gain_ref, bf16[3,576,128]{2,1,0:T(8,128)(2,1)S(1)} %copy-done.32, ...), custom_call_target="tpu_custom_call" | custom-call | flops 165000003584 | bytes 150000000 | tf_op jit(solution)/shard_map/hidden_grad/pallas_call | solution.py:81
  232.6 6.5 %collective-permute-start.24 = (bf16[192,768]{1,0:T(8,128)(2,1)S(1)}, bf16[192,768]{1,0:T(8,128)(2,1)S(1)}, u32[]{:S(2)}, u32[]{:S(2)}) collective-permute-start(bf16[192,768]{1,0:T(8,128)(2,1)S(1)} %slice.102), channel_id=1, source_target_pairs={{0,2},{1,3},{2,0},{3,1},{4,6},{5,7},{6,4},{7,5},{8,10},{9,11},{10,... | collective-permute-start | bytes 884744 | tf_op jit(solution)/shard_map/ppermute | solution.py:666
  241.0 5.6 %reduce-scatter.3.cloned.1.call-done = bf16[176,768]{1,0:T(8,128)(2,1)} async-done(((bf16[1408,768]{1,0:T(8,128)(2,1)}), bf16[176,768]{1,0:T(8,128)(2,1)}) %reduce-scatter.3.cloned.1.call-update) | async-done | bytes 270352 | tf_op jit(solution)/shard_map/reduce_scatter | solution.py:862
  253.6 2.9 collective-permute-done.32
  260.5 5.5 %collective-permute-done.34 = bf16[1,104,768]{2,1,0:T(8,128)(2,1)S(1)} collective-permute-done((bf16[1,104,768]{2,1,0:T(8,128)(2,1)S(1)}, bf16[1,104,768]{2,1,0:T(8,128)(2,1)S(1)}, u32[]{:S(2)}, u32[]{:S(2)}) %collective-permute-start.34) | collective-permute-done | bytes 159776 | tf_op jit(solution)/shard_map/ppermute | solution.py:688
  267.6 12.1 %collective-permute-done.35 = bf16[2,104,768]{2,1,0:T(8,128)(2,1)S(1)} collective-permute-done((bf16[2,104,768]{2,1,0:T(8,128)(2,1)S(1)}, bf16[2,104,768]{2,1,0:T(8,128)(2,1)S(1)}, u32[]{:S(2)}, u32[]{:S(2)}) %collective-permute-start.35) | collective-permute-done | bytes 319520 | tf_op jit(solution)/shard_map/ppermute | solution.py:688
  281.2 4.3 %collective-permute-start.30 = (f32[3,768]{1,0:T(4,128)S(1)}, f32[3,768]{1,0:T(4,128)S(1)}, u32[]{:S(2)}, u32[]{:S(2)}) collective-permute-start(f32[3,768]{1,0:T(4,128)S(1)} %broadcast_divide_fusion), channel_id=1, source_target_pairs={{0,3},{1,2},{2,1},{3,0},{4,7},{5,6},{6,5},{7,4},{8,11},{9,10},{10,... | collective-permute-start | bytes 27656 | tf_op jit(solution)/shard_map/ppermute | solution.py:666
  293.7 4.2 %fusion.8 = (f32[768,768]{1,0:T(8,128)}, f32[768,768]{1,0:T(8,128)}) fusion(bf16[1536,768]{1,0:T(8,128)(2,1)} %all-gather.6.cloned.1.call-done), kind=kLoop, calls=%fused_computation.55 | loop fusion | bytes 9437184 | tf_op jit(solution)/shard_map/slice | solution.py:918
  (238 shorter events, 81.4 us)
Async XLA Ops:
  7.2 100.4 %all-gather.8.cloned.1.call-start = ((), (), s32[]{:S(2)}) async-start(), calls=%async_computation.5 | async-start | bytes 3981312 | tf_op jit(solution)/shard_map/all_gather | solution.py:749
  9.3 16.5 %collective-permute-start = (bf16[3,128,768]{2,1,0:T(8,128)(2,1)S(1)}, bf16[3,128,768]{2,1,0:T(8,128)(2,1)}, u32[]{:S(2)}, u32[]{:S(2)}) collective-permute-start(bf16[3,128,768]{2,1,0:T(8,128)(2,1)S(1)} %norm_one.1.own_ref), channel_id=1, source_target_pairs={{0,1},{1,0},{2,3},{3,2},{4,5},{5,4},{6,7},{7,6},{8,9},{9,8},{10,11... | collective-permute-start | bytes 1769480 | tf_op jit(solution)/shard_map/ppermute | solution.py:666
  12.4 13.4 %collective-permute-start.1 = (bf16[3,128,768]{2,1,0:T(8,128)(2,1)S(1)}, bf16[3,128,768]{2,1,0:T(8,128)(2,1)}, u32[]{:S(2)}, u32[]{:S(2)}) collective-permute-start(bf16[3,128,768]{2,1,0:T(8,128)(2,1)S(1)} %norm_one.1.own_ref), channel_id=1, source_target_pairs={{1,2},{2,1},{5,6},{6,5},{9,10},{10,9},{13,14},{14,13},{17,18},{18,... | collective-permute-start | bytes 1769480 | tf_op jit(solution)/shard_map/ppermute | solution.py:677
  25.8 22.3 %collective-permute-start.2 = (bf16[3,128,768]{2,1,0:T(8,128)(2,1)}, bf16[3,128,768]{2,1,0:T(8,128)(2,1)}, u32[]{:S(2)}, u32[]{:S(2)}) collective-permute-start(bf16[3,128,768]{2,1,0:T(8,128)(2,1)} %collective-permute-done.pair_ref), channel_id=1, source_target_pairs={{1,2},{2,1},{5,6},{6,5},{9,10},{10,9},{13,14},{14,13},{17,18},{18,... | collective-permute-start | bytes 1769480 | tf_op jit(solution)/shard_map/ppermute | solution.py:679
  27.3 20.7 %collective-permute-start.3 = (bf16[3,128,768]{2,1,0:T(8,128)(2,1)}, bf16[3,128,768]{2,1,0:T(8,128)(2,1)}, u32[]{:S(2)}, u32[]{:S(2)}) collective-permute-start(bf16[3,128,768]{2,1,0:T(8,128)(2,1)} %collective-permute-done.1.last_low_ref), channel_id=1, source_target_pairs={{1,0},{2,3},{5,4},{6,7},{9,8},{10,11},{13,12},{14,15},{17,16},{18,... | collective-permute-start | bytes 1769480 | tf_op jit(solution)/shard_map/ppermute | solution.py:680
  28.8 19.2 %collective-permute-start.4 = (bf16[3,768]{1,0:T(4,128)(2,1)S(1)}, bf16[3,768]{1,0:T(4,128)(2,1)}, u32[]{:S(2)}, u32[]{:S(2)}) collective-permute-start(bf16[3,768]{1,0:T(4,128)(2,1)S(1)} %dynamic_update_slice.3), channel_id=1, source_target_pairs={{0,1},{1,0},{2,3},{3,2},{4,5},{5,4},{6,7},{7,6},{8,9},{9,8},{10,11... | collective-permute-start | bytes 13832 | tf_op jit(solution)/shard_map/ppermute | solution.py:666
  36.7 11.4 %collective-permute-start.5 = (bf16[3,768]{1,0:T(4,128)(2,1)S(1)}, bf16[3,768]{1,0:T(4,128)(2,1)}, u32[]{:S(2)}, u32[]{:S(2)}) collective-permute-start(bf16[3,768]{1,0:T(4,128)(2,1)S(1)} %dynamic_update_slice.3), channel_id=1, source_target_pairs={{0,2},{1,3},{2,0},{3,1},{4,6},{5,7},{6,4},{7,5},{8,10},{9,11},{10,... | collective-permute-start | bytes 13832 | tf_op jit(solution)/shard_map/ppermute | solution.py:666
  36.7 11.4 %collective-permute-start.6 = (bf16[3,768]{1,0:T(4,128)(2,1)S(1)}, bf16[3,768]{1,0:T(4,128)(2,1)}, u32[]{:S(2)}, u32[]{:S(2)}) collective-permute-start(bf16[3,768]{1,0:T(4,128)(2,1)S(1)} %dynamic_update_slice.3), channel_id=1, source_target_pairs={{0,3},{1,2},{2,1},{3,0},{4,7},{5,6},{6,5},{7,4},{8,11},{9,10},{10,... | collective-permute-start | bytes 13832 | tf_op jit(solution)/shard_map/ppermute | solution.py:666
  48.1 15.6 %collective-permute-start.8 = (bf16[216,768]{1,0:T(8,128)(2,1)S(1)}, bf16[216,768]{1,0:T(8,128)(2,1)S(1)}, u32[]{:S(2)}, u32[]{:S(2)}) collective-permute-start(bf16[216,768]{1,0:T(8,128)(2,1)S(1)} %pad_maximum_fusion.1), channel_id=1, source_target_pairs={{0,2},{1,3},{2,0},{3,1},{4,6},{5,7},{6,4},{7,5},{8,10},{9,11},{10,... | collective-permute-start | bytes 995336 | tf_op jit(solution)/shard_map/ppermute | solution.py:666
  48.5 16.6 %collective-permute-start.9 = (bf16[24,768]{1,0:T(8,128)(2,1)S(1)}, bf16[24,768]{1,0:T(8,128)(2,1)S(1)}, u32[]{:S(2)}, u32[]{:S(2)}) collective-permute-start(bf16[24,768]{1,0:T(8,128)(2,1)S(1)} %constant_dynamic-slice_fusion), channel_id=1, source_target_pairs={{0,1},{1,0},{2,3},{3,2},{4,5},{5,4},{6,7},{7,6},{8,9},{9,8},{10,11... | collective-permute-start | bytes 110600 | tf_op jit(solution)/shard_map/ppermute | solution.py:666
  50.3 16.1 %collective-permute-start.10 = (bf16[24,768]{1,0:T(8,128)(2,1)S(1)}, bf16[24,768]{1,0:T(8,128)(2,1)S(1)}, u32[]{:S(2)}, u32[]{:S(2)}) collective-permute-start(bf16[24,768]{1,0:T(8,128)(2,1)S(1)} %constant_dynamic-slice_fusion), channel_id=1, source_target_pairs={{0,3},{1,2},{2,1},{3,0},{4,7},{5,6},{6,5},{7,4},{8,11},{9,10},{10,... | collective-permute-start | bytes 110600 | tf_op jit(solution)/shard_map/ppermute | solution.py:666
  52.6 21.4 %collective-permute-start.7 = (bf16[3,128,768]{2,1,0:T(8,128)(2,1)}, bf16[3,128,768]{2,1,0:T(8,128)(2,1)}, u32[]{:S(2)}, u32[]{:S(2)}) collective-permute-start(bf16[3,128,768]{2,1,0:T(8,128)(2,1)} %collective-permute-done.2.far_low_ref), channel_id=1, source_target_pairs={{1,0},{2,3},{5,4},{6,7},{9,8},{10,11},{13,12},{14,15},{17,16},{18,... | collective-permute-start | bytes 1769480 | tf_op jit(solution)/shard_map/ppermute | solution.py:682
  74.0 91.9 %all-gather.10.cloned.1.call-start = ((), (), s32[]{:S(2)}) async-start(), calls=%async_computation.6 | async-start | bytes 3981312 | tf_op jit(solution)/shard_map/all_gather | solution.py:749
  76.6 15.2 %collective-permute-start.12 = (bf16[72,768]{1,0:T(8,128)(2,1)S(1)}, bf16[72,768]{1,0:T(8,128)(2,1)S(1)}, u32[]{:S(2)}, u32[]{:S(2)}) collective-permute-start(bf16[72,768]{1,0:T(8,128)(2,1)S(1)} %fusion.3), channel_id=1, source_target_pairs={{0,1},{1,0},{2,3},{3,2},{4,5},{5,4},{6,7},{7,6},{8,9},{9,8},{10,11... | collective-permute-start | bytes 331784 | tf_op jit(solution)/shard_map/ppermute | solution.py:666
  76.6 15.2 %collective-permute-start.13 = (bf16[72,768]{1,0:T(8,128)(2,1)S(1)}, bf16[72,768]{1,0:T(8,128)(2,1)S(1)}, u32[]{:S(2)}, u32[]{:S(2)}) collective-permute-start(bf16[72,768]{1,0:T(8,128)(2,1)S(1)} %fusion.3), channel_id=1, source_target_pairs={{0,2},{1,3},{2,0},{3,1},{4,6},{5,7},{6,4},{7,5},{8,10},{9,11},{10,... | collective-permute-start | bytes 331784 | tf_op jit(solution)/shard_map/ppermute | solution.py:666
  78.9 12.8 %collective-permute-start.14 = (bf16[72,768]{1,0:T(8,128)(2,1)S(1)}, bf16[72,768]{1,0:T(8,128)(2,1)S(1)}, u32[]{:S(2)}, u32[]{:S(2)}) collective-permute-start(bf16[72,768]{1,0:T(8,128)(2,1)S(1)} %fusion.3), channel_id=1, source_target_pairs={{0,3},{1,2},{2,1},{3,0},{4,7},{5,6},{6,5},{7,4},{8,11},{9,10},{10,... | collective-permute-start | bytes 331784 | tf_op jit(solution)/shard_map/ppermute | solution.py:666
  81.0 16.7 %collective-permute-start.11 = (bf16[384,768]{1,0:T(8,128)(2,1)S(1)}, bf16[384,768]{1,0:T(8,128)(2,1)}, u32[]{:S(2)}, u32[]{:S(2)}) collective-permute-start(bf16[384,768]{1,0:T(8,128)(2,1)S(1)} %bitcast.60), channel_id=1, source_target_pairs={{0,1},{1,0},{2,3},{3,2},{4,5},{5,4},{6,7},{7,6},{8,9},{9,8},{10,11... | collective-permute-start | bytes 1769480 | tf_op jit(solution)/shard_map/ppermute | solution.py:666
  97.7 133.9 %reduce-scatter.5.cloned.1.call-start = ((), (), s32[]{:S(2)}) async-start(), calls=%async_computation.3 | async-start | bytes 5308416 | tf_op jit(solution)/shard_map/reduce_scatter | solution.py:822
  97.9 11.2 %collective-permute-start.15 = (bf16[3,192,128]{2,1,0:T(8,128)(2,1)S(1)}, bf16[3,192,128]{2,1,0:T(8,128)(2,1)S(1)}, u32[]{:S(2)}, u32[]{:S(2)}) collective-permute-start(bf16[3,192,128]{2,1,0:T(8,128)(2,1)S(1)} %copy-done.23), channel_id=1, source_target_pairs={{0,1},{1,0},{2,3},{3,2},{4,5},{5,4},{6,7},{7,6},{8,9},{9,8},{10,11... | collective-permute-start | bytes 442376 | tf_op jit(solution)/shard_map/ppermute | solution.py:666
  98.0 13.8 %collective-permute-start.16 = (bf16[3,192,128]{2,1,0:T(8,128)(2,1)S(1)}, bf16[3,192,128]{2,1,0:T(8,128)(2,1)}, u32[]{:S(2)}, u32[]{:S(2)}) collective-permute-start(bf16[3,192,128]{2,1,0:T(8,128)(2,1)S(1)} %get-tuple-element.92), channel_id=1, source_target_pairs={{0,2},{1,3},{2,0},{3,1},{4,6},{5,7},{6,4},{7,5},{8,10},{9,11},{10,... | collective-permute-start | bytes 442376 | tf_op jit(solution)/shard_map/ppermute | solution.py:666
  100.3 11.4 %collective-permute-start.17 = (bf16[3,192,128]{2,1,0:T(8,128)(2,1)S(1)}, bf16[3,192,128]{2,1,0:T(8,128)(2,1)}, u32[]{:S(2)}, u32[]{:S(2)}) collective-permute-start(bf16[3,192,128]{2,1,0:T(8,128)(2,1)S(1)} %get-tuple-element.93), channel_id=1, source_target_pairs={{0,3},{1,2},{2,1},{3,0},{4,7},{5,6},{6,5},{7,4},{8,11},{9,10},{10,... | collective-permute-start | bytes 442376 | tf_op jit(solution)/shard_map/ppermute | solution.py:666
  115.3 14.2 %collective-permute-start.18 = (bf16[384,768]{1,0:T(8,128)(2,1)S(1)}, bf16[384,768]{1,0:T(8,128)(2,1)S(1)}, u32[]{:S(2)}, u32[]{:S(2)}) collective-permute-start(bf16[384,768]{1,0:T(8,128)(2,1)S(1)} %bitcast.72), channel_id=1, source_target_pairs={{0,1},{1,0},{2,3},{3,2},{4,5},{5,4},{6,7},{7,6},{8,9},{9,8},{10,11... | collective-permute-start | bytes 1769480 | tf_op jit(solution)/shard_map/ppermute | solution.py:666
  142.4 104.2 %reduce-scatter.3.cloned.1.call-start = ((), (), s32[]{:S(2)}) async-start(), calls=%async_computation.2 | async-start | bytes 2433024 | tf_op jit(solution)/shard_map/reduce_scatter | solution.py:862
  142.7 13.3 %collective-permute-start.19 = (bf16[384,768]{1,0:T(8,128)(2,1)}, bf16[384,768]{1,0:T(8,128)(2,1)S(1)}, u32[]{:S(2)}, u32[]{:S(2)}) collective-permute-start(bf16[384,768]{1,0:T(8,128)(2,1)} %get-tuple-element.97), channel_id=1, source_target_pairs={{0,1},{1,0},{2,3},{3,2},{4,5},{5,4},{6,7},{7,6},{8,9},{9,8},{10,11... | collective-permute-start | bytes 1769480 | tf_op jit(solution)/shard_map/ppermute | solution.py:666
  165.4 11.0 %collective-permute-start.21 = (bf16[3,192,128]{2,1,0:T(8,128)(2,1)}, bf16[3,192,128]{2,1,0:T(8,128)(2,1)}, u32[]{:S(2)}, u32[]{:S(2)}) collective-permute-start(bf16[3,192,128]{2,1,0:T(8,128)(2,1)} %get-tuple-element.109), channel_id=1, source_target_pairs={{0,2},{1,3},{2,0},{3,1},{4,6},{5,7},{6,4},{7,5},{8,10},{9,11},{10,... | collective-permute-start | bytes 442376 | tf_op jit(solution)/shard_map/ppermute | solution.py:666
  170.6 31.0 %collective-permute-start.23 = (bf16[384,768]{1,0:T(8,128)(2,1)}, bf16[384,768]{1,0:T(8,128)(2,1)}, u32[]{:S(2)}, u32[]{:S(2)}) collective-permute-start(bf16[384,768]{1,0:T(8,128)(2,1)} %get-tuple-element.120), channel_id=1, source_target_pairs={{0,1},{1,0},{2,3},{3,2},{4,5},{5,4},{6,7},{7,6},{8,9},{9,8},{10,11... | collective-permute-start | bytes 1769480 | tf_op jit(solution)/shard_map/ppermute | solution.py:666
  189.0 19.6 %collective-permute-start.25 = (bf16[3,576,128]{2,1,0:T(8,128)(2,1)}, bf16[3,576,128]{2,1,0:T(8,128)(2,1)}, u32[]{:S(2)}, u32[]{:S(2)}) collective-permute-start(bf16[3,576,128]{2,1,0:T(8,128)(2,1)} %get-tuple-element.115.refs_1_), channel_id=1, source_target_pairs={{0,1},{1,0},{2,3},{3,2},{4,5},{5,4},{6,7},{7,6},{8,9},{9,8},{10,11... | collective-permute-start | bytes 1327112 | tf_op jit(solution)/shard_map/ppermute | solution.py:666
  190.0 33.3 %collective-permute-start.26 = (bf16[3,576,128]{2,1,0:T(8,128)(2,1)}, bf16[3,576,128]{2,1,0:T(8,128)(2,1)}, u32[]{:S(2)}, u32[]{:S(2)}) collective-permute-start(bf16[3,576,128]{2,1,0:T(8,128)(2,1)} %get-tuple-element.116.refs_2_), channel_id=1, source_target_pairs={{0,2},{1,3},{2,0},{3,1},{4,6},{5,7},{6,4},{7,5},{8,10},{9,11},{10,... | collective-permute-start | bytes 1327112 | tf_op jit(solution)/shard_map/ppermute | solution.py:666
  192.4 30.9 %collective-permute-start.27 = (bf16[3,576,128]{2,1,0:T(8,128)(2,1)}, bf16[3,576,128]{2,1,0:T(8,128)(2,1)}, u32[]{:S(2)}, u32[]{:S(2)}) collective-permute-start(bf16[3,576,128]{2,1,0:T(8,128)(2,1)} %get-tuple-element.117.refs_3_), channel_id=1, source_target_pairs={{0,3},{1,2},{2,1},{3,0},{4,7},{5,6},{6,5},{7,4},{8,11},{9,10},{10,... | collective-permute-start | bytes 1327112 | tf_op jit(solution)/shard_map/ppermute | solution.py:666
  201.5 92.1 %all-gather.6.cloned.1.call-start = ((), (), s32[]{:S(2)}) async-start(), calls=%async_computation.4 | async-start | bytes 2654208 | tf_op jit(solution)/shard_map/all_gather | solution.py:867
  232.6 15.6 %collective-permute-start.24 = (bf16[192,768]{1,0:T(8,128)(2,1)S(1)}, bf16[192,768]{1,0:T(8,128)(2,1)S(1)}, u32[]{:S(2)}, u32[]{:S(2)}) collective-permute-start(bf16[192,768]{1,0:T(8,128)(2,1)S(1)} %slice.102), channel_id=1, source_target_pairs={{0,2},{1,3},{2,0},{3,1},{4,6},{5,7},{6,4},{7,5},{8,10},{9,11},{10,... | collective-permute-start | bytes 884744 | tf_op jit(solution)/shard_map/ppermute | solution.py:666
  266.1 13.6 %collective-permute-start.35 = (bf16[2,104,768]{2,1,0:T(8,128)(2,1)S(1)}, bf16[2,104,768]{2,1,0:T(8,128)(2,1)S(1)}, u32[]{:S(2)}, u32[]{:S(2)}) collective-permute-start(bf16[2,104,768]{2,1,0:T(8,128)(2,1)S(1)} %maximum_select_fusion.2), channel_id=1, source_target_pairs={{0,8},{4,12},{8,0},{12,4},{16,24},{20,28},{24,16},{28,20},{1,9},{5... | collective-permute-start | bytes 958472 | tf_op jit(solution)/shard_map/ppermute | solution.py:688
  (69 other events, 721.2 us)
Sparse Core Ops, SparseCore 0:
  74.2 33.4 all-gather.7
  109.5 33.9 all-gather.9
  147.0 53.8 reduce-scatter.4
  205.0 41.6 reduce-scatter.2
  249.2 33.3 all-gather.5

commit v4 on v3

--- a/solution.py
+++ b/solution.py
@@ -770,8 +770,8 @@
         jnp.zeros((rows, width), BF16), grad_pooled, (0, me * columns)
     )
     spread = swap_all([spread] * parts)
-    blocks, (bias,), (out_part, other_share, *spread) = gather_line(
-        first, [bias], [out_part, other_share] + spread
+    blocks, (bias, *spread), (out_part, other_share, out_one, out_three) = gather_line(
+        first, [bias] + spread, [out_part, other_share, swap(out_part, 1), swap(out_part, 3)]
     )
     pool_cot = sum(block.astype(F32) for block in spread)
     counts = (lengths - inst_lengths).astype(F32)
@@ -785,7 +785,7 @@
     )
     grad_low = grad_result.astype(BF16).reshape(tokens, width)
 
-    came = swap_all([out_part, out_part, jnp.concatenate((out_part, other_share), axis=0), out_part])
+    came = [out_part, out_one, swap(jnp.concatenate((out_part, other_share), axis=0), 2), out_three]
     out_size = out_part.shape[0]
     out_gathered, other_weights, _ = fetched(
         after(

time: 305 us -> 305 us (level)
  local copies, waits for them, and re-layouts: 28.7 us -> 33.7 us
    ppermute x1, waiting for transfers between devices: 7.06 us -> 2.08 us  [gather_line(): last_high = lax.ppermute(far_low, 'tp', outer)]
    unnamed x120 -> x138, local copies, waits for them, and re-layouts: 12.1 us -> 15.7 us
  transfers between devices with their start and end apart: 42 -> 42, of which waited for: 21 -> 22; matrix products, arithmetic and copies ran while one was open for 7% -> 8% of each run, Pallas kernels for 20% -> 20%
where the time goes in v4:
time: 305 us; the launch traced here: 303 us
  waiting for transfers between devices  120 us (39%)
  starting transfers between devices  66.1 us (22%)
  Pallas kernels  60.7 us (20%)
  local copies, waits for them, and re-layouts  33.7 us (11%)
  between operations  14.6 us (5%)
  other arithmetic  8.52 us (3%)
    ppermute x30, waiting for transfers between devices, swap(): return lax.ppermute(values, 'tp', [(i, i ^ distance) for i in range(parts)])  89 us
    ppermute x30, starting transfers between devices, swap(): return lax.ppermute(values, 'tp', [(i, i ^ distance) for i in range(parts)])  56.9 us
    pallas_call x10, Pallas kernels, call(): pl.pallas_call(kernel, grid=(rows,), in_specs=[SCALARS] * len(scalars) +...  54.1 us
    ppermute x3, waiting for transfers between devices, across(): return lax.ppermute(values, 'dp', [(i, i ^ 1 << bit) for i in range(count)])  17.6 us
    unnamed x138, local copies, waits for them, and re-layouts  15.7 us
    pallas_call x1, Pallas kernels, ffn_grad(): pl.pallas_call(ffn_grad_kernel, grid=(steps,), in_specs=[WIDE] * len(arra...  6.68 us
  transfers between devices with their start and end apart: 42, of which 22 were waited for; matrix products, arithmetic and copies ran while one was open for 8% of the time, Pallas kernels for 20%

profile of v4, /device:TPU:0, one launch (start us, length us, event | category | flops | bytes accessed | tf_op | source)
XLA Modules:
  0.0 303.4 jit_solution(12554482239165169446)
XLA Ops:
  9.3 3.1 %collective-permute-start = (bf16[3,128,768]{2,1,0:T(8,128)(2,1)S(1)}, bf16[3,128,768]{2,1,0:T(8,128)(2,1)}, u32[]{:S(2)}, u32[]{:S(2)}) collective-permute-start(bf16[3,128,768]{2,1,0:T(8,128)(2,1)S(1)} %norm_one.1.own_ref), channel_id=1, source_target_pairs={{0,1},{1,0},{2,3},{3,2},{4,5},{5,4},{6,7},{7,6},{8,9},{9,8},{10,11... | collective-permute-start | bytes 1769480 | tf_op jit(solution)/shard_map/ppermute | solution.py:666
  14.0 3.8 %collective-permute-start.2 = (bf16[3,768]{1,0:T(4,128)(2,1)S(1)}, bf16[3,768]{1,0:T(4,128)(2,1)S(1)}, u32[]{:S(2)}, u32[]{:S(2)}) collective-permute-start(bf16[3,768]{1,0:T(4,128)(2,1)S(1)} %dynamic_update_slice.3), channel_id=1, source_target_pairs={{0,1},{1,0},{2,3},{3,2},{4,5},{5,4},{6,7},{7,6},{8,9},{9,8},{10,11... | collective-permute-start | bytes 13832 | tf_op jit(solution)/shard_map/ppermute | solution.py:666
  22.8 3.1 %collective-permute-done.2 = bf16[3,768]{1,0:T(4,128)(2,1)S(1)} collective-permute-done((bf16[3,768]{1,0:T(4,128)(2,1)S(1)}, bf16[3,768]{1,0:T(4,128)(2,1)S(1)}, u32[]{:S(2)}, u32[]{:S(2)}) %collective-permute-start.2) | collective-permute-done | bytes 4640 | tf_op jit(solution)/shard_map/ppermute | solution.py:666
  25.9 4.5 %collective-permute-done.3 = bf16[3,768]{1,0:T(4,128)(2,1)S(1)} collective-permute-done((bf16[3,768]{1,0:T(4,128)(2,1)S(1)}, bf16[3,768]{1,0:T(4,128)(2,1)S(1)}, u32[]{:S(2)}, u32[]{:S(2)}) %collective-permute-start.3) | collective-permute-done | bytes 4640 | tf_op jit(solution)/shard_map/ppermute | solution.py:666
  33.8 3.5 %collective-permute-start.7 = (bf16[24,768]{1,0:T(8,128)(2,1)}, bf16[24,768]{1,0:T(8,128)(2,1)}, u32[]{:S(2)}, u32[]{:S(2)}) collective-permute-start(bf16[24,768]{1,0:T(8,128)(2,1)} %constant_dynamic-slice_fusion), channel_id=1, source_target_pairs={{0,1},{1,0},{2,3},{3,2},{4,5},{5,4},{6,7},{7,6},{8,9},{9,8},{10,11... | collective-permute-start | bytes 110600 | tf_op jit(solution)/shard_map/ppermute | solution.py:666
  37.4 2.5 collective-permute-start.8
  40.3 9.5 %collective-permute-done.7 = bf16[24,768]{1,0:T(8,128)(2,1)} collective-permute-done((bf16[24,768]{1,0:T(8,128)(2,1)}, bf16[24,768]{1,0:T(8,128)(2,1)}, u32[]{:S(2)}, u32[]{:S(2)}) %collective-permute-start.7) | collective-permute-done | bytes 36896 | tf_op jit(solution)/shard_map/ppermute | solution.py:666
  52.2 13.3 %collective-permute-done.10 = bf16[216,768]{1,0:T(8,128)(2,1)S(1)} collective-permute-done((bf16[216,768]{1,0:T(8,128)(2,1)S(1)}, bf16[216,768]{1,0:T(8,128)(2,1)S(1)}, u32[]{:S(2)}, u32[]{:S(2)}) %collective-permute-start.10) | collective-permute-done | bytes 331808 | tf_op jit(solution)/shard_map/ppermute | solution.py:666
  79.8 9.5 %attend.1 = (bf16[3,512,768]{2,1,0:T(8,128)(2,1)}, bf16[3,576,512]{2,1,0:T(8,128)(2,1)}, f32[3,3,512]{2,1,0:T(4,128)}, bf16[3,192,128]{2,1,0:T(8,128)(2,1)S(1)},...) custom-call(s32[1]{0:T(128)} %bitcast.place_ref, ...), custom_call_target="tpu_custom_call" | custom-call | flops 13200000000 | bytes 12000000 | tf_op jit(solution)/shard_map/attend/pallas_call | solution.py:81
  92.8 3.7 %collective-permute-done.11.grad_ref.grad_pair_ref = bf16[384,768]{1,0:T(8,128)(2,1)} collective-permute-done((bf16[384,768]{1,0:T(8,128)(2,1)S(1)}, bf16[384,768]{1,0:T(8,128)(2,1)}, u32[]{:S(2)}, u32[]{:S(2)}) %collective-permute-start.11) | collective-permute-done | bytes 589856 | tf_op jit(solution)/shard_map/ppermute | solution.py:666
  101.2 5.4 %all-gather.8.cloned.1.call-done = bf16[2304,768]{1,0:T(8,128)(2,1)} async-done(((bf16[288,768]{1,0:T(8,128)(2,1)}), bf16[2304,768]{1,0:T(8,128)(2,1)}) %all-gather.8.cloned.1.call-update) | async-done | bytes 3538960 | tf_op jit(solution)/shard_map/all_gather | solution.py:749
  110.4 3.5 %middle_of.1 = (f32[3,128,768]{2,1,0:T(8,128)}, bf16[3,128,768]{2,1,0:T(8,128)(2,1)S(1)}, bf16[3,768,128]{2,1,0:T(8,128)(2,1)}) custom-call(bf16[768,768]{1,0:T(8,128)(2,1)S(1)} %bitcast.54, bf16[3,128,768]{2,1,0:T(8,128)(2,1)S(1)} %copy-done.17, f32[1,768]{1,0:T(1,128)S(1)} %reshape.280.gain_ref, bf16[3,192,128]{2,1,0:T(8,128)(2,1)S(1)} %copy-done.37, ...), custom_call_target="tpu_custom_call" | custom-call | flops 3300000000 | bytes 3000000 | tf_op jit(solution)/shard_map/middle_of/pallas_call | solution.py:81
  116.2 5.0 %feed_forward.2 = (bf16[2,384,768]{2,1,0:T(8,128)(2,1)S(1)}, bf16[2,384,768]{2,1,0:T(8,128)(2,1)S(1)}, bf16[384,768]{1,0:T(8,128)(2,1)}, bf16[384,768]{1,0:T(8,128)(2,1)}) custom-call(bf16[384,768]{1,0:T(8,128)(2,1)S(1)} %bitcast.73, bf16[384,768]{1,0:T(8,128)(2,1)S(1)} %bitcast.61, bf16[768,768]{1,0:T(8,128)(2,1)S(1)} %copy-done.3, ...), custom_call_target="tpu_custom_call" | custom-call | flops 6600000000 | bytes 6000000 | tf_op jit(solution)/shard_map/feed_forward/pallas_call | solution.py:81
  121.2 7.0 %collective-permute-done.18.normed_ref.normed_pair_ref = bf16[384,768]{1,0:T(8,128)(2,1)S(1)} collective-permute-done((bf16[384,768]{1,0:T(8,128)(2,1)S(1)}, bf16[384,768]{1,0:T(8,128)(2,1)S(1)}, u32[]{:S(2)}, u32[]{:S(2)}) %collective-permute-start.18) | collective-permute-done | bytes 589856 | tf_op jit(solution)/shard_map/ppermute | solution.py:666
  128.2 6.1 %feed_forward.3 = (bf16[2,384,768]{2,1,0:T(8,128)(2,1)S(1)}, bf16[2,384,768]{2,1,0:T(8,128)(2,1)S(1)}, bf16[384,768]{1,0:T(8,128)(2,1)}, bf16[384,768]{1,0:T(8,128)(2,1)}) custom-call(bf16[384,768]{1,0:T(8,128)(2,1)S(1)} %collective-permute-done.18.normed_ref.normed_pair_ref, bf16[384,768]{1,0:T(8,128)(2,1)} %collective-permute-done.11.grad_ref.grad_pair_ref, ...), custom_call_target="tpu_custom_call" | custom-call | flops 6600000000 | bytes 6000000 | tf_op jit(solution)/shard_map/feed_forward/pallas_call | solution.py:81
  134.3 6.7 %ffn_grad.1 = bf16[2,4,384,768]{3,2,1,0:T(8,128)(2,1)} custom-call(bf16[384,768]{1,0:T(8,128)(2,1)S(1)} %bitcast.74, bf16[384,768]{1,0:T(8,128)(2,1)S(1)} %collective-permute-done.18.normed_ref.normed_pair_ref, bf16[384,768]{1,0:T(8,128)(2,1)S(1)} %bitcast.62, bf16[384,768]{1,0:T(8,128)(2,1)} %collective-permute-done.11.grad_ref.grad_pair_ref, ...), custom_call_target="tpu_custom_call" | custom-call | flops 6600000000 | bytes 6000000 | tf_op jit(solution)/shard_map/ffn_grad/pallas_call | solution.py:508
  142.8 11.9 %collective-permute-done.19 = bf16[384,768]{1,0:T(8,128)(2,1)S(1)} collective-permute-done((bf16[384,768]{1,0:T(8,128)(2,1)}, bf16[384,768]{1,0:T(8,128)(2,1)S(1)}, u32[]{:S(2)}, u32[]{:S(2)}) %collective-permute-start.19) | collective-permute-done | bytes 589856 | tf_op jit(solution)/shard_map/ppermute | solution.py:666
  155.9 3.1 %middle_back.1 = (f32[3,128,768]{2,1,0:T(8,128)}, bf16[3,128,768]{2,1,0:T(8,128)(2,1)}, f32[1,768]{1,0:T(1,128)}, bf16[3,192,128]{2,1,0:T(8,128)(2,1)S(1)}, bf16...) custom-call(bf16[768,768]{1,0:T(8,128)(2,1)S(1)} %bitcast.55, ...), custom_call_target="tpu_custom_call" | custom-call | flops 4400000000 | bytes 4000000 | tf_op jit(solution)/shard_map/middle_back/pallas_call | solution.py:81
  159.6 4.8 %collective-permute-start.22 = (bf16[3,192,128]{2,1,0:T(8,128)(2,1)}, bf16[3,192,128]{2,1,0:T(8,128)(2,1)}, u32[]{:S(2)}, u32[]{:S(2)}) collective-permute-start(bf16[3,192,128]{2,1,0:T(8,128)(2,1)} %get-tuple-element.114), channel_id=1, source_target_pairs={{0,3},{1,2},{2,1},{3,0},{4,7},{5,6},{6,5},{7,4},{8,11},{9,10},{10,... | collective-permute-start | bytes 442376 | tf_op jit(solution)/shard_map/ppermute | solution.py:666
  169.6 3.1 %collective-permute-start.23 = (bf16[384,768]{1,0:T(8,128)(2,1)}, bf16[384,768]{1,0:T(8,128)(2,1)}, u32[]{:S(2)}, u32[]{:S(2)}) collective-permute-start(bf16[384,768]{1,0:T(8,128)(2,1)} %get-tuple-element.124), channel_id=1, source_target_pairs={{0,1},{1,0},{2,3},{3,2},{4,5},{5,4},{6,7},{7,6},{8,9},{9,8},{10,11... | collective-permute-start | bytes 1769480 | tf_op jit(solution)/shard_map/ppermute | solution.py:666
  175.5 12.5 %attend_back.1 = (bf16[3,576,128]{2,1,0:T(8,128)(2,1)S(1)}, bf16[3,576,128]{2,1,0:T(8,128)(2,1)}, bf16[3,576,128]{2,1,0:T(8,128)(2,1)}, bf16[3,576,128]{2,1,0:T(8,128)(2,1)}, f32[3,8,128]{2,1,0:T(8,128)}) custom-call(s32[1]{0:T(128)} %bitcast.place_ref, s32[3]{0:T(128)S(1)} %copy-done.15, bf16[3,576,512]{2,1,0:T(8,128)(2,1)S(1)} %copy-done.40, ...), custom_call_target="tpu_custom_call" | custom-call | flops 15399999488 | bytes 14000000 | tf_op jit(solution)/shard_map/attend_back/pallas_call | solution.py:81
  193.5 6.9 %joint_grad.1 = bf16[8,176,768]{2,1,0:T(8,128)(2,1)} custom-call(bf16[3,512,768]{2,1,0:T(8,128)(2,1)S(1)} %copy-done.30, bf16[192,768]{1,0:T(8,128)(2,1)S(1)} %bitcast.65, bf16[192,768]{1,0:T(8,128)(2,1)S(1)} %bitcast.68, bf16[192,768]{1,0:T(8,128)(2,1)S(1)} %bitcast.71, f32[1,768]{1,0:T(1,128)S(1)} %reshape.278.gain_ref, f32[1,768]{1,0:T(1,128)S(1)} %copy-done.42, ...), custom_call_target="tpu_custom_call" | custom-call | flops 6600000000 | bytes 6000000 | tf_op jit(solution)/shard_map/joint_grad/pallas_call | solution.py:81
  200.6 7.0 %collective-permute-done.25.refs_1_ = bf16[3,576,128]{2,1,0:T(8,128)(2,1)} collective-permute-done((bf16[3,576,128]{2,1,0:T(8,128)(2,1)}, bf16[3,576,128]{2,1,0:T(8,128)(2,1)}, u32[]{:S(2)}, u32[]{:S(2)}) %collective-permute-start.25) | collective-permute-done | bytes 442400 | tf_op jit(solution)/shard_map/ppermute | solution.py:666
  207.5 14.7 %collective-permute-done.26.refs_2_ = bf16[3,576,128]{2,1,0:T(8,128)(2,1)} collective-permute-done((bf16[3,576,128]{2,1,0:T(8,128)(2,1)}, bf16[3,576,128]{2,1,0:T(8,128)(2,1)}, u32[]{:S(2)}, u32[]{:S(2)}) %collective-permute-start.26) | collective-permute-done | bytes 442400 | tf_op jit(solution)/shard_map/ppermute | solution.py:666
  225.7 4.8 %hidden_grad.1 = f32[3,128,768]{2,1,0:T(8,128)} custom-call(s32[1]{0:T(128)} %bitcast.place_ref, bf16[4,576,768]{2,1,0:T(8,128)(2,1)S(1)} %bitcast.53, f32[3,128,768]{2,1,0:T(8,128)S(1)} %copy-done.31, bf16[3,128,768]{2,1,0:T(8,128)(2,1)S(1)} %copy-done.18, f32[1,768]{1,0:T(1,128)S(1)} %reshape.278.gain_ref, bf16[3,576,128]{2,1,0:T(8,128)(2,1)S(1)} %copy-done.35, ...), custom_call_target="tpu_custom_call" | custom-call | flops 165000003584 | bytes 150000000 | tf_op jit(solution)/shard_map/hidden_grad/pallas_call | solution.py:81
  231.6 6.5 %collective-permute-start.24 = (bf16[192,768]{1,0:T(8,128)(2,1)S(1)}, bf16[192,768]{1,0:T(8,128)(2,1)S(1)}, u32[]{:S(2)}, u32[]{:S(2)}) collective-permute-start(bf16[192,768]{1,0:T(8,128)(2,1)S(1)} %slice.102), channel_id=1, source_target_pairs={{0,2},{1,3},{2,0},{3,1},{4,6},{5,7},{6,4},{7,5},{8,10},{9,11},{10,... | collective-permute-start | bytes 884744 | tf_op jit(solution)/shard_map/ppermute | solution.py:666
  240.0 5.6 %reduce-scatter.3.cloned.1.call-done = bf16[176,768]{1,0:T(8,128)(2,1)} async-done(((bf16[1408,768]{1,0:T(8,128)(2,1)}), bf16[176,768]{1,0:T(8,128)(2,1)}) %reduce-scatter.3.cloned.1.call-update) | async-done | bytes 270352 | tf_op jit(solution)/shard_map/reduce_scatter | solution.py:862
  252.5 2.9 collective-permute-done.32
  259.4 5.5 %collective-permute-done.34 = bf16[1,104,768]{2,1,0:T(8,128)(2,1)S(1)} collective-permute-done((bf16[1,104,768]{2,1,0:T(8,128)(2,1)S(1)}, bf16[1,104,768]{2,1,0:T(8,128)(2,1)S(1)}, u32[]{:S(2)}, u32[]{:S(2)}) %collective-permute-start.34) | collective-permute-done | bytes 159776 | tf_op jit(solution)/shard_map/ppermute | solution.py:688
  266.6 12.1 %collective-permute-done.35 = bf16[2,104,768]{2,1,0:T(8,128)(2,1)S(1)} collective-permute-done((bf16[2,104,768]{2,1,0:T(8,128)(2,1)S(1)}, bf16[2,104,768]{2,1,0:T(8,128)(2,1)S(1)}, u32[]{:S(2)}, u32[]{:S(2)}) %collective-permute-start.35) | collective-permute-done | bytes 319520 | tf_op jit(solution)/shard_map/ppermute | solution.py:688
  280.1 4.3 %collective-permute-start.30 = (f32[3,768]{1,0:T(4,128)S(1)}, f32[3,768]{1,0:T(4,128)S(1)}, u32[]{:S(2)}, u32[]{:S(2)}) collective-permute-start(f32[3,768]{1,0:T(4,128)S(1)} %broadcast_divide_fusion), channel_id=1, source_target_pairs={{0,3},{1,2},{2,1},{3,0},{4,7},{5,6},{6,5},{7,4},{8,11},{9,10},{10,... | collective-permute-start | bytes 27656 | tf_op jit(solution)/shard_map/ppermute | solution.py:666
  292.6 4.2 %fusion.8 = (f32[768,768]{1,0:T(8,128)}, f32[768,768]{1,0:T(8,128)}) fusion(bf16[1536,768]{1,0:T(8,128)(2,1)} %all-gather.6.cloned.1.call-done), kind=kLoop, calls=%fused_computation.55 | loop fusion | bytes 9437184 | tf_op jit(solution)/shard_map/slice | solution.py:918
  (256 shorter events, 88.8 us)
Async XLA Ops:
  7.2 99.4 %all-gather.8.cloned.1.call-start = ((), (), s32[]{:S(2)}) async-start(), calls=%async_computation.5 | async-start | bytes 3981312 | tf_op jit(solution)/shard_map/all_gather | solution.py:749
  9.3 21.1 %collective-permute-start = (bf16[3,128,768]{2,1,0:T(8,128)(2,1)S(1)}, bf16[3,128,768]{2,1,0:T(8,128)(2,1)}, u32[]{:S(2)}, u32[]{:S(2)}) collective-permute-start(bf16[3,128,768]{2,1,0:T(8,128)(2,1)S(1)} %norm_one.1.own_ref), channel_id=1, source_target_pairs={{0,1},{1,0},{2,3},{3,2},{4,5},{5,4},{6,7},{7,6},{8,9},{9,8},{10,11... | collective-permute-start | bytes 1769480 | tf_op jit(solution)/shard_map/ppermute | solution.py:666
  12.4 18.0 %collective-permute-start.1 = (bf16[3,128,768]{2,1,0:T(8,128)(2,1)S(1)}, bf16[3,128,768]{2,1,0:T(8,128)(2,1)}, u32[]{:S(2)}, u32[]{:S(2)}) collective-permute-start(bf16[3,128,768]{2,1,0:T(8,128)(2,1)S(1)} %norm_one.1.own_ref), channel_id=1, source_target_pairs={{1,2},{2,1},{5,6},{6,5},{9,10},{10,9},{13,14},{14,13},{17,18},{18,... | collective-permute-start | bytes 1769480 | tf_op jit(solution)/shard_map/ppermute | solution.py:677
  14.0 11.9 %collective-permute-start.2 = (bf16[3,768]{1,0:T(4,128)(2,1)S(1)}, bf16[3,768]{1,0:T(4,128)(2,1)S(1)}, u32[]{:S(2)}, u32[]{:S(2)}) collective-permute-start(bf16[3,768]{1,0:T(4,128)(2,1)S(1)} %dynamic_update_slice.3), channel_id=1, source_target_pairs={{0,1},{1,0},{2,3},{3,2},{4,5},{5,4},{6,7},{7,6},{8,9},{9,8},{10,11... | collective-permute-start | bytes 13832 | tf_op jit(solution)/shard_map/ppermute | solution.py:666
  17.8 12.5 %collective-permute-start.3 = (bf16[3,768]{1,0:T(4,128)(2,1)S(1)}, bf16[3,768]{1,0:T(4,128)(2,1)S(1)}, u32[]{:S(2)}, u32[]{:S(2)}) collective-permute-start(bf16[3,768]{1,0:T(4,128)(2,1)S(1)} %dynamic_update_slice.3), channel_id=1, source_target_pairs={{0,2},{1,3},{2,0},{3,1},{4,6},{5,7},{6,4},{7,5},{8,10},{9,11},{10,... | collective-permute-start | bytes 13832 | tf_op jit(solution)/shard_map/ppermute | solution.py:666
  17.8 12.5 %collective-permute-start.4 = (bf16[3,768]{1,0:T(4,128)(2,1)S(1)}, bf16[3,768]{1,0:T(4,128)(2,1)S(1)}, u32[]{:S(2)}, u32[]{:S(2)}) collective-permute-start(bf16[3,768]{1,0:T(4,128)(2,1)S(1)} %dynamic_update_slice.3), channel_id=1, source_target_pairs={{0,3},{1,2},{2,1},{3,0},{4,7},{5,6},{6,5},{7,4},{8,11},{9,10},{10,... | collective-permute-start | bytes 13832 | tf_op jit(solution)/shard_map/ppermute | solution.py:666
  30.4 19.4 %collective-permute-start.5 = (bf16[3,128,768]{2,1,0:T(8,128)(2,1)}, bf16[3,128,768]{2,1,0:T(8,128)(2,1)}, u32[]{:S(2)}, u32[]{:S(2)}) collective-permute-start(bf16[3,128,768]{2,1,0:T(8,128)(2,1)} %collective-permute-done.pair_ref), channel_id=1, source_target_pairs={{1,2},{2,1},{5,6},{6,5},{9,10},{10,9},{13,14},{14,13},{17,18},{18,... | collective-permute-start | bytes 1769480 | tf_op jit(solution)/shard_map/ppermute | solution.py:679
  31.9 17.9 %collective-permute-start.6 = (bf16[3,128,768]{2,1,0:T(8,128)(2,1)}, bf16[3,128,768]{2,1,0:T(8,128)(2,1)}, u32[]{:S(2)}, u32[]{:S(2)}) collective-permute-start(bf16[3,128,768]{2,1,0:T(8,128)(2,1)} %collective-permute-done.1.last_low_ref), channel_id=1, source_target_pairs={{1,0},{2,3},{5,4},{6,7},{9,8},{10,11},{13,12},{14,15},{17,16},{18,... | collective-permute-start | bytes 1769480 | tf_op jit(solution)/shard_map/ppermute | solution.py:680
  33.8 15.9 %collective-permute-start.7 = (bf16[24,768]{1,0:T(8,128)(2,1)}, bf16[24,768]{1,0:T(8,128)(2,1)}, u32[]{:S(2)}, u32[]{:S(2)}) collective-permute-start(bf16[24,768]{1,0:T(8,128)(2,1)} %constant_dynamic-slice_fusion), channel_id=1, source_target_pairs={{0,1},{1,0},{2,3},{3,2},{4,5},{5,4},{6,7},{7,6},{8,9},{9,8},{10,11... | collective-permute-start | bytes 110600 | tf_op jit(solution)/shard_map/ppermute | solution.py:666
  37.4 12.4 %collective-permute-start.8 = (bf16[24,768]{1,0:T(8,128)(2,1)}, bf16[24,768]{1,0:T(8,128)(2,1)}, u32[]{:S(2)}, u32[]{:S(2)}) collective-permute-start(bf16[24,768]{1,0:T(8,128)(2,1)} %constant_dynamic-slice_fusion), channel_id=1, source_target_pairs={{0,3},{1,2},{2,1},{3,0},{4,7},{5,6},{6,5},{7,4},{8,11},{9,10},{10,... | collective-permute-start | bytes 110600 | tf_op jit(solution)/shard_map/ppermute | solution.py:666
  50.7 14.8 %collective-permute-start.10 = (bf16[216,768]{1,0:T(8,128)(2,1)S(1)}, bf16[216,768]{1,0:T(8,128)(2,1)S(1)}, u32[]{:S(2)}, u32[]{:S(2)}) collective-permute-start(bf16[216,768]{1,0:T(8,128)(2,1)S(1)} %pad_maximum_fusion.1), channel_id=1, source_target_pairs={{0,2},{1,3},{2,0},{3,1},{4,6},{5,7},{6,4},{7,5},{8,10},{9,11},{10,... | collective-permute-start | bytes 995336 | tf_op jit(solution)/shard_map/ppermute | solution.py:666
  50.9 22.1 %collective-permute-start.9 = (bf16[3,128,768]{2,1,0:T(8,128)(2,1)}, bf16[3,128,768]{2,1,0:T(8,128)(2,1)}, u32[]{:S(2)}, u32[]{:S(2)}) collective-permute-start(bf16[3,128,768]{2,1,0:T(8,128)(2,1)} %collective-permute-done.5.far_low_ref), channel_id=1, source_target_pairs={{1,0},{2,3},{5,4},{6,7},{9,8},{10,11},{13,12},{14,15},{17,16},{18,... | collective-permute-start | bytes 1769480 | tf_op jit(solution)/shard_map/ppermute | solution.py:682
  73.0 91.9 %all-gather.10.cloned.1.call-start = ((), (), s32[]{:S(2)}) async-start(), calls=%async_computation.6 | async-start | bytes 3981312 | tf_op jit(solution)/shard_map/all_gather | solution.py:749
  75.4 16.5 %collective-permute-start.12 = (bf16[72,768]{1,0:T(8,128)(2,1)S(1)}, bf16[72,768]{1,0:T(8,128)(2,1)S(1)}, u32[]{:S(2)}, u32[]{:S(2)}) collective-permute-start(bf16[72,768]{1,0:T(8,128)(2,1)S(1)} %fusion.3), channel_id=1, source_target_pairs={{0,1},{1,0},{2,3},{3,2},{4,5},{5,4},{6,7},{7,6},{8,9},{9,8},{10,11... | collective-permute-start | bytes 331784 | tf_op jit(solution)/shard_map/ppermute | solution.py:666
  75.4 16.5 %collective-permute-start.13 = (bf16[72,768]{1,0:T(8,128)(2,1)S(1)}, bf16[72,768]{1,0:T(8,128)(2,1)S(1)}, u32[]{:S(2)}, u32[]{:S(2)}) collective-permute-start(bf16[72,768]{1,0:T(8,128)(2,1)S(1)} %fusion.3), channel_id=1, source_target_pairs={{0,2},{1,3},{2,0},{3,1},{4,6},{5,7},{6,4},{7,5},{8,10},{9,11},{10,... | collective-permute-start | bytes 331784 | tf_op jit(solution)/shard_map/ppermute | solution.py:666
  77.7 14.3 %collective-permute-start.14 = (bf16[72,768]{1,0:T(8,128)(2,1)S(1)}, bf16[72,768]{1,0:T(8,128)(2,1)S(1)}, u32[]{:S(2)}, u32[]{:S(2)}) collective-permute-start(bf16[72,768]{1,0:T(8,128)(2,1)S(1)} %fusion.3), channel_id=1, source_target_pairs={{0,3},{1,2},{2,1},{3,0},{4,7},{5,6},{6,5},{7,4},{8,11},{9,10},{10,... | collective-permute-start | bytes 331784 | tf_op jit(solution)/shard_map/ppermute | solution.py:666
  79.8 16.7 %collective-permute-start.11 = (bf16[384,768]{1,0:T(8,128)(2,1)S(1)}, bf16[384,768]{1,0:T(8,128)(2,1)}, u32[]{:S(2)}, u32[]{:S(2)}) collective-permute-start(bf16[384,768]{1,0:T(8,128)(2,1)S(1)} %bitcast.60), channel_id=1, source_target_pairs={{0,1},{1,0},{2,3},{3,2},{4,5},{5,4},{6,7},{7,6},{8,9},{9,8},{10,11... | collective-permute-start | bytes 1769480 | tf_op jit(solution)/shard_map/ppermute | solution.py:666
  96.5 134.1 %reduce-scatter.5.cloned.1.call-start = ((), (), s32[]{:S(2)}) async-start(), calls=%async_computation.3 | async-start | bytes 5308416 | tf_op jit(solution)/shard_map/reduce_scatter | solution.py:822
  96.7 11.3 %collective-permute-start.15 = (bf16[3,192,128]{2,1,0:T(8,128)(2,1)S(1)}, bf16[3,192,128]{2,1,0:T(8,128)(2,1)S(1)}, u32[]{:S(2)}, u32[]{:S(2)}) collective-permute-start(bf16[3,192,128]{2,1,0:T(8,128)(2,1)S(1)} %copy-done.26), channel_id=1, source_target_pairs={{0,1},{1,0},{2,3},{3,2},{4,5},{5,4},{6,7},{7,6},{8,9},{9,8},{10,11... | collective-permute-start | bytes 442376 | tf_op jit(solution)/shard_map/ppermute | solution.py:666
  97.3 13.1 %collective-permute-start.16 = (bf16[3,192,128]{2,1,0:T(8,128)(2,1)S(1)}, bf16[3,192,128]{2,1,0:T(8,128)(2,1)}, u32[]{:S(2)}, u32[]{:S(2)}) collective-permute-start(bf16[3,192,128]{2,1,0:T(8,128)(2,1)S(1)} %copy-done.24), channel_id=1, source_target_pairs={{0,2},{1,3},{2,0},{3,1},{4,6},{5,7},{6,4},{7,5},{8,10},{9,11},{10,... | collective-permute-start | bytes 442376 | tf_op jit(solution)/shard_map/ppermute | solution.py:666
  99.1 11.3 %collective-permute-start.17 = (bf16[3,192,128]{2,1,0:T(8,128)(2,1)S(1)}, bf16[3,192,128]{2,1,0:T(8,128)(2,1)}, u32[]{:S(2)}, u32[]{:S(2)}) collective-permute-start(bf16[3,192,128]{2,1,0:T(8,128)(2,1)S(1)} %copy-done.22), channel_id=1, source_target_pairs={{0,3},{1,2},{2,1},{3,0},{4,7},{5,6},{6,5},{7,4},{8,11},{9,10},{10,... | collective-permute-start | bytes 442376 | tf_op jit(solution)/shard_map/ppermute | solution.py:666
  113.9 14.3 %collective-permute-start.18 = (bf16[384,768]{1,0:T(8,128)(2,1)S(1)}, bf16[384,768]{1,0:T(8,128)(2,1)S(1)}, u32[]{:S(2)}, u32[]{:S(2)}) collective-permute-start(bf16[384,768]{1,0:T(8,128)(2,1)S(1)} %bitcast.72), channel_id=1, source_target_pairs={{0,1},{1,0},{2,3},{3,2},{4,5},{5,4},{6,7},{7,6},{8,9},{9,8},{10,11... | collective-permute-start | bytes 1769480 | tf_op jit(solution)/shard_map/ppermute | solution.py:666
  141.0 104.6 %reduce-scatter.3.cloned.1.call-start = ((), (), s32[]{:S(2)}) async-start(), calls=%async_computation.2 | async-start | bytes 2433024 | tf_op jit(solution)/shard_map/reduce_scatter | solution.py:862
  141.3 13.5 %collective-permute-start.19 = (bf16[384,768]{1,0:T(8,128)(2,1)}, bf16[384,768]{1,0:T(8,128)(2,1)S(1)}, u32[]{:S(2)}, u32[]{:S(2)}) collective-permute-start(bf16[384,768]{1,0:T(8,128)(2,1)} %get-tuple-element.101), channel_id=1, source_target_pairs={{0,1},{1,0},{2,3},{3,2},{4,5},{5,4},{6,7},{7,6},{8,9},{9,8},{10,11... | collective-permute-start | bytes 1769480 | tf_op jit(solution)/shard_map/ppermute | solution.py:666
  164.4 11.0 %collective-permute-start.21 = (bf16[3,192,128]{2,1,0:T(8,128)(2,1)}, bf16[3,192,128]{2,1,0:T(8,128)(2,1)}, u32[]{:S(2)}, u32[]{:S(2)}) collective-permute-start(bf16[3,192,128]{2,1,0:T(8,128)(2,1)} %get-tuple-element.113), channel_id=1, source_target_pairs={{0,2},{1,3},{2,0},{3,1},{4,6},{5,7},{6,4},{7,5},{8,10},{9,11},{10,... | collective-permute-start | bytes 442376 | tf_op jit(solution)/shard_map/ppermute | solution.py:666
  169.6 31.0 %collective-permute-start.23 = (bf16[384,768]{1,0:T(8,128)(2,1)}, bf16[384,768]{1,0:T(8,128)(2,1)}, u32[]{:S(2)}, u32[]{:S(2)}) collective-permute-start(bf16[384,768]{1,0:T(8,128)(2,1)} %get-tuple-element.124), channel_id=1, source_target_pairs={{0,1},{1,0},{2,3},{3,2},{4,5},{5,4},{6,7},{7,6},{8,9},{9,8},{10,11... | collective-permute-start | bytes 1769480 | tf_op jit(solution)/shard_map/ppermute | solution.py:666
  187.9 19.6 %collective-permute-start.25 = (bf16[3,576,128]{2,1,0:T(8,128)(2,1)}, bf16[3,576,128]{2,1,0:T(8,128)(2,1)}, u32[]{:S(2)}, u32[]{:S(2)}) collective-permute-start(bf16[3,576,128]{2,1,0:T(8,128)(2,1)} %get-tuple-element.119.refs_1_), channel_id=1, source_target_pairs={{0,1},{1,0},{2,3},{3,2},{4,5},{5,4},{6,7},{7,6},{8,9},{9,8},{10,11... | collective-permute-start | bytes 1327112 | tf_op jit(solution)/shard_map/ppermute | solution.py:666
  189.0 33.3 %collective-permute-start.26 = (bf16[3,576,128]{2,1,0:T(8,128)(2,1)}, bf16[3,576,128]{2,1,0:T(8,128)(2,1)}, u32[]{:S(2)}, u32[]{:S(2)}) collective-permute-start(bf16[3,576,128]{2,1,0:T(8,128)(2,1)} %get-tuple-element.120.refs_2_), channel_id=1, source_target_pairs={{0,2},{1,3},{2,0},{3,1},{4,6},{5,7},{6,4},{7,5},{8,10},{9,11},{10,... | collective-permute-start | bytes 1327112 | tf_op jit(solution)/shard_map/ppermute | solution.py:666
  191.4 30.9 %collective-permute-start.27 = (bf16[3,576,128]{2,1,0:T(8,128)(2,1)}, bf16[3,576,128]{2,1,0:T(8,128)(2,1)}, u32[]{:S(2)}, u32[]{:S(2)}) collective-permute-start(bf16[3,576,128]{2,1,0:T(8,128)(2,1)} %get-tuple-element.121.refs_3_), channel_id=1, source_target_pairs={{0,3},{1,2},{2,1},{3,0},{4,7},{5,6},{6,5},{7,4},{8,11},{9,10},{10,... | collective-permute-start | bytes 1327112 | tf_op jit(solution)/shard_map/ppermute | solution.py:666
  200.5 92.1 %all-gather.6.cloned.1.call-start = ((), (), s32[]{:S(2)}) async-start(), calls=%async_computation.4 | async-start | bytes 2654208 | tf_op jit(solution)/shard_map/all_gather | solution.py:867
  231.6 15.6 %collective-permute-start.24 = (bf16[192,768]{1,0:T(8,128)(2,1)S(1)}, bf16[192,768]{1,0:T(8,128)(2,1)S(1)}, u32[]{:S(2)}, u32[]{:S(2)}) collective-permute-start(bf16[192,768]{1,0:T(8,128)(2,1)S(1)} %slice.102), channel_id=1, source_target_pairs={{0,2},{1,3},{2,0},{3,1},{4,6},{5,7},{6,4},{7,5},{8,10},{9,11},{10,... | collective-permute-start | bytes 884744 | tf_op jit(solution)/shard_map/ppermute | solution.py:666
  265.0 13.6 %collective-permute-start.35 = (bf16[2,104,768]{2,1,0:T(8,128)(2,1)S(1)}, bf16[2,104,768]{2,1,0:T(8,128)(2,1)S(1)}, u32[]{:S(2)}, u32[]{:S(2)}) collective-permute-start(bf16[2,104,768]{2,1,0:T(8,128)(2,1)S(1)} %maximum_select_fusion.2), channel_id=1, source_target_pairs={{0,8},{4,12},{8,0},{12,4},{16,24},{20,28},{24,16},{28,20},{1,9},{5... | collective-permute-start | bytes 958472 | tf_op jit(solution)/shard_map/ppermute | solution.py:688
  (78 other events, 792.5 us)
Sparse Core Ops, SparseCore 0:
  73.2 33.3 all-gather.7
  108.4 33.9 all-gather.9
  145.9 53.8 reduce-scatter.4
  203.9 41.6 reduce-scatter.2
  248.1 33.3 all-gather.5
